TPU v7x, 256 devices: a whole 4x4x8 slice. The times are simulated.
256 devices in a mesh: blk: 64 (over x, y_lo, z), rep: 4 (over y_hi, core).
Axes of the slice: x: 4, y: 4 (y_hi: 2, y_lo: 2; y = y_hi * 2 + y_lo), z: 8, core: 2. Of those that a mesh axis runs over, the one named last changes fastest.
Arguments:
- node_feats: bfloat16 [131072, 128], P(('blk', 'rep')), may hold values from -6 to 6
- adj_tiles: bfloat16 [1024, 4, 4, 128, 128], P('blk', 'rep'), as said below
- col_index: int32 [1024, 4, 4], P('blk', 'rep'), may hold values from 0 to 255, as said below
- w_in: bfloat16 [128, 512], replicated, may hold values from -0.5 to 0.5
- b_in: float32 [512], replicated, may hold values from -3 to 3
- w_out: bfloat16 [512, 128], replicated, may hold values from -0.25 to 0.25
- b_out: float32 [128], replicated, may hold values from -3 to 3
- cot_out: bfloat16 [131072, 128], P(('blk', 'rep')), may hold values from -6 to 6
Outputs:
- out_feats: bfloat16 [131072, 128], P(('blk', 'rep'))
- grad_feats: bfloat16 [131072, 128], P(('blk', 'rep'))
Inputs may be any that keep to these rules, and one draw needn't show every extreme that they name: The matrix A described by adj_tiles and col_index is symmetric (A equals its transpose). `col_index`: column block numbers within a quarter.
All inputs are finite; a program needn't handle non-finite values.
Results may differ from a plain program's by a relative error of at most 0.0045.
Values may be sent and summed in bfloat16 or wider, within the bound.
A program may use at most 128 MiB of HBM per device.

v0:
```python
import jax
import jax.numpy as jnp
from jax import lax
from jax.sharding import PartitionSpec as P

BLOCK = 128


def tile_products(panels, adj_tiles, col_index):
    width = panels.shape[1]
    grouped = panels.reshape(-1, BLOCK, width)
    picked = grouped[col_index[:, 0, :]]
    summed = jnp.einsum(
        "rkij,rkjh->rih", adj_tiles[:, 0], picked, preferred_element_type=jnp.float32
    )
    return summed.reshape(-1, width)


def own_rows(full_rows, count):
    return lax.dynamic_slice_in_dim(full_rows, lax.axis_index("rep") * count, count, 0)


def local(node_feats, adj_tiles, col_index, w_in, b_in, w_out, b_out, cot_out):
    quarter = node_feats.shape[0]
    width = node_feats.shape[1]
    panels = lax.all_gather(node_feats, "blk", axis=0, tiled=True)
    partial_sum = tile_products(panels, adj_tiles, col_index)
    agg_rows = lax.psum(partial_sum, "rep")
    cot_rows = lax.all_gather(cot_out, "rep", axis=0, tiled=True)
    agg_b = agg_rows.astype(jnp.bfloat16)
    pre = jnp.dot(agg_b, w_in, preferred_element_type=jnp.float32) + b_in
    hidden = jax.nn.silu(pre).astype(jnp.bfloat16)
    projected = jnp.dot(hidden, w_out, preferred_element_type=jnp.float32) + b_out
    g_hidden = jnp.einsum("nh,fh->nf", cot_rows, w_out, preferred_element_type=jnp.float32)
    sigma = jax.nn.sigmoid(pre)
    g_pre = (g_hidden * sigma * (1.0 + pre * (1.0 - sigma))).astype(jnp.bfloat16)
    g_agg = jnp.einsum("nf,hf->nh", g_pre, w_in, preferred_element_type=jnp.float32).astype(
        jnp.bfloat16
    )
    projected_own = own_rows(projected, quarter)
    out_feats = (node_feats.astype(jnp.float32) + projected_own).astype(jnp.bfloat16)
    blocks = g_agg.reshape(-1, BLOCK, width)
    contrib = jnp.einsum(
        "rkij,rih->rkjh", adj_tiles[:, 0], blocks, preferred_element_type=jnp.float32
    )
    segments = lax.axis_size("blk") * quarter // BLOCK
    term = jax.ops.segment_sum(
        contrib.reshape(-1, BLOCK, width), col_index[:, 0, :].reshape(-1), num_segments=segments
    )
    back_rows = lax.psum_scatter(term.reshape(-1, width), "blk", scatter_dimension=0, tiled=True)
    grad_feats = (cot_out.astype(jnp.float32) + back_rows).astype(jnp.bfloat16)
    return (out_feats, grad_feats)


def solution(mesh):
    placed = (
        P(("blk", "rep"), None),
        P("blk", "rep", None, None, None),
        P("blk", "rep", None),
        P(),
        P(),
        P(),
        P(),
        P(("blk", "rep"), None),
    )
    return jax.shard_map(
        local,
        mesh=mesh,
        in_specs=placed,
        out_specs=(P(("blk", "rep"), None), P(("blk", "rep"), None)),
        check_vma=False,
    )
```

profile of v0, /device:TPU:16, one launch (start us, length us, event | category | flops | bytes accessed | tf_op | source)
XLA Modules:
  0.0 759.3 jit_solution(3380160100845776851)
XLA Ops:
  7.2 0.0 all-gather.2.cloned.1.call-start
  7.2 0.7 all-gather.2.cloned.1.call-update
  7.9 0.0 reduce-scatter.2.cloned.1.call-start
  8.0 0.8 copy.14
  8.7 0.7 compare_select_fusion
  9.4 0.1 copy.13
  9.5 0.1 reshape.56
  9.6 0.1 reshape.64
  9.7 8.9 %all_gather.7 = bf16[2048,128]{1,0:T(8,128)(2,1)} all-gather(bf16[512,128]{1,0:T(8,128)(2,1)} %param.15), channel_id=1, replica_groups=mesh['blk'=64,'rep'=4] {'rep'}, dimensions={0}, use_global_device_ids=true | all-gather | bytes 655360 | tf_op jit(solution)/shard_map/all_gather | solution.py:29
  18.6 305.6 %all-gather.2.cloned.1.call-done = bf16[32768,128]{1,0:T(8,128)(2,1)} async-done(((bf16[512,128]{1,0:T(8,128)(2,1)}), bf16[32768,128]{1,0:T(8,128)(2,1)}) %all-gather.2.cloned.1.call-update) | async-done | bytes 8388624 | tf_op jit(solution)/shard_map/all_gather | solution.py:26
  324.2 5.6 gather_fusion
  329.7 2.3 fusion.2
  332.1 30.4 %all-reduce.1 = bf16[2048,128]{1,0:T(8,128)(2,1)} all-reduce(f32[2048,128]{1,0:T(8,128)S(1)} %bitcast.39), channel_id=1, replica_groups=mesh['blk'=64,'rep'=4] {'rep'}, use_global_device_ids=true, to_apply=%region_0.0 | all-reduce | flops 262144 | bytes 1572864 | tf_op jit(solution)/shard_map/psum | solution.py:28
  362.5 3.7 fusion.11
  366.3 4.0 convolution_convert_fusion
  370.3 2.7 fusion
  373.0 5.6 copy.16
  378.6 7.9 %broadcast_in_dim.2 = f32[256,128,128]{2,1,0:T(8,128)} broadcast(f32[]{:T(128)} %constant.5.clone.1), dimensions={} | broadcast | bytes 16777220 | tf_op jit(solution)/shard_map/broadcast_in_dim | solution.py:47
  386.4 13.6 %scatter_fusion = f32[256,128,128]{2,1,0:T(8,128)} fusion(f32[256,128,128]{2,1,0:T(8,128)} %broadcast_in_dim.2, s32[64]{0:T(128)S(1)} %reshape.64, f32[64,128,128]{2,1,0:T(8,128)} %copy.16), kind=kCustom, calls=%fused_computation.1 | custom fusion | flops 1048576 | bytes 12583168 | tf_op jit(solution)/shard_map/scatter-add | solution.py:47
  400.1 0.0 reduce-scatter.2.cloned.1.call-update
  400.1 3.5 fusion.4
  403.6 0.7 fusion.8
  404.3 346.5 %reduce-scatter.2.cloned.1.call-done = f32[512,128]{1,0:T(8,128)} async-done(((f32[32768,128]{1,0:T(8,128)}), f32[512,128]{1,0:T(8,128)}) %reduce-scatter.2.cloned.1.call-update) | async-done | bytes 262160 | tf_op jit(solution)/shard_map/reduce_scatter | solution.py:50
  750.8 1.6 add_convert_fusion
  (17 shorter events, 0.1 us)
Async XLA Ops:
  7.2 322.6 %copy-start = (bf16[16,1,4,128,128]{4,3,2,1,0:T(8,128)(2,1)S(1)}, bf16[16,1,4,128,128]{4,3,2,1,0:T(8,128)(2,1)}, u32[]{:S(2)}) copy-start(bf16[16,1,4,128,128]{4,3,2,1,0:T(8,128)(2,1)} %param.9) | copy-start | bytes 6291460
  7.2 317.0 %all-gather.2.cloned.1.call-start = ((), (), s32[]{:S(2)}) async-start(), calls=%async_computation.1 | async-start | bytes 8519680 | tf_op jit(solution)/shard_map/all_gather | solution.py:26
  7.9 742.9 %reduce-scatter.2.cloned.1.call-start = ((), (), s32[]{:S(2)}) async-start(), calls=%async_computation.2 | async-start | bytes 17039360 | tf_op jit(solution)/shard_map/reduce_scatter | solution.py:50
  329.7 32.8 %copy-start.4 = (bf16[128,512]{1,0:T(8,128)(2,1)S(1)}, bf16[128,512]{1,0:T(8,128)(2,1)}, u32[]{:S(2)}) copy-start(bf16[128,512]{1,0:T(8,128)(2,1)} %param.11) | copy-start | bytes 393220
  332.1 34.2 %copy-start.6 = (bf16[512,128]{1,0:T(8,128)(2,1)S(1)}, bf16[512,128]{1,0:T(8,128)(2,1)}, u32[]{:S(2)}) copy-start(bf16[512,128]{1,0:T(8,128)(2,1)} %param.13) | copy-start | bytes 393220
  332.1 34.2 %copy-start.7 = (f32[512]{0:T(512)S(1)}, f32[512]{0:T(512)}, u32[]{:S(2)}) copy-start(f32[512]{0:T(512)} %param.12) | copy-start | bytes 6148
  362.5 3.7 copy-start.1
  400.1 3.5 copy-start.3
  400.1 3.5 copy-start.5
  400.1 350.7 %copy-start.2 = (bf16[512,128]{1,0:T(8,128)(2,1)S(1)}, bf16[512,128]{1,0:T(8,128)(2,1)}, u32[]{:S(2)}) copy-start(bf16[512,128]{1,0:T(8,128)(2,1)} %param.15) | copy-start | bytes 393220
Sparse Core Ops, SparseCore 0:
  9.8 314.3 all-gather.1
  400.2 350.5 reduce-scatter.1
where the time goes:
time: 760 us; the launch traced here: 759 us
  waiting for transfers between devices  653 us (86%)
  blocking collectives  39.4 us (5%)
  local copies, waits for them, and re-layouts  20.1 us (3%)
  other arithmetic  16.6 us (2%)
  matrix products  16.2 us (2%)
  between operations  14.1 us (2%)
    reduce_scatter x1, waiting for transfers between devices, local(): lax.psum_scatter(term.reshape(-1, width), 'blk', scatter_dimension=0, til...  346 us
    all_gather x1, waiting for transfers between devices, local(): panels = lax.all_gather(node_feats, 'blk', axis=0, tiled=True)  306 us
    psum x1, blocking collectives, local(): agg_rows = lax.psum(partial_sum, 'rep')  30.4 us
  transfers between devices with their start and end apart: 2, of which 2 were waited for; matrix products, arithmetic and copies ran while one was open for 1% of the time, Pallas kernels for 0%

commit v1 on v0

v1 whole, which is shorter than its diff:
```python
import jax
import jax.numpy as jnp
from jax import lax
from jax.sharding import Mesh
from jax.sharding import PartitionSpec as P

BLOCK = 128
NAMES = ("x", "ylo", "z", "yhi", "core")
BLK = ("x", "ylo", "z")
REP = ("yhi", "core")


def gather_blk(rows):
    part = lax.all_gather(rows, "ylo", axis=0, tiled=False)
    part = lax.all_gather(part, "x", axis=0, tiled=False)
    part = lax.all_gather(part, "z", axis=0, tiled=False)
    return part.reshape(-1, BLOCK, rows.shape[1])


def staged_index(col, per_owner):
    nz = lax.axis_size("z")
    nylo = lax.axis_size("ylo")
    nx = lax.axis_size("x")
    owner = col // per_owner
    sub = col % per_owner
    z = owner % nz
    ylo = (owner // nz) % nylo
    x = owner // (nz * nylo)
    return ((z * nx + x) * nylo + ylo) * per_owner + sub


def tile_products(grouped, adj_tiles, index):
    picked = grouped[index]
    summed = jnp.einsum(
        "rkij,rkjh->rih", adj_tiles[:, 0], picked, preferred_element_type=jnp.float32
    )
    return summed.reshape(-1, grouped.shape[2])


def local(node_feats, adj_tiles, col_index, w_in, b_in, w_out, b_out, cot_out):
    per_owner = node_feats.shape[0] // BLOCK
    index = staged_index(col_index[:, 0, :], per_owner)
    panels = gather_blk(node_feats)
    partial_sum = tile_products(panels, adj_tiles, index)
    agg = lax.psum_scatter(partial_sum, REP, scatter_dimension=0, tiled=True)
    agg_b = agg.astype(jnp.bfloat16)
    pre = jnp.dot(agg_b, w_in, preferred_element_type=jnp.float32) + b_in
    hidden = jax.nn.silu(pre).astype(jnp.bfloat16)
    projected = jnp.dot(hidden, w_out, preferred_element_type=jnp.float32) + b_out
    out_feats = (node_feats.astype(jnp.float32) + projected).astype(jnp.bfloat16)
    g_hidden = jnp.einsum("nh,fh->nf", cot_out, w_out, preferred_element_type=jnp.float32)
    sigma = jax.nn.sigmoid(pre)
    g_pre = (g_hidden * sigma * (1.0 + pre * (1.0 - sigma))).astype(jnp.bfloat16)
    g_agg = jnp.einsum("nf,hf->nh", g_pre, w_in, preferred_element_type=jnp.float32).astype(
        jnp.bfloat16
    )
    g_panels = gather_blk(g_agg)
    back_partial = tile_products(g_panels, adj_tiles, index)
    back_rows = lax.psum_scatter(back_partial, REP, scatter_dimension=0, tiled=True)
    grad_feats = (cot_out.astype(jnp.float32) + back_rows).astype(jnp.bfloat16)
    return (out_feats, grad_feats)


def solution(mesh):
    nblk = mesh.shape["blk"]
    nrep = mesh.shape["rep"]
    fine = Mesh(mesh.devices.reshape(nblk // 16, 2, 8, nrep // 2, 2), NAMES)
    rows = P(BLK + REP, None)
    placed = (
        rows,
        P(BLK, REP, None, None, None),
        P(BLK, REP, None),
        P(),
        P(),
        P(),
        P(),
        rows,
    )
    return jax.shard_map(
        local,
        mesh=fine,
        in_specs=placed,
        out_specs=(rows, rows),
        check_vma=False,
    )
```

time: 760 us -> 371 us (0.49)
  the two profiles are of different devices: /device:TPU:16 before, /device:TPU:9 now
where the time goes in v1:
time: 371 us; the launch traced here: 369 us
  waiting for transfers between devices  320 us (86%)
  between operations  14.2 us (4%)
  local copies, waits for them, and re-layouts  11.4 us (3%)
  matrix products  10.4 us (3%)
  blocking collectives  10.1 us (3%)
    all_gather x2, waiting for transfers between devices, gather_blk(): part = lax.all_gather(part, 'z', axis=0, tiled=False)  193 us
    all_gather x2, waiting for transfers between devices, gather_blk(): part = lax.all_gather(part, 'x', axis=0, tiled=False)  57.9 us
    reduce_scatter x1, waiting for transfers between devices, local(): agg = lax.psum_scatter(partial_sum, REP, scatter_dimension=0, tiled=True)  34.8 us
    reduce_scatter x1, waiting for transfers between devices, local(): lax.psum_scatter(back_partial, REP, scatter_dimension=0, tiled=True)  33.7 us
    gather x2, local copies, waits for them, and re-layouts, tile_products(): picked = grouped[index]  11.2 us
    all_gather x2, blocking collectives, gather_blk(): part = lax.all_gather(rows, 'ylo', axis=0, tiled=False)  10.1 us
  transfers between devices with their start and end apart: 6, of which 6 were waited for; matrix products, arithmetic and copies ran while one was open for 1% of the time, Pallas kernels for 0%

profile of v1, /device:TPU:9, one launch (start us, length us, event | category | flops | bytes accessed | tf_op | source)
XLA Modules:
  0.0 368.5 jit_solution(16021569696241940374)
XLA Ops:
  7.2 4.9 %all-gather = bf16[1024,128]{1,0:T(8,128)(2,1)} all-gather(bf16[512,128]{1,0:T(8,128)(2,1)} %param.8), channel_id=2, replica_groups=mesh['x'=4,'ylo'=2,'z'=8,'yhi'=2,'core'=2] {'ylo'}, dimensions={0}, use_global_device_ids=true | all-gather | bytes 393216 | tf_op jit(solution)/shard_map/all_gather | solution.py:14
  12.2 0.0 all-gather.13.cloned.1.call-start
  12.2 31.1 %all-gather.11.cloned.1.call-done = bf16[8,512,128]{2,1,0:T(8,128)(2,1)} async-done(((bf16[2,512,128]{2,1,0:T(8,128)(2,1)}), bf16[8,512,128]{2,1,0:T(8,128)(2,1)}) %all-gather.11.cloned.1.call-update) | async-done | bytes 1048592 | tf_op jit(solution)/shard_map/all_gather | solution.py:15
  43.3 0.0 reduce-scatter.3.cloned.1.call-start
  43.4 0.7 compare_select_fusion
  44.1 0.1 copy.12
  44.2 0.1 reshape.273
  44.3 96.3 %all-gather.13.cloned.1.call-done = bf16[32,2,512,128]{3,2,1,0:T(8,128)(2,1)} async-done(((bf16[4,2,512,128]{3,2,1,0:T(8,128)(2,1)}), bf16[32,2,512,128]{3,2,1,0:T(8,128)(2,1)}) %all-gather.13.cloned.1.call-update) | async-done | bytes 8388624 | tf_op jit(solution)/shard_map/all_gather | solution.py:16
  140.5 5.6 %gather_fusion = bf16[64,128,128]{2,1,0:T(8,128)(2,1)} fusion(bf16[256,128,128]{2,1,0:T(8,128)(2,1)} %bitcast.60, s32[1024]{0:T(1024)S(1)} %pad_clamp_fusion), kind=kCustom, calls=%fused_computation | custom fusion | bytes 4194560 | tf_op jit(solution)/shard_map/gather | solution.py:33
  146.1 3.3 fusion
  149.5 0.0 all-gather.15.cloned.1.call-start
  149.5 34.8 %reduce-scatter.3.cloned.1.call-done = f32[512,128]{1,0:T(8,128)} async-done(((f32[2048,128]{1,0:T(8,128)}), f32[512,128]{1,0:T(8,128)}) %reduce-scatter.3.cloned.1.call-update) | async-done | bytes 262160 | tf_op jit(solution)/shard_map/reduce_scatter | solution.py:45
  184.3 1.2 convolution_add_fusion
  185.5 1.5 fusion.8
  187.0 5.1 %all-gather.3 = bf16[1024,128]{1,0:T(8,128)(2,1)} all-gather(bf16[512,128]{1,0:T(8,128)(2,1)S(1)} %fusion.8), channel_id=5, replica_groups=mesh['x'=4,'ylo'=2,'z'=8,'yhi'=2,'core'=2] {'ylo'}, dimensions={0}, use_global_device_ids=true | all-gather | bytes 393216 | tf_op jit(solution)/shard_map/all_gather | solution.py:14
  192.2 0.0 all-gather.17.cloned.1.call-start
  192.2 26.9 %all-gather.15.cloned.1.call-done = bf16[8,512,128]{2,1,0:T(8,128)(2,1)} async-done(((bf16[2,512,128]{2,1,0:T(8,128)(2,1)}), bf16[8,512,128]{2,1,0:T(8,128)(2,1)}) %all-gather.15.cloned.1.call-update) | async-done | bytes 1048592 | tf_op jit(solution)/shard_map/all_gather | solution.py:15
  219.1 0.0 reduce-scatter.5.cloned.1.call-start
  219.2 97.1 %all-gather.17.cloned.1.call-done = bf16[32,2,512,128]{3,2,1,0:T(8,128)(2,1)} async-done(((bf16[4,2,512,128]{3,2,1,0:T(8,128)(2,1)}), bf16[32,2,512,128]{3,2,1,0:T(8,128)(2,1)}) %all-gather.17.cloned.1.call-update) | async-done | bytes 8388624 | tf_op jit(solution)/shard_map/all_gather | solution.py:16
  316.3 5.6 %gather_fusion.1 = bf16[64,128,128]{2,1,0:T(8,128)(2,1)} fusion(bf16[256,128,128]{2,1,0:T(8,128)(2,1)} %bitcast.61, s32[1024]{0:T(1024)S(1)} %pad_clamp_fusion), kind=kCustom, calls=%fused_computation.1 | custom fusion | bytes 4194560 | tf_op jit(solution)/shard_map/gather | solution.py:33
  321.9 3.3 fusion.2
  325.3 1.1 fusion.9
  326.4 33.7 %reduce-scatter.5.cloned.1.call-done = f32[512,128]{1,0:T(8,128)} async-done(((f32[2048,128]{1,0:T(8,128)}), f32[512,128]{1,0:T(8,128)}) %reduce-scatter.5.cloned.1.call-update) | async-done | bytes 262160 | tf_op jit(solution)/shard_map/reduce_scatter | solution.py:59
  360.0 1.6 add_convert_fusion
  (22 shorter events, 0.2 us)
Async XLA Ops:
  7.2 139.0 %copy-start = (bf16[16,1,4,128,128]{4,3,2,1,0:T(8,128)(2,1)S(1)}, bf16[16,1,4,128,128]{4,3,2,1,0:T(8,128)(2,1)}, u32[]{:S(2)}) copy-start(bf16[16,1,4,128,128]{4,3,2,1,0:T(8,128)(2,1)} %param.9) | copy-start | bytes 6291460
  7.2 36.1 %all-gather.11.cloned.1.call-start = ((), (), s32[]{:S(2)}) async-start(), calls=%async_computation.4 | async-start | bytes 1310720 | tf_op jit(solution)/shard_map/all_gather | solution.py:15
  12.2 128.3 %all-gather.13.cloned.1.call-start = ((), (), s32[]{:S(2)}) async-start(), calls=%async_computation.5 | async-start | bytes 9437184 | tf_op jit(solution)/shard_map/all_gather | solution.py:16
  43.3 140.9 %reduce-scatter.3.cloned.1.call-start = ((), (), s32[]{:S(2)}) async-start(), calls=%async_computation.2 | async-start | bytes 1310720 | tf_op jit(solution)/shard_map/reduce_scatter | solution.py:45
  146.1 38.2 %copy-start.3 = (bf16[128,512]{1,0:T(8,128)(2,1)S(1)}, bf16[128,512]{1,0:T(8,128)(2,1)}, u32[]{:S(2)}) copy-start(bf16[128,512]{1,0:T(8,128)(2,1)} %param.11) | copy-start | bytes 393220
  146.1 38.2 %copy-start.4 = (f32[512]{0:T(512)S(1)}, f32[512]{0:T(512)}, u32[]{:S(2)}) copy-start(f32[512]{0:T(512)} %param.12) | copy-start | bytes 6148
  149.4 36.1 %copy-start.2 = (bf16[512,128]{1,0:T(8,128)(2,1)S(1)}, bf16[512,128]{1,0:T(8,128)(2,1)}, u32[]{:S(2)}) copy-start(bf16[512,128]{1,0:T(8,128)(2,1)} %param.15) | copy-start | bytes 393220
  149.5 69.6 %all-gather.15.cloned.1.call-start = ((), (), s32[]{:S(2)}) async-start(), calls=%async_computation.6 | async-start | bytes 1310720 | tf_op jit(solution)/shard_map/all_gather | solution.py:15
  192.2 124.1 %all-gather.17.cloned.1.call-start = ((), (), s32[]{:S(2)}) async-start(), calls=%async_computation.7 | async-start | bytes 9437184 | tf_op jit(solution)/shard_map/all_gather | solution.py:16
  219.1 140.9 %reduce-scatter.5.cloned.1.call-start = ((), (), s32[]{:S(2)}) async-start(), calls=%async_computation.3 | async-start | bytes 1310720 | tf_op jit(solution)/shard_map/reduce_scatter | solution.py:59
  321.9 3.3 copy-start.1
  321.9 3.4 copy-start.5
  321.9 3.4 copy-start.6
Sparse Core Ops, SparseCore 0:
  12.3 30.9 all-gather.10
  45.1 95.3 all-gather.12
  149.6 34.6 reduce-scatter.2
  192.3 26.7 all-gather.14
  220.9 95.3 all-gather.16
  325.4 34.6 reduce-scatter.4

commit v2 on v1

--- a/solution.py
+++ b/solution.py
@@ -1,6 +1,10 @@
+import functools
+
 import jax
 import jax.numpy as jnp
 from jax import lax
+from jax.experimental import pallas as pl
+from jax.experimental.pallas import tpu as pltpu
 from jax.sharding import Mesh
 from jax.sharding import PartitionSpec as P
 
@@ -10,23 +14,86 @@
 REP = ("yhi", "core")
 
 
-def gather_blk(rows):
-    part = lax.all_gather(rows, "ylo", axis=0, tiled=False)
-    part = lax.all_gather(part, "x", axis=0, tiled=False)
+def group_place(axes):
+    sizes = [lax.axis_size(a) for a in axes]
+    me = 0
+    for a, n in zip(axes, sizes):
+        me = me * n + lax.axis_index(a)
+    return me, sizes
+
+
+def peer_id(axes, sizes, p):
+    coords = {}
+    for a, n in reversed(list(zip(axes, sizes))):
+        coords[a] = p % n
+        p = p // n
+    return coords
+
+
+def exchange_kernel(axes, gather, src_ref, out_ref, send_sem, recv_sem, local_sem):
+    me, sizes = group_place(axes)
+    n = out_ref.shape[0]
+    barrier = pltpu.get_barrier_semaphore()
+    for d in range(1, n):
+        p = lax.rem(me + d, n)
+        pl.semaphore_signal(barrier, 1, device_id=peer_id(axes, sizes, p))
+    pl.semaphore_wait(barrier, n - 1)
+    copies = []
+    for d in range(1, n):
+        p = lax.rem(me + d, n)
+        copy = pltpu.make_async_remote_copy(
+            src_ref=src_ref if gather else src_ref.at[p],
+            dst_ref=out_ref.at[me],
+            send_sem=send_sem.at[d],
+            recv_sem=recv_sem.at[d],
+            device_id=peer_id(axes, sizes, p),
+        )
+        copy.start()
+        copies.append(copy)
+    own = pltpu.make_async_copy(src_ref if gather else src_ref.at[me], out_ref.at[me], local_sem)
+    own.start()
+    for copy in copies:
+        copy.wait()
+    own.wait()
+
+
+def group_exchange(src, axes, gather, cid):
+    n = 1
+    for a in axes:
+        n *= lax.axis_size(a)
+    block = src.shape if gather else src.shape[1:]
+    return pl.pallas_call(
+        functools.partial(exchange_kernel, axes, gather),
+        out_shape=jax.ShapeDtypeStruct((n, *block), src.dtype),
+        in_specs=[pl.BlockSpec(memory_space=pl.ANY)],
+        out_specs=pl.BlockSpec(memory_space=pl.ANY),
+        scratch_shapes=[
+            pltpu.SemaphoreType.DMA((n,)),
+            pltpu.SemaphoreType.DMA((n,)),
+            pltpu.SemaphoreType.DMA,
+        ],
+        compiler_params=pltpu.CompilerParams(collective_id=cid, has_side_effects=True),
+    )(src)
+
+
+def gather_blk(rows, cid):
+    part = group_exchange(rows, ("x", "ylo"), True, cid)
     part = lax.all_gather(part, "z", axis=0, tiled=False)
     return part.reshape(-1, BLOCK, rows.shape[1])
 
 
+def reduce_rep(partial, cid):
+    nrep = lax.axis_size("yhi") * lax.axis_size("core")
+    pieces = partial.reshape(nrep, -1, partial.shape[1])
+    return jnp.sum(group_exchange(pieces, REP, False, cid), axis=0)
+
+
 def staged_index(col, per_owner):
     nz = lax.axis_size("z")
-    nylo = lax.axis_size("ylo")
-    nx = lax.axis_size("x")
+    nxy = lax.axis_size("x") * lax.axis_size("ylo")
     owner = col // per_owner
     sub = col % per_owner
-    z = owner % nz
-    ylo = (owner // nz) % nylo
-    x = owner // (nz * nylo)
-    return ((z * nx + x) * nylo + ylo) * per_owner + sub
+    return ((owner % nz) * nxy + owner // nz) * per_owner + sub
 
 
 def tile_products(grouped, adj_tiles, index):
@@ -40,9 +107,9 @@
 def local(node_feats, adj_tiles, col_index, w_in, b_in, w_out, b_out, cot_out):
     per_owner = node_feats.shape[0] // BLOCK
     index = staged_index(col_index[:, 0, :], per_owner)
-    panels = gather_blk(node_feats)
+    panels = gather_blk(node_feats, 0)
     partial_sum = tile_products(panels, adj_tiles, index)
-    agg = lax.psum_scatter(partial_sum, REP, scatter_dimension=0, tiled=True)
+    agg = reduce_rep(partial_sum, 2)
     agg_b = agg.astype(jnp.bfloat16)
     pre = jnp.dot(agg_b, w_in, preferred_element_type=jnp.float32) + b_in
     hidden = jax.nn.silu(pre).astype(jnp.bfloat16)
@@ -54,9 +121,9 @@
     g_agg = jnp.einsum("nf,hf->nh", g_pre, w_in, preferred_element_type=jnp.float32).astype(
         jnp.bfloat16
     )
-    g_panels = gather_blk(g_agg)
+    g_panels = gather_blk(g_agg, 1)
     back_partial = tile_products(g_panels, adj_tiles, index)
-    back_rows = lax.psum_scatter(back_partial, REP, scatter_dimension=0, tiled=True)
+    back_rows = reduce_rep(back_partial, 3)
     grad_feats = (cot_out.astype(jnp.float32) + back_rows).astype(jnp.bfloat16)
     return (out_feats, grad_feats)
 

time: 371 us -> 297 us (0.80)
  waiting for transfers between devices: 320 us -> 189 us
  Pallas kernels: 0 us -> 68.4 us
  blocking collectives: 10.1 us -> 0 us
    reduce_scatter x2 -> x0, waiting for transfers between devices: 68.5 us -> none  [the longest x1 34.8 us: local(): agg = lax.psum_scatter(partial_sum, REP, scatter_dimension=0, tiled=True)]
    pallas_call x0 -> x4, Pallas kernels: none -> 68.4 us  [group_exchange(): pl.pallas_call(functools.partial(exchange_kernel, axes, gather), out_shap...]
    all_gather x2 -> x0, waiting for transfers between devices: 57.9 us -> none  [gather_blk(): part = lax.all_gather(part, 'x', axis=0, tiled=False)]
    all_gather x2 -> x0, blocking collectives: 10.1 us -> none  [gather_blk(): part = lax.all_gather(rows, 'ylo', axis=0, tiled=False)]
    all_gather x2, waiting for transfers between devices: 193 us -> 189 us  [gather_blk(): part = lax.all_gather(part, 'z', axis=0, tiled=False)]
  transfers between devices with their start and end apart: 6 -> 2, of which waited for: 6 -> 2; matrix products, arithmetic and copies ran while one was open for 1% -> 0% of each run, Pallas kernels for 0% -> 0%
where the time goes in v2:
time: 297 us; the launch traced here: 296 us
  waiting for transfers between devices  189 us (64%)
  Pallas kernels  68.4 us (23%)
  between operations  14.2 us (5%)
  local copies, waits for them, and re-layouts  11.3 us (4%)
  matrix products  10 us (3%)
  other arithmetic  3.31 us (1%)
    all_gather x2, waiting for transfers between devices, gather_blk(): part = lax.all_gather(part, 'z', axis=0, tiled=False)  189 us
    pallas_call x4, Pallas kernels, group_exchange(): pl.pallas_call(functools.partial(exchange_kernel, axes, gather), out_shap...  68.4 us
    gather x2, local copies, waits for them, and re-layouts, tile_products(): picked = grouped[index]  11.1 us
    dot_general x2, matrix products, tile_products(): jnp.einsum('rkij,rkjh->rih', adj_tiles[:, 0], picked, preferred_element_t...  6.51 us
  transfers between devices with their start and end apart: 2, of which 2 were waited for; matrix products, arithmetic and copies ran while one was open for 0% of the time, Pallas kernels for 0%

profile of v2, /device:TPU:9, one launch (start us, length us, event | category | flops | bytes accessed | tf_op | source)
XLA Modules:
  0.0 296.2 jit_solution(4023236236600116213)
XLA Ops:
  7.2 0.0 copy-start
  7.2 0.0 copy-start.5
  7.2 0.0 all-gather.5.cloned.1.call-start
  7.2 17.1 %shard_map.95 = bf16[8,512,128]{2,1,0:T(8,128)(2,1)} custom-call(bf16[512,128]{1,0:T(8,128)(2,1)} %src_ref.1), custom_call_target="tpu_custom_call" | custom-call | tf_op jit(solution)/shard_map/pallas_call | solution.py:65
  24.3 0.0 all-gather.5.cloned.1.call-update
  24.4 0.0 all-gather.7.cloned.1.call-start
  24.5 0.1 copy.12
  24.5 0.1 reshape.196
  24.6 97.7 %all-gather.5.cloned.1.call-done = bf16[64,512,128]{2,1,0:T(8,128)(2,1)} async-done(((bf16[8,512,128]{2,1,0:T(8,128)(2,1)}), bf16[64,512,128]{2,1,0:T(8,128)(2,1)}) %all-gather.5.cloned.1.call-update) | async-done | bytes 8388624 | tf_op jit(solution)/shard_map/all_gather | solution.py:81
  122.3 5.6 %gather_fusion = bf16[64,128,128]{2,1,0:T(8,128)(2,1)} fusion(bf16[256,128,128]{2,1,0:T(8,128)(2,1)} %bitcast.53, s32[1024]{0:T(1024)S(1)} %pad_clamp_fusion), kind=kCustom, calls=%fused_computation | custom fusion | bytes 4194560 | tf_op jit(solution)/shard_map/gather | solution.py:100
  127.9 3.3 %fusion = f32[16,128,128,1]{1,2,3,0:T(8,128)} fusion(bf16[16,4,128,128]{3,2,1,0:T(8,128)(2,1)} %bitcast.50, bf16[16,1,4,128,128]{4,3,2,1,0:T(8,128)(2,1)S(1)} %copy-done), kind=kOutput, calls=%fused_computation.2 | convolution fusion | flops 268435456 | bytes 5242880 | tf_op jit(solution)/shard_map/rkij,rkjh->rih/dot_general | solution.py:101
  131.2 16.1 %shard_map.96 = f32[4,512,128]{2,1,0:T(8,128)} custom-call(f32[4,512,128]{2,1,0:T(8,128)} %bitcast.51), custom_call_target="tpu_custom_call" | custom-call | tf_op jit(solution)/shard_map/pallas_call | solution.py:65
  147.3 1.3 reduce_sum.18
  148.6 0.3 convolution_add_fusion
  148.9 2.1 fusion.8.src_ref
  151.1 19.0 %shard_map.97 = bf16[8,512,128]{2,1,0:T(8,128)(2,1)} custom-call(bf16[512,128]{1,0:T(8,128)(2,1)} %fusion.8.src_ref), custom_call_target="tpu_custom_call" | custom-call | tf_op jit(solution)/shard_map/pallas_call | solution.py:65
  170.1 0.0 all-gather.7.cloned.1.call-update
  170.1 1.1 fusion.9
  171.2 91.2 %all-gather.7.cloned.1.call-done = bf16[64,512,128]{2,1,0:T(8,128)(2,1)} async-done(((bf16[8,512,128]{2,1,0:T(8,128)(2,1)}), bf16[64,512,128]{2,1,0:T(8,128)(2,1)}) %all-gather.7.cloned.1.call-update) | async-done | bytes 8388624 | tf_op jit(solution)/shard_map/all_gather | solution.py:81
  262.4 5.6 %gather_fusion.1 = bf16[64,128,128]{2,1,0:T(8,128)(2,1)} fusion(bf16[256,128,128]{2,1,0:T(8,128)(2,1)} %bitcast.54, s32[1024]{0:T(1024)S(1)} %pad_clamp_fusion), kind=kCustom, calls=%fused_computation.1 | custom fusion | bytes 4194560 | tf_op jit(solution)/shard_map/gather | solution.py:100
  268.0 3.3 %fusion.2 = f32[16,128,128,1]{1,2,3,0:T(8,128)} fusion(bf16[16,4,128,128]{3,2,1,0:T(8,128)(2,1)} %bitcast.49, bf16[16,1,4,128,128]{4,3,2,1,0:T(8,128)(2,1)S(1)} %copy-done), kind=kOutput, calls=%fused_computation.4 | convolution fusion | flops 268435456 | bytes 5242880 | tf_op jit(solution)/shard_map/rkij,rkjh->rih/dot_general | solution.py:101
  271.2 16.1 %shard_map.98 = f32[4,512,128]{2,1,0:T(8,128)} custom-call(f32[4,512,128]{2,1,0:T(8,128)} %bitcast.52), custom_call_target="tpu_custom_call" | custom-call | tf_op jit(solution)/shard_map/pallas_call | solution.py:65
  287.4 1.3 reduce_sum.19
  288.7 0.7 add_convert_fusion
  (16 shorter events, 0.1 us)
Async XLA Ops:
  7.2 120.7 %copy-start = (bf16[16,1,4,128,128]{4,3,2,1,0:T(8,128)(2,1)S(1)}, bf16[16,1,4,128,128]{4,3,2,1,0:T(8,128)(2,1)}, u32[]{:S(2)}) copy-start(bf16[16,1,4,128,128]{4,3,2,1,0:T(8,128)(2,1)} %param.9) | copy-start | bytes 6291460
  7.2 17.2 %copy-start.5 = (s32[16,1,4]{0,2,1:T(4,128)S(1)}, s32[16,1,4]{0,2,1:T(4,128)}, u32[]{:S(2)}) copy-start(s32[16,1,4]{0,2,1:T(4,128)} %param.10) | copy-start | bytes 772
  7.2 115.1 %all-gather.5.cloned.1.call-start = ((), (), s32[]{:S(2)}) async-start(), calls=%async_computation | async-start | bytes 9437184 | tf_op jit(solution)/shard_map/all_gather | solution.py:81
  24.4 238.0 %all-gather.7.cloned.1.call-start = ((), (), s32[]{:S(2)}) async-start(), calls=%async_computation.1 | async-start | bytes 9437184 | tf_op jit(solution)/shard_map/all_gather | solution.py:81
  131.2 17.5 %copy-start.1 = (bf16[128,512]{1,0:T(8,128)(2,1)S(1)}, bf16[128,512]{1,0:T(8,128)(2,1)}, u32[]{:S(2)}) copy-start(bf16[128,512]{1,0:T(8,128)(2,1)} %param.11) | copy-start | bytes 393220
  131.2 17.5 %copy-start.4 = (f32[512]{0:T(512)S(1)}, f32[512]{0:T(512)}, u32[]{:S(2)}) copy-start(f32[512]{0:T(512)} %param.12) | copy-start | bytes 6148
  131.2 17.8 %copy-start.3 = (bf16[512,128]{1,0:T(8,128)(2,1)S(1)}, bf16[512,128]{1,0:T(8,128)(2,1)}, u32[]{:S(2)}) copy-start(bf16[512,128]{1,0:T(8,128)(2,1)} %param.15) | copy-start | bytes 393220
  151.0 19.1 %copy-start.2 = (bf16[512,128]{1,0:T(8,128)(2,1)S(1)}, bf16[512,128]{1,0:T(8,128)(2,1)}, u32[]{:S(2)}) copy-start(bf16[512,128]{1,0:T(8,128)(2,1)} %src_ref.1) | copy-start | bytes 393220
  151.0 19.1 %copy-start.6 = (bf16[512,128]{1,0:T(8,128)(2,1)S(1)}, bf16[512,128]{1,0:T(8,128)(2,1)}, u32[]{:S(2)}) copy-start(bf16[512,128]{1,0:T(8,128)(2,1)} %param.13) | copy-start | bytes 393220
  151.0 19.1 %copy-start.7 = (f32[128]{0:T(128)S(1)}, f32[128]{0:T(128)}, u32[]{:S(2)}) copy-start(f32[128]{0:T(128)} %param.14) | copy-start | bytes 1540
Sparse Core Ops, SparseCore 0:
  24.5 97.7 all-gather.4
  170.2 92.1 all-gather.6

commit v3 on v2

--- a/solution.py
+++ b/solution.py
@@ -77,9 +77,13 @@
 
 
 def gather_blk(rows, cid):
-    part = group_exchange(rows, ("x", "ylo"), True, cid)
-    part = lax.all_gather(part, "z", axis=0, tiled=False)
-    return part.reshape(-1, BLOCK, rows.shape[1])
+    half = rows.shape[0] // 2
+    first = group_exchange(rows[:half], ("x", "ylo"), True, cid)
+    first = lax.all_gather(first, "z", axis=0, tiled=False)
+    second = lax.all_gather(rows[half:], "z", axis=0, tiled=False)
+    second = group_exchange(second, ("x", "ylo"), True, cid + 4)
+    width = rows.shape[1]
+    return first.reshape(-1, BLOCK, width), second.reshape(-1, BLOCK, width)
 
 
 def reduce_rep(partial, cid):
@@ -91,17 +95,24 @@
 def staged_index(col, per_owner):
     nz = lax.axis_size("z")
     nxy = lax.axis_size("x") * lax.axis_size("ylo")
+    half = per_owner // 2
     owner = col // per_owner
     sub = col % per_owner
-    return ((owner % nz) * nxy + owner // nz) * per_owner + sub
+    z = owner % nz
+    xy = owner // nz
+    in_first = sub < half
+    first = (z * nxy + xy) * half + jnp.where(in_first, sub, 0)
+    second = (xy * nz + z) * half + jnp.where(in_first, 0, sub - half)
+    return in_first, first, second
 
 
-def tile_products(grouped, adj_tiles, index):
-    picked = grouped[index]
+def tile_products(panels, adj_tiles, index):
+    in_first, first, second = index
+    picked = jnp.where(in_first[..., None, None], panels[0][first], panels[1][second])
     summed = jnp.einsum(
         "rkij,rkjh->rih", adj_tiles[:, 0], picked, preferred_element_type=jnp.float32
     )
-    return summed.reshape(-1, grouped.shape[2])
+    return summed.reshape(-1, panels[0].shape[2])
 
 
 def local(node_feats, adj_tiles, col_index, w_in, b_in, w_out, b_out, cot_out):
@@ -109,7 +120,7 @@
     index = staged_index(col_index[:, 0, :], per_owner)
     panels = gather_blk(node_feats, 0)
     partial_sum = tile_products(panels, adj_tiles, index)
-    agg = reduce_rep(partial_sum, 2)
+    agg = reduce_rep(partial_sum, 8)
     agg_b = agg.astype(jnp.bfloat16)
     pre = jnp.dot(agg_b, w_in, preferred_element_type=jnp.float32) + b_in
     hidden = jax.nn.silu(pre).astype(jnp.bfloat16)
@@ -123,7 +134,7 @@
     )
     g_panels = gather_blk(g_agg, 1)
     back_partial = tile_products(g_panels, adj_tiles, index)
-    back_rows = reduce_rep(back_partial, 3)
+    back_rows = reduce_rep(back_partial, 9)
     grad_feats = (cot_out.astype(jnp.float32) + back_rows).astype(jnp.bfloat16)
     return (out_feats, grad_feats)
 

time: 297 us -> 296 us (level)
  waiting for transfers between devices: 189 us -> 0.04 us
  Pallas kernels: 68.4 us -> 194 us
  blocking collectives: 0 us -> 50.5 us
  local copies, waits for them, and re-layouts: 11.3 us -> 20.2 us
    all_gather x2, waiting for transfers between devices: 189 us -> 0.01 us  [gather_blk(): first = lax.all_gather(first, 'z', axis=0, tiled=False)]
    pallas_call x4 -> x6, Pallas kernels: 68.4 us -> 194 us  [group_exchange(): pl.pallas_call(functools.partial(exchange_kernel, axes, gather), out_shap...]
    all_gather x0 -> x2, blocking collectives: none -> 50.5 us  [gather_blk(): second = lax.all_gather(rows[half:], 'z', axis=0, tiled=False)]
    gather x2 -> x4, local copies, waits for them, and re-layouts: 11.1 us -> 17.4 us  [the longest x2 8.77 us: tile_products(): panels[1][second]]
  transfers between devices with their start and end apart: 2 -> 2, of which waited for: 2 -> 0; matrix products, arithmetic and copies ran while one was open for 0% -> 4% of each run, Pallas kernels for 0% -> 45%
where the time goes in v3:
time: 296 us; the launch traced here: 295 us
  Pallas kernels  194 us (66%)
  blocking collectives  50.5 us (17%)
  local copies, waits for them, and re-layouts  20.2 us (7%)
  between operations  14.2 us (5%)
  matrix products  11 us (4%)
  other arithmetic  4.69 us (2%)
    pallas_call x6, Pallas kernels, group_exchange(): pl.pallas_call(functools.partial(exchange_kernel, axes, gather), out_shap...  194 us
    all_gather x2, blocking collectives, gather_blk(): second = lax.all_gather(rows[half:], 'z', axis=0, tiled=False)  50.5 us
    gather x2, local copies, waits for them, and re-layouts, tile_products(): panels[1][second]  8.77 us
    gather x2, local copies, waits for them, and re-layouts, tile_products(): panels[0][first]  8.66 us
    dot_general x2, matrix products, tile_products(): jnp.einsum('rkij,rkjh->rih', adj_tiles[:, 0], picked, preferred_element_t...  8.1 us
  transfers between devices with their start and end apart: 2, of which 0 were waited for; matrix products, arithmetic and copies ran while one was open for 4% of the time, Pallas kernels for 45%

profile of v3, /device:TPU:9, one launch (start us, length us, event | category | flops | bytes accessed | tf_op | source)
XLA Modules:
  0.0 294.6 jit_solution(17877954647054968427)
XLA Ops:
  7.2 1.7 fusion.29
  8.9 10.7 %shard_map.95 = bf16[8,256,128]{2,1,0:T(8,128)(2,1)} custom-call(bf16[256,128]{1,0:T(8,128)(2,1)} %get-tuple-element.5.src_ref), custom_call_target="tpu_custom_call" | custom-call | tf_op jit(solution)/shard_map/pallas_call | solution.py:65
  19.6 0.7 fusion.22
  20.4 0.7 compare_select_fusion
  21.5 26.8 %all-gather.1 = bf16[2048,128]{1,0:T(8,128)(2,1)} all-gather(bf16[256,128]{1,0:T(8,128)(2,1)S(1)} %get-tuple-element.4), channel_id=3, replica_groups=mesh['x'=4,'ylo'=2,'z'=8,'yhi'=2,'core'=2] {'z'}, dimensions={0}, use_global_device_ids=true | all-gather | bytes 589824 | tf_op jit(solution)/shard_map/all_gather | solution.py:83
  48.3 66.8 %shard_map.96 = bf16[8,8,256,128]{3,2,1,0:T(8,128)(2,1)} custom-call(bf16[8,256,128]{2,1,0:T(8,128)(2,1)} %bitcast.77), custom_call_target="tpu_custom_call" | custom-call | tf_op jit(solution)/shard_map/pallas_call | solution.py:65
  115.1 4.4 %gather_fusion.1 = bf16[64,128,128]{2,1,0:T(8,128)(2,1)} fusion(bf16[128,128,128]{2,1,0:T(8,128)(2,1)} %bitcast.69, s32[1024]{0:T(1024)S(1)} %pad_clamp_fusion), kind=kCustom, calls=%fused_computation.1 | custom fusion | bytes 4194560 | tf_op jit(solution)/shard_map/gather | solution.py:111
  119.4 4.3 %gather_fusion = bf16[64,128,128]{2,1,0:T(8,128)(2,1)} fusion(bf16[128,128,128]{2,1,0:T(8,128)(2,1)} %bitcast.79, s32[1024]{0:T(1024)S(1)} %pad_clamp_fusion.1), kind=kCustom, calls=%fused_computation | custom fusion | bytes 4194560 | tf_op jit(solution)/shard_map/gather | solution.py:111
  123.8 4.0 %fusion = f32[16,128,128,1]{1,2,3,0:T(8,128)} fusion(bf16[16,1,4,128,128]{4,3,2,1,0:T(8,128)(2,1)S(1)} %copy-done, bf16[16,4,128,128]{3,2,1,0:T(8,128)(2,1)} %bitcast.74, bf16[16,4,128,128]{3,2,1,0:T(8,128)(2,1)} %bitcast.72, pred[16,4]{1,0:T(8,128)(4,1)S(1)} %copy.16), kind=kOutput, calls=%fused_computation.4 | convolution fusion | flops 269484032 | bytes 7340096 | tf_op jit(solution)/shard_map/rkij,rkjh->rih/dot_general | solution.py:112
  127.8 18.8 %shard_map.97 = f32[4,512,128]{2,1,0:T(8,128)} custom-call(f32[4,512,128]{2,1,0:T(8,128)} %bitcast.76), custom_call_target="tpu_custom_call" | custom-call | tf_op jit(solution)/shard_map/pallas_call | solution.py:65
  146.6 1.3 reduce_sum.18
  147.9 0.3 convolution_add_fusion
  148.2 1.5 fusion.12
  149.7 0.6 fusion.28
  150.4 12.8 %shard_map.98 = bf16[8,256,128]{2,1,0:T(8,128)(2,1)} custom-call(bf16[256,128]{1,0:T(8,128)(2,1)} %get-tuple-element.3.src_ref), custom_call_target="tpu_custom_call" | custom-call | tf_op jit(solution)/shard_map/pallas_call | solution.py:65
  163.2 23.6 %all-gather.3 = bf16[2048,128]{1,0:T(8,128)(2,1)} all-gather(bf16[256,128]{1,0:T(8,128)(2,1)S(1)} %get-tuple-element.2), channel_id=5, replica_groups=mesh['x'=4,'ylo'=2,'z'=8,'yhi'=2,'core'=2] {'z'}, dimensions={0}, use_global_device_ids=true | all-gather | bytes 589824 | tf_op jit(solution)/shard_map/all_gather | solution.py:83
  186.8 66.4 %shard_map.99 = bf16[8,8,256,128]{3,2,1,0:T(8,128)(2,1)} custom-call(bf16[8,256,128]{2,1,0:T(8,128)(2,1)} %bitcast.78), custom_call_target="tpu_custom_call" | custom-call | tf_op jit(solution)/shard_map/pallas_call | solution.py:65
  253.3 4.4 %gather_fusion.3 = bf16[64,128,128]{2,1,0:T(8,128)(2,1)} fusion(bf16[128,128,128]{2,1,0:T(8,128)(2,1)} %bitcast.70, s32[1024]{0:T(1024)S(1)} %pad_clamp_fusion), kind=kCustom, calls=%fused_computation.3 | custom fusion | bytes 4194560 | tf_op jit(solution)/shard_map/gather | solution.py:111
  257.7 1.1 fusion.13
  258.8 4.3 %gather_fusion.2 = bf16[64,128,128]{2,1,0:T(8,128)(2,1)} fusion(bf16[128,128,128]{2,1,0:T(8,128)(2,1)} %bitcast.80, s32[1024]{0:T(1024)S(1)} %pad_clamp_fusion.1), kind=kCustom, calls=%fused_computation.2 | custom fusion | bytes 4194560 | tf_op jit(solution)/shard_map/gather | solution.py:111
  263.1 4.0 %fusion.2 = f32[16,128,128,1]{1,2,3,0:T(8,128)} fusion(bf16[16,1,4,128,128]{4,3,2,1,0:T(8,128)(2,1)S(1)} %copy-done, bf16[16,4,128,128]{3,2,1,0:T(8,128)(2,1)} %bitcast.73, bf16[16,4,128,128]{3,2,1,0:T(8,128)(2,1)} %bitcast.71, pred[16,4]{1,0:T(8,128)(4,1)S(1)} %copy.16), kind=kOutput, calls=%fused_computation.6 | convolution fusion | flops 269484032 | bytes 7340096 | tf_op jit(solution)/shard_map/rkij,rkjh->rih/dot_general | solution.py:112
  267.2 18.6 %shard_map.100 = f32[4,512,128]{2,1,0:T(8,128)} custom-call(f32[4,512,128]{2,1,0:T(8,128)} %bitcast.75), custom_call_target="tpu_custom_call" | custom-call | tf_op jit(solution)/shard_map/pallas_call | solution.py:65
  285.8 1.3 reduce_sum.19
  287.1 0.7 add_convert_fusion
  (27 shorter events, 0.6 us)
Async XLA Ops:
  7.2 116.6 %copy-start = (bf16[16,1,4,128,128]{4,3,2,1,0:T(8,128)(2,1)S(1)}, bf16[16,1,4,128,128]{4,3,2,1,0:T(8,128)(2,1)}, u32[]{:S(2)}) copy-start(bf16[16,1,4,128,128]{4,3,2,1,0:T(8,128)(2,1)} %param.9) | copy-start | bytes 6291460
  7.2 112.3 %all-gather.7.cloned.1.call-start = ((), (), s32[]{:S(2)}) async-start(), calls=%async_computation | async-start | bytes 4718592 | tf_op jit(solution)/shard_map/all_gather | solution.py:82
  19.6 239.2 %all-gather.9.cloned.1.call-start = ((), (), s32[]{:S(2)}) async-start(), calls=%async_computation.1 | async-start | bytes 4718592 | tf_op jit(solution)/shard_map/all_gather | solution.py:82
  127.8 20.1 %copy-start.1 = (bf16[128,512]{1,0:T(8,128)(2,1)S(1)}, bf16[128,512]{1,0:T(8,128)(2,1)}, u32[]{:S(2)}) copy-start(bf16[128,512]{1,0:T(8,128)(2,1)} %param.11) | copy-start | bytes 393220
  127.8 20.1 %copy-start.4 = (f32[512]{0:T(512)S(1)}, f32[512]{0:T(512)}, u32[]{:S(2)}) copy-start(f32[512]{0:T(512)} %param.12) | copy-start | bytes 6148
  253.2 4.4 %copy-start.2 = (bf16[512,128]{1,0:T(8,128)(2,1)S(1)}, bf16[512,128]{1,0:T(8,128)(2,1)}, u32[]{:S(2)}) copy-start(bf16[512,128]{1,0:T(8,128)(2,1)} %param.8) | copy-start | bytes 393220
  253.2 4.4 %copy-start.5 = (bf16[512,128]{1,0:T(8,128)(2,1)S(1)}, bf16[512,128]{1,0:T(8,128)(2,1)}, u32[]{:S(2)}) copy-start(bf16[512,128]{1,0:T(8,128)(2,1)} %param.13) | copy-start | bytes 393220
  253.3 4.4 %copy-start.6 = (f32[128]{0:T(128)S(1)}, f32[128]{0:T(128)}, u32[]{:S(2)}) copy-start(f32[128]{0:T(128)} %param.14) | copy-start | bytes 1540
  267.2 19.9 %copy-start.3 = (bf16[512,128]{1,0:T(8,128)(2,1)S(1)}, bf16[512,128]{1,0:T(8,128)(2,1)}, u32[]{:S(2)}) copy-start(bf16[512,128]{1,0:T(8,128)(2,1)} %param.15) | copy-start | bytes 393220
Sparse Core Ops, SparseCore 0:
  19.7 61.0 all-gather.6
  163.3 53.1 all-gather.8

commit v4 on v3

--- a/solution.py
+++ b/solution.py
@@ -30,58 +30,75 @@
     return coords
 
 
-def exchange_kernel(axes, gather, src_ref, out_ref, send_sem, recv_sem, local_sem):
-    me, sizes = group_place(axes)
-    n = out_ref.shape[0]
+def exchange_kernel(jobs, *refs):
+    count = len(jobs)
+    src_refs, out_refs = refs[:count], refs[count : 2 * count]
+    send_sem, recv_sem, local_sem = refs[2 * count :]
+    places = [group_place(axes) for axes, _ in jobs]
     barrier = pltpu.get_barrier_semaphore()
-    for d in range(1, n):
-        p = lax.rem(me + d, n)
-        pl.semaphore_signal(barrier, 1, device_id=peer_id(axes, sizes, p))
-    pl.semaphore_wait(barrier, n - 1)
+    total = 0
+    for (axes, _), (me, sizes), out_ref in zip(jobs, places, out_refs):
+        n = out_ref.shape[0]
+        total += n - 1
+        for d in range(1, n):
+            p = lax.rem(me + d, n)
+            pl.semaphore_signal(barrier, 1, device_id=peer_id(axes, sizes, p))
+    pl.semaphore_wait(barrier, total)
     copies = []
-    for d in range(1, n):
-        p = lax.rem(me + d, n)
-        copy = pltpu.make_async_remote_copy(
-            src_ref=src_ref if gather else src_ref.at[p],
-            dst_ref=out_ref.at[me],
-            send_sem=send_sem.at[d],
-            recv_sem=recv_sem.at[d],
-            device_id=peer_id(axes, sizes, p),
+    for j, ((axes, gather), (me, sizes)) in enumerate(zip(jobs, places)):
+        src_ref, out_ref = src_refs[j], out_refs[j]
+        n = out_ref.shape[0]
+        for d in range(1, n):
+            p = lax.rem(me + d, n)
+            copy = pltpu.make_async_remote_copy(
+                src_ref=src_ref if gather else src_ref.at[p],
+                dst_ref=out_ref.at[me],
+                send_sem=send_sem.at[j, d],
+                recv_sem=recv_sem.at[j, d],
+                device_id=peer_id(axes, sizes, p),
+            )
+            copy.start()
+            copies.append(copy)
+        own = pltpu.make_async_copy(
+            src_ref if gather else src_ref.at[me], out_ref.at[me], local_sem.at[j]
         )
-        copy.start()
-        copies.append(copy)
-    own = pltpu.make_async_copy(src_ref if gather else src_ref.at[me], out_ref.at[me], local_sem)
-    own.start()
+        own.start()
+        copies.append(own)
     for copy in copies:
         copy.wait()
-    own.wait()
 
 
-def group_exchange(src, axes, gather, cid):
-    n = 1
-    for a in axes:
-        n *= lax.axis_size(a)
-    block = src.shape if gather else src.shape[1:]
+def group_exchange(srcs, jobs, cid):
+    shapes = []
+    most = 1
+    for src, (axes, gather) in zip(srcs, jobs):
+        n = 1
+        for a in axes:
+            n *= lax.axis_size(a)
+        most = max(most, n)
+        block = src.shape if gather else src.shape[1:]
+        shapes.append(jax.ShapeDtypeStruct((n, *block), src.dtype))
+    count = len(jobs)
     return pl.pallas_call(
-        functools.partial(exchange_kernel, axes, gather),
-        out_shape=jax.ShapeDtypeStruct((n, *block), src.dtype),
-        in_specs=[pl.BlockSpec(memory_space=pl.ANY)],
-        out_specs=pl.BlockSpec(memory_space=pl.ANY),
+        functools.partial(exchange_kernel, tuple(jobs)),
+        out_shape=tuple(shapes),
+        in_specs=[pl.BlockSpec(memory_space=pl.ANY)] * count,
+        out_specs=tuple([pl.BlockSpec(memory_space=pl.ANY)] * count),
         scratch_shapes=[
-            pltpu.SemaphoreType.DMA((n,)),
-            pltpu.SemaphoreType.DMA((n,)),
-            pltpu.SemaphoreType.DMA,
+            pltpu.SemaphoreType.DMA((count, most)),
+            pltpu.SemaphoreType.DMA((count, most)),
+            pltpu.SemaphoreType.DMA((count,)),
         ],
         compiler_params=pltpu.CompilerParams(collective_id=cid, has_side_effects=True),
-    )(src)
+    )(*srcs)
 
 
 def gather_blk(rows, cid):
     half = rows.shape[0] // 2
-    first = group_exchange(rows[:half], ("x", "ylo"), True, cid)
+    xy = (("x", "ylo"), True)
+    first, second = group_exchange((rows[:half], rows[half:]), (xy, (("z",), True)), cid)
     first = lax.all_gather(first, "z", axis=0, tiled=False)
-    second = lax.all_gather(rows[half:], "z", axis=0, tiled=False)
-    second = group_exchange(second, ("x", "ylo"), True, cid + 4)
+    (second,) = group_exchange((second,), (xy,), cid + 4)
     width = rows.shape[1]
     return first.reshape(-1, BLOCK, width), second.reshape(-1, BLOCK, width)
 
@@ -89,7 +106,8 @@
 def reduce_rep(partial, cid):
     nrep = lax.axis_size("yhi") * lax.axis_size("core")
     pieces = partial.reshape(nrep, -1, partial.shape[1])
-    return jnp.sum(group_exchange(pieces, REP, False, cid), axis=0)
+    (pieces,) = group_exchange((pieces,), ((REP, False),), cid)
+    return jnp.sum(pieces, axis=0)
 
 
 def staged_index(col, per_owner):

time: 296 us -> 270 us (0.912)
  blocking collectives: 50.5 us -> 0 us
  Pallas kernels: 194 us -> 219 us
    all_gather x2 -> x0, blocking collectives: 50.5 us -> none  [gather_blk(): second = lax.all_gather(rows[half:], 'z', axis=0, tiled=False)]
    pallas_call x6, Pallas kernels: 194 us -> 219 us  [group_exchange(): pl.pallas_call(functools.partial(exchange_kernel, tuple(jobs)), out_shape...]
  transfers between devices with their start and end apart: 2 -> 2, of which waited for: 0 -> 0; matrix products, arithmetic and copies ran while one was open for 4% -> 4% of each run, Pallas kernels for 45% -> 55%
where the time goes in v4:
time: 270 us; the launch traced here: 269 us
  Pallas kernels  219 us (81%)
  local copies, waits for them, and re-layouts  20.3 us (8%)
  between operations  14.2 us (5%)
  matrix products  10.9 us (4%)
  other arithmetic  4.69 us (2%)
    pallas_call x6, Pallas kernels, group_exchange(): pl.pallas_call(functools.partial(exchange_kernel, tuple(jobs)), out_shape...  219 us
    gather x2, local copies, waits for them, and re-layouts, tile_products(): panels[1][second]  8.79 us
    gather x2, local copies, waits for them, and re-layouts, tile_products(): panels[0][first]  8.64 us
    dot_general x2, matrix products, tile_products(): jnp.einsum('rkij,rkjh->rih', adj_tiles[:, 0], picked, preferred_element_t...  8.06 us
  transfers between devices with their start and end apart: 2, of which 0 were waited for; matrix products, arithmetic and copies ran while one was open for 4% of the time, Pallas kernels for 55%

profile of v4, /device:TPU:9, one launch (start us, length us, event | category | flops | bytes accessed | tf_op | source)
XLA Modules:
  0.0 269.1 jit_solution(15254380615000261923)
XLA Ops:
  7.2 1.7 fusion.29
  8.9 20.3 %shard_map.95 = (bf16[8,256,128]{2,1,0:T(8,128)(2,1)}, bf16[8,256,128]{2,1,0:T(8,128)(2,1)}) custom-call(bf16[256,128]{1,0:T(8,128)(2,1)} %get-tuple-element.13.refs_0_, bf16[256,128]{1,0:T(8,128)(2,1)} %get-tuple-element.12.refs_1_), custom_call_target="tpu_custom_call" | custom-call | tf_op jit(solution)/shard_map/pallas_call | solution.py:82
  29.3 0.7 fusion.22
  29.9 0.1 copy.16
  30.0 0.7 compare_select_fusion
  31.0 0.1 reshape.275
  31.1 71.4 %shard_map.96 = bf16[8,8,256,128]{3,2,1,0:T(8,128)(2,1)} custom-call(bf16[8,256,128]{2,1,0:T(8,128)(2,1)} %get-tuple-element.7.refs_0_), custom_call_target="tpu_custom_call" | custom-call | tf_op jit(solution)/shard_map/pallas_call | solution.py:82
  102.5 4.4 %gather_fusion.1 = bf16[64,128,128]{2,1,0:T(8,128)(2,1)} fusion(bf16[128,128,128]{2,1,0:T(8,128)(2,1)} %bitcast.67, s32[1024]{0:T(1024)S(1)} %pad_clamp_fusion), kind=kCustom, calls=%fused_computation.1 | custom fusion | bytes 4194560 | tf_op jit(solution)/shard_map/gather | solution.py:129
  106.9 4.3 %gather_fusion = bf16[64,128,128]{2,1,0:T(8,128)(2,1)} fusion(bf16[128,128,128]{2,1,0:T(8,128)(2,1)} %bitcast.75, s32[1024]{0:T(1024)S(1)} %pad_clamp_fusion.1), kind=kCustom, calls=%fused_computation | custom fusion | bytes 4194560 | tf_op jit(solution)/shard_map/gather | solution.py:129
  111.2 4.0 %fusion = f32[16,128,128,1]{1,2,3,0:T(8,128)} fusion(bf16[16,1,4,128,128]{4,3,2,1,0:T(8,128)(2,1)S(1)} %copy-done, bf16[16,4,128,128]{3,2,1,0:T(8,128)(2,1)} %bitcast.72, bf16[16,4,128,128]{3,2,1,0:T(8,128)(2,1)} %bitcast.70, pred[16,4]{1,0:T(8,128)(4,1)S(1)} %copy.16), kind=kOutput, calls=%fused_computation.4 | convolution fusion | flops 269484032 | bytes 7340096 | tf_op jit(solution)/shard_map/rkij,rkjh->rih/dot_general | solution.py:130
  115.2 17.1 %shard_map.97 = f32[4,512,128]{2,1,0:T(8,128)} custom-call(f32[4,512,128]{2,1,0:T(8,128)} %bitcast.74), custom_call_target="tpu_custom_call" | custom-call | tf_op jit(solution)/shard_map/pallas_call | solution.py:82
  132.4 1.3 reduce_sum.18
  133.7 0.3 convolution_add_fusion
  134.0 1.5 fusion.12
  135.4 0.7 fusion.28
  136.1 18.0 %shard_map.98 = (bf16[8,256,128]{2,1,0:T(8,128)(2,1)}, bf16[8,256,128]{2,1,0:T(8,128)(2,1)}) custom-call(bf16[256,128]{1,0:T(8,128)(2,1)} %get-tuple-element.11.refs_0_, bf16[256,128]{1,0:T(8,128)(2,1)} %get-tuple-element.10.refs_1_), custom_call_target="tpu_custom_call" | custom-call | tf_op jit(solution)/shard_map/pallas_call | solution.py:82
  154.1 75.5 %shard_map.99 = bf16[8,8,256,128]{3,2,1,0:T(8,128)(2,1)} custom-call(bf16[8,256,128]{2,1,0:T(8,128)(2,1)} %get-tuple-element.9.refs_0_), custom_call_target="tpu_custom_call" | custom-call | tf_op jit(solution)/shard_map/pallas_call | solution.py:82
  229.7 4.4 %gather_fusion.3 = bf16[64,128,128]{2,1,0:T(8,128)(2,1)} fusion(bf16[128,128,128]{2,1,0:T(8,128)(2,1)} %bitcast.68, s32[1024]{0:T(1024)S(1)} %pad_clamp_fusion), kind=kCustom, calls=%fused_computation.3 | custom fusion | bytes 4194560 | tf_op jit(solution)/shard_map/gather | solution.py:129
  234.1 1.1 fusion.13
  235.2 4.3 %gather_fusion.2 = bf16[64,128,128]{2,1,0:T(8,128)(2,1)} fusion(bf16[128,128,128]{2,1,0:T(8,128)(2,1)} %bitcast.76, s32[1024]{0:T(1024)S(1)} %pad_clamp_fusion.1), kind=kCustom, calls=%fused_computation.2 | custom fusion | bytes 4194560 | tf_op jit(solution)/shard_map/gather | solution.py:129
  239.5 4.0 %fusion.2 = f32[16,128,128,1]{1,2,3,0:T(8,128)} fusion(bf16[16,1,4,128,128]{4,3,2,1,0:T(8,128)(2,1)S(1)} %copy-done, bf16[16,4,128,128]{3,2,1,0:T(8,128)(2,1)} %bitcast.71, bf16[16,4,128,128]{3,2,1,0:T(8,128)(2,1)} %bitcast.69, pred[16,4]{1,0:T(8,128)(4,1)S(1)} %copy.16), kind=kOutput, calls=%fused_computation.6 | convolution fusion | flops 269484032 | bytes 7340096 | tf_op jit(solution)/shard_map/rkij,rkjh->rih/dot_general | solution.py:130
  243.6 16.7 %shard_map.100 = f32[4,512,128]{2,1,0:T(8,128)} custom-call(f32[4,512,128]{2,1,0:T(8,128)} %bitcast.73), custom_call_target="tpu_custom_call" | custom-call | tf_op jit(solution)/shard_map/pallas_call | solution.py:82
  260.3 1.3 reduce_sum.19
  261.6 0.7 add_convert_fusion
  (25 shorter events, 0.4 us)
Async XLA Ops:
  7.2 104.0 %copy-start = (bf16[16,1,4,128,128]{4,3,2,1,0:T(8,128)(2,1)S(1)}, bf16[16,1,4,128,128]{4,3,2,1,0:T(8,128)(2,1)}, u32[]{:S(2)}) copy-start(bf16[16,1,4,128,128]{4,3,2,1,0:T(8,128)(2,1)} %param.9) | copy-start | bytes 6291460
  7.2 99.7 %all-gather.5.cloned.1.call-start = ((), (), s32[]{:S(2)}) async-start(), calls=%async_computation | async-start | bytes 4718592 | tf_op jit(solution)/shard_map/all_gather | solution.py:100
  29.2 206.0 %all-gather.7.cloned.1.call-start = ((), (), s32[]{:S(2)}) async-start(), calls=%async_computation.1 | async-start | bytes 4718592 | tf_op jit(solution)/shard_map/all_gather | solution.py:100
  115.2 18.4 %copy-start.1 = (bf16[128,512]{1,0:T(8,128)(2,1)S(1)}, bf16[128,512]{1,0:T(8,128)(2,1)}, u32[]{:S(2)}) copy-start(bf16[128,512]{1,0:T(8,128)(2,1)} %param.11) | copy-start | bytes 393220
  115.2 18.4 %copy-start.4 = (f32[512]{0:T(512)S(1)}, f32[512]{0:T(512)}, u32[]{:S(2)}) copy-start(f32[512]{0:T(512)} %param.12) | copy-start | bytes 6148
  115.2 18.7 %copy-start.3 = (bf16[512,128]{1,0:T(8,128)(2,1)S(1)}, bf16[512,128]{1,0:T(8,128)(2,1)}, u32[]{:S(2)}) copy-start(bf16[512,128]{1,0:T(8,128)(2,1)} %param.15) | copy-start | bytes 393220
  229.7 4.5 %copy-start.2 = (bf16[512,128]{1,0:T(8,128)(2,1)S(1)}, bf16[512,128]{1,0:T(8,128)(2,1)}, u32[]{:S(2)}) copy-start(bf16[512,128]{1,0:T(8,128)(2,1)} %param.8) | copy-start | bytes 393220
  229.7 4.4 %copy-start.5 = (bf16[512,128]{1,0:T(8,128)(2,1)S(1)}, bf16[512,128]{1,0:T(8,128)(2,1)}, u32[]{:S(2)}) copy-start(bf16[512,128]{1,0:T(8,128)(2,1)} %param.13) | copy-start | bytes 393220
  229.7 4.4 %copy-start.6 = (f32[128]{0:T(128)S(1)}, f32[128]{0:T(128)}, u32[]{:S(2)}) copy-start(f32[128]{0:T(128)} %param.14) | copy-start | bytes 1540
Sparse Core Ops, SparseCore 0:
  29.3 54.7 all-gather.4
  154.2 52.7 all-gather.6

commit v5 on v4

--- a/solution.py
+++ b/solution.py
@@ -93,14 +93,87 @@
     )(*srcs)
 
 
-def gather_blk(rows, cid):
+def push_products_kernel(axes, flag_ref, first_ref, hi_ref, lo_ref, src_ref, panel_ref, adj_ref,
+                         out_ref, landed, send_sem, recv_sem, local_sem):
+    me, sizes = group_place(axes)
+    n = landed.shape[0]
+    rows, kq = adj_ref.shape[0], adj_ref.shape[1]
+    barrier = pltpu.get_barrier_semaphore()
+    for d in range(1, n):
+        p = lax.rem(me + d, n)
+        pl.semaphore_signal(barrier, 1, device_id=peer_id(axes, sizes, p))
+    pl.semaphore_wait(barrier, n - 1)
+    copies = []
+    for d in range(1, n):
+        p = lax.rem(me + d, n)
+        copy = pltpu.make_async_remote_copy(
+            src_ref=src_ref,
+            dst_ref=landed.at[me],
+            send_sem=send_sem.at[d],
+            recv_sem=recv_sem.at[d],
+            device_id=peer_id(axes, sizes, p),
+        )
+        copy.start()
+        copies.append(copy)
+    own = pltpu.make_async_copy(src_ref, landed.at[me], local_sem)
+    own.start()
+
+    def first_half(g, carry):
+        acc = jnp.zeros(out_ref.shape[1:], jnp.float32)
+        for k in range(kq):
+            block = panel_ref[first_ref[g, k]]
+            block = jnp.where(flag_ref[g, k] != 0, block, jnp.zeros_like(block))
+            acc = acc + jnp.dot(adj_ref[g, k], block, preferred_element_type=jnp.float32)
+        out_ref[g] = acc
+        return carry
+
+    def second_half(g, carry):
+        acc = out_ref[g]
+        for k in range(kq):
+            block = landed[hi_ref[g, k], lo_ref[g, k]]
+            block = jnp.where(flag_ref[g, k] != 0, jnp.zeros_like(block), block)
+            acc = acc + jnp.dot(adj_ref[g, k], block, preferred_element_type=jnp.float32)
+        out_ref[g] = acc
+        return carry
+
+    lax.fori_loop(0, rows, first_half, 0)
+    for copy in copies:
+        copy.wait()
+    own.wait()
+    lax.fori_loop(0, rows, second_half, 0)
+
+
+def push_products(index, src, panel, adj, axes, cid):
+    n = 1
+    for a in axes:
+        n *= lax.axis_size(a)
+    rows = adj.shape[0]
+    smem = pl.BlockSpec(memory_space=pltpu.SMEM)
+    vmem = pl.BlockSpec(memory_space=pltpu.VMEM)
+    return pl.pallas_call(
+        functools.partial(push_products_kernel, axes),
+        out_shape=jax.ShapeDtypeStruct((rows, BLOCK, panel.shape[2]), jnp.float32),
+        in_specs=[smem] * 4 + [pl.BlockSpec(memory_space=pl.ANY), vmem, vmem],
+        out_specs=vmem,
+        scratch_shapes=[
+            pltpu.VMEM((n, *src.shape), src.dtype),
+            pltpu.SemaphoreType.DMA((n,)),
+            pltpu.SemaphoreType.DMA((n,)),
+            pltpu.SemaphoreType.DMA,
+        ],
+        compiler_params=pltpu.CompilerParams(collective_id=cid, has_side_effects=True),
+    )(*index, src, panel, adj)
+
+
+def aggregate(rows, adj, index, cid):
     half = rows.shape[0] // 2
+    width = rows.shape[1]
     xy = (("x", "ylo"), True)
     first, second = group_exchange((rows[:half], rows[half:]), (xy, (("z",), True)), cid)
-    first = lax.all_gather(first, "z", axis=0, tiled=False)
-    (second,) = group_exchange((second,), (xy,), cid + 4)
-    width = rows.shape[1]
-    return first.reshape(-1, BLOCK, width), second.reshape(-1, BLOCK, width)
+    first = lax.all_gather(first, "z", axis=0, tiled=False).reshape(-1, BLOCK, width)
+    second = second.reshape(-1, BLOCK, width)
+    summed = push_products(index, second, first, adj, ("x", "ylo"), cid + 4)
+    return summed.reshape(-1, width)
 
 
 def reduce_rep(partial, cid):
@@ -120,24 +193,15 @@
     xy = owner // nz
     in_first = sub < half
     first = (z * nxy + xy) * half + jnp.where(in_first, sub, 0)
-    second = (xy * nz + z) * half + jnp.where(in_first, 0, sub - half)
-    return in_first, first, second
-
-
-def tile_products(panels, adj_tiles, index):
-    in_first, first, second = index
-    picked = jnp.where(in_first[..., None, None], panels[0][first], panels[1][second])
-    summed = jnp.einsum(
-        "rkij,rkjh->rih", adj_tiles[:, 0], picked, preferred_element_type=jnp.float32
-    )
-    return summed.reshape(-1, panels[0].shape[2])
+    lo = z * half + jnp.where(in_first, 0, sub - half)
+    return in_first.astype(jnp.int32), first, xy, lo
 
 
 def local(node_feats, adj_tiles, col_index, w_in, b_in, w_out, b_out, cot_out):
     per_owner = node_feats.shape[0] // BLOCK
     index = staged_index(col_index[:, 0, :], per_owner)
-    panels = gather_blk(node_feats, 0)
-    partial_sum = tile_products(panels, adj_tiles, index)
+    adj = adj_tiles[:, 0]
+    partial_sum = aggregate(node_feats, adj, index, 0)
     agg = reduce_rep(partial_sum, 8)
     agg_b = agg.astype(jnp.bfloat16)
     pre = jnp.dot(agg_b, w_in, preferred_element_type=jnp.float32) + b_in
@@ -150,8 +214,7 @@
     g_agg = jnp.einsum("nf,hf->nh", g_pre, w_in, preferred_element_type=jnp.float32).astype(
         jnp.bfloat16
     )
-    g_panels = gather_blk(g_agg, 1)
-    back_partial = tile_products(g_panels, adj_tiles, index)
+    back_partial = aggregate(g_agg, adj, index, 1)
     back_rows = reduce_rep(back_partial, 9)
     grad_feats = (cot_out.astype(jnp.float32) + back_rows).astype(jnp.bfloat16)
     return (out_feats, grad_feats)

time: 270 us -> 359 us (1.33)
  waiting for transfers between devices: 0.04 us -> 105 us
  local copies, waits for them, and re-layouts: 20.3 us -> 3.03 us
  Pallas kernels: 219 us -> 229 us
  matrix products: 10.9 us -> 1.94 us
    pallas_call x0 -> x2, Pallas kernels: none -> 158 us  [push_products(): pl.pallas_call(functools.partial(push_products_kernel, axes), out_shape=j...]
    pallas_call x6 -> x4, Pallas kernels: 219 us -> 70.9 us  [group_exchange(): pl.pallas_call(functools.partial(exchange_kernel, tuple(jobs)), out_shape...]
    all_gather x2, waiting for transfers between devices: 0.01 us -> 105 us  [aggregate(): lax.all_gather(first, 'z', axis=0, tiled=False).reshape(-1, BLOCK, width)]
    gather x4 -> x0, local copies, waits for them, and re-layouts: 17.4 us -> none  [the longest x2 8.79 us: tile_products(): panels[1][second]]
    dot_general x2 -> x0, matrix products: 8.06 us -> none  [tile_products(): jnp.einsum('rkij,rkjh->rih', adj_tiles[:, 0], picked, preferred_element_t...]
  transfers between devices with their start and end apart: 2 -> 2, of which waited for: 0 -> 2; matrix products, arithmetic and copies ran while one was open for 4% -> 1% of each run, Pallas kernels for 55% -> 0%
where the time goes in v5:
time: 359 us; the launch traced here: 358 us
  Pallas kernels  229 us (64%)
  waiting for transfers between devices  105 us (29%)
  between operations  14.2 us (4%)
  other arithmetic  4.51 us (1%)
    pallas_call x2, Pallas kernels, push_products(): pl.pallas_call(functools.partial(push_products_kernel, axes), out_shape=j...  158 us
    all_gather x2, waiting for transfers between devices, aggregate(): lax.all_gather(first, 'z', axis=0, tiled=False).reshape(-1, BLOCK, width)  105 us
    pallas_call x4, Pallas kernels, group_exchange(): pl.pallas_call(functools.partial(exchange_kernel, tuple(jobs)), out_shape...  70.9 us
  transfers between devices with their start and end apart: 2, of which 2 were waited for; matrix products, arithmetic and copies ran while one was open for 1% of the time, Pallas kernels for 0%

profile of v5, /device:TPU:9, one launch (start us, length us, event | category | flops | bytes accessed | tf_op | source)
XLA Modules:
  0.0 358.0 jit_solution(12748717701441550500)
XLA Ops:
  7.2 0.0 copy-start
  7.2 0.0 all-gather.5.cloned.1.call-start
  7.2 1.6 fusion.19
  8.8 20.3 %shard_map.95 = (bf16[8,256,128]{2,1,0:T(8,128)(2,1)}, bf16[8,256,128]{2,1,0:T(8,128)(2,1)}) custom-call(bf16[256,128]{1,0:T(8,128)(2,1)} %get-tuple-element.13.refs_0_, bf16[256,128]{1,0:T(8,128)(2,1)} %get-tuple-element.12.refs_1_), custom_call_target="tpu_custom_call" | custom-call | tf_op jit(solution)/shard_map/pallas_call | solution.py:82
  29.1 0.0 all-gather.5.cloned.1.call-update
  29.1 0.0 all-gather.7.cloned.1.call-start
  29.1 0.8 copy.14
  29.9 0.6 fusion.15.flag_ref
  30.5 0.6 select_add_fusion
  31.1 52.9 %all-gather.5.cloned.1.call-done = bf16[64,256,128]{2,1,0:T(8,128)(2,1)} async-done(((bf16[8,256,128]{2,1,0:T(8,128)(2,1)}), bf16[64,256,128]{2,1,0:T(8,128)(2,1)}) %all-gather.5.cloned.1.call-update) | async-done | bytes 4194320 | tf_op jit(solution)/shard_map/all_gather | solution.py:173
  84.0 79.2 %shard_map.96 = f32[16,128,128]{2,1,0:T(8,128)} custom-call(s32[16,4]{1,0:T(8,128)} %fusion.15.flag_ref, s32[16,4]{1,0:T(8,128)} %get-tuple-element.15.first_ref, s32[16,4]{1,0:T(8,128)} %get-tuple-element.16.hi_ref, s32[16,4]{1,0:T(8,128)} %get-tuple-element.14.lo_ref, bf16[16,128,128]{2,1,0:T(8,128)(2,1)} %bitcast.20, bf16[128,128,128]{2,1,0:T(8,128)(2,1)} %bitcast.18, ...), custom_call_target="tpu_custom_call" | custom-call | tf_op jit(solution)/shard_map/pallas_call | solution.py:153
  163.2 17.1 %shard_map.97 = f32[4,512,128]{2,1,0:T(8,128)} custom-call(f32[4,512,128]{2,1,0:T(8,128)} %bitcast.17), custom_call_target="tpu_custom_call" | custom-call | tf_op jit(solution)/shard_map/pallas_call | solution.py:82
  180.3 1.3 reduce_sum.18
  181.7 0.3 convolution_add_fusion
  182.0 0.6 fusion.4
  182.5 0.7 fusion.18
  183.2 16.4 %shard_map.98 = (bf16[8,256,128]{2,1,0:T(8,128)(2,1)}, bf16[8,256,128]{2,1,0:T(8,128)(2,1)}) custom-call(bf16[256,128]{1,0:T(8,128)(2,1)} %get-tuple-element.11.refs_0_, bf16[256,128]{1,0:T(8,128)(2,1)} %get-tuple-element.10.refs_1_), custom_call_target="tpu_custom_call" | custom-call | tf_op jit(solution)/shard_map/pallas_call | solution.py:82
  199.7 0.0 all-gather.7.cloned.1.call-update
  199.7 1.1 fusion.5
  200.8 52.1 %all-gather.7.cloned.1.call-done = bf16[64,256,128]{2,1,0:T(8,128)(2,1)} async-done(((bf16[8,256,128]{2,1,0:T(8,128)(2,1)}), bf16[64,256,128]{2,1,0:T(8,128)(2,1)}) %all-gather.7.cloned.1.call-update) | async-done | bytes 4194320 | tf_op jit(solution)/shard_map/all_gather | solution.py:173
  252.9 79.2 %shard_map.99 = f32[16,128,128]{2,1,0:T(8,128)} custom-call(s32[16,4]{1,0:T(8,128)} %fusion.15.flag_ref, s32[16,4]{1,0:T(8,128)} %get-tuple-element.15.first_ref, s32[16,4]{1,0:T(8,128)} %get-tuple-element.16.hi_ref, s32[16,4]{1,0:T(8,128)} %get-tuple-element.14.lo_ref, bf16[16,128,128]{2,1,0:T(8,128)(2,1)} %bitcast.21, bf16[128,128,128]{2,1,0:T(8,128)(2,1)} %bitcast.19, ...), custom_call_target="tpu_custom_call" | custom-call | tf_op jit(solution)/shard_map/pallas_call | solution.py:153
  332.1 17.1 %shard_map.100 = f32[4,512,128]{2,1,0:T(8,128)} custom-call(f32[4,512,128]{2,1,0:T(8,128)} %bitcast.16), custom_call_target="tpu_custom_call" | custom-call | tf_op jit(solution)/shard_map/pallas_call | solution.py:82
  349.2 1.3 reduce_sum.19
  350.5 0.7 add_convert_fusion
  (11 shorter events, 0.0 us)
Async XLA Ops:
  7.2 174.5 %copy-start = (bf16[128,512]{1,0:T(8,128)(2,1)S(1)}, bf16[128,512]{1,0:T(8,128)(2,1)}, u32[]{:S(2)}) copy-start(bf16[128,512]{1,0:T(8,128)(2,1)} %param.11) | copy-start | bytes 393220
  7.2 76.8 %all-gather.5.cloned.1.call-start = ((), (), s32[]{:S(2)}) async-start(), calls=%async_computation | async-start | bytes 4718592 | tf_op jit(solution)/shard_map/all_gather | solution.py:173
  29.1 223.8 %all-gather.7.cloned.1.call-start = ((), (), s32[]{:S(2)}) async-start(), calls=%async_computation.1 | async-start | bytes 4718592 | tf_op jit(solution)/shard_map/all_gather | solution.py:173
  84.0 97.6 %copy-start.3 = (f32[512]{0:T(512)S(1)}, f32[512]{0:T(512)}, u32[]{:S(2)}) copy-start(f32[512]{0:T(512)} %param.12) | copy-start | bytes 6148
  163.2 18.8 %copy-start.2 = (bf16[512,128]{1,0:T(8,128)(2,1)S(1)}, bf16[512,128]{1,0:T(8,128)(2,1)}, u32[]{:S(2)}) copy-start(bf16[512,128]{1,0:T(8,128)(2,1)} %param.15) | copy-start | bytes 393220
  163.2 18.8 %copy-start.4 = (bf16[512,128]{1,0:T(8,128)(2,1)S(1)}, bf16[512,128]{1,0:T(8,128)(2,1)}, u32[]{:S(2)}) copy-start(bf16[512,128]{1,0:T(8,128)(2,1)} %param.13) | copy-start | bytes 393220
  181.6 18.0 %copy-start.1 = (bf16[512,128]{1,0:T(8,128)(2,1)S(1)}, bf16[512,128]{1,0:T(8,128)(2,1)}, u32[]{:S(2)}) copy-start(bf16[512,128]{1,0:T(8,128)(2,1)} %param.8) | copy-start | bytes 393220
  181.7 18.0 %copy-start.5 = (f32[128]{0:T(128)S(1)}, f32[128]{0:T(128)}, u32[]{:S(2)}) copy-start(f32[128]{0:T(128)} %param.14) | copy-start | bytes 1540
Sparse Core Ops, SparseCore 0:
  29.2 54.7 all-gather.4
  199.8 53.0 all-gather.6

commit v6 on v4

--- a/solution.py
+++ b/solution.py
@@ -121,16 +121,44 @@
     in_first = sub < half
     first = (z * nxy + xy) * half + jnp.where(in_first, sub, 0)
     second = (xy * nz + z) * half + jnp.where(in_first, 0, sub - half)
-    return in_first, first, second
+    return in_first.astype(jnp.int32), first, second
+
+
+def products_kernel(flag_ref, first_ref, second_ref, *refs):
+    kq = len(refs) // 2 - 1
+    firsts, seconds = refs[:kq], refs[kq : 2 * kq]
+    adj_ref, out_ref = refs[2 * kq :]
+    g = pl.program_id(0)
+    acc = jnp.zeros(out_ref.shape[1:], jnp.float32)
+    for k in range(kq):
+        block = jnp.where(flag_ref[g, k] != 0, firsts[k][0], seconds[k][0])
+        acc = acc + jnp.dot(adj_ref[0, k], block, preferred_element_type=jnp.float32)
+    out_ref[0] = acc
 
 
 def tile_products(panels, adj_tiles, index):
-    in_first, first, second = index
-    picked = jnp.where(in_first[..., None, None], panels[0][first], panels[1][second])
-    summed = jnp.einsum(
-        "rkij,rkjh->rih", adj_tiles[:, 0], picked, preferred_element_type=jnp.float32
-    )
-    return summed.reshape(-1, panels[0].shape[2])
+    flag, first, second = index
+    rows, kq = flag.shape
+    width = panels[0].shape[2]
+    tile = (1, BLOCK, width)
+
+    def pick(table, k):
+        return pl.BlockSpec(tile, lambda g, f, a, b: (table(f, a, b)[g, k], 0, 0))
+
+    specs = [pick(lambda f, a, b: a, k) for k in range(kq)]
+    specs += [pick(lambda f, a, b: b, k) for k in range(kq)]
+    specs.append(pl.BlockSpec((1, kq, BLOCK, BLOCK), lambda g, f, a, b: (g, 0, 0, 0)))
+    summed = pl.pallas_call(
+        products_kernel,
+        out_shape=jax.ShapeDtypeStruct((rows, BLOCK, width), jnp.float32),
+        grid_spec=pltpu.PrefetchScalarGridSpec(
+            num_scalar_prefetch=3,
+            grid=(rows,),
+            in_specs=specs,
+            out_specs=pl.BlockSpec(tile, lambda g, f, a, b: (g, 0, 0)),
+        ),
+    )(flag, first, second, *([panels[0]] * kq), *([panels[1]] * kq), adj_tiles[:, 0])
+    return summed.reshape(-1, width)
 
 
 def local(node_feats, adj_tiles, col_index, w_in, b_in, w_out, b_out, cot_out):

time: 270 us -> 270 us (level)
  Pallas kernels: 219 us -> 244 us
  local copies, waits for them, and re-layouts: 20.3 us -> 3.02 us
  matrix products: 10.9 us -> 1.93 us
    pallas_call x0 -> x2, Pallas kernels: none -> 25.6 us  [tile_products(): pl.pallas_call(products_kernel, out_shape=jax.ShapeDtypeStruct((rows, BLO...]
    gather x4 -> x0, local copies, waits for them, and re-layouts: 17.4 us -> none  [the longest x2 8.79 us: tile_products(): panels[1][second]]
    dot_general x2 -> x0, matrix products: 8.06 us -> none  [tile_products(): jnp.einsum('rkij,rkjh->rih', adj_tiles[:, 0], picked, preferred_element_t...]
  transfers between devices with their start and end apart: 2 -> 2, of which waited for: 0 -> 0; matrix products, arithmetic and copies ran while one was open for 4% -> 1% of each run, Pallas kernels for 55% -> 55%
where the time goes in v6:
time: 270 us; the launch traced here: 268 us
  Pallas kernels  244 us (90%)
  between operations  14.2 us (5%)
  other arithmetic  4.52 us (2%)
  local copies, waits for them, and re-layouts  3.02 us (1%)
    pallas_call x6, Pallas kernels, group_exchange(): pl.pallas_call(functools.partial(exchange_kernel, tuple(jobs)), out_shape...  219 us
    pallas_call x2, Pallas kernels, tile_products(): pl.pallas_call(products_kernel, out_shape=jax.ShapeDtypeStruct((rows, BLO...  25.6 us
  transfers between devices with their start and end apart: 2, of which 0 were waited for; matrix products, arithmetic and copies ran while one was open for 1% of the time, Pallas kernels for 55%

profile of v6, /device:TPU:9, one launch (start us, length us, event | category | flops | bytes accessed | tf_op | source)
XLA Modules:
  0.0 268.2 jit_solution(6932956379414800226)
XLA Ops:
  7.2 0.0 copy-start
  7.2 0.0 all-gather.5.cloned.1.call-start
  7.2 1.6 fusion.19
  8.8 20.3 %shard_map.95 = (bf16[8,256,128]{2,1,0:T(8,128)(2,1)}, bf16[8,256,128]{2,1,0:T(8,128)(2,1)}) custom-call(bf16[256,128]{1,0:T(8,128)(2,1)} %get-tuple-element.13.refs_0_, bf16[256,128]{1,0:T(8,128)(2,1)} %get-tuple-element.12.refs_1_), custom_call_target="tpu_custom_call" | custom-call | tf_op jit(solution)/shard_map/pallas_call | solution.py:82
  29.1 0.0 all-gather.5.cloned.1.call-update
  29.1 0.0 all-gather.7.cloned.1.call-start
  29.1 0.8 copy.14
  29.9 71.1 %shard_map.96 = bf16[8,8,256,128]{3,2,1,0:T(8,128)(2,1)} custom-call(bf16[8,256,128]{2,1,0:T(8,128)(2,1)} %get-tuple-element.7.refs_0_), custom_call_target="tpu_custom_call" | custom-call | tf_op jit(solution)/shard_map/pallas_call | solution.py:82
  101.1 0.6 fusion.15.flag_ref
  101.7 0.6 select_add_fusion
  102.3 12.9 %shard_map.97 = f32[16,128,128]{2,1,0:T(8,128)} custom-call(s32[16,4]{1,0:T(8,128)} %fusion.15.flag_ref, s32[16,4]{1,0:T(8,128)} %get-tuple-element.15.first_ref, s32[16,4]{1,0:T(8,128)} %get-tuple-element.14.second_ref, bf16[128,128,128]{2,1,0:T(8,128)(2,1)} %bitcast.22, bf16[128,128,128]{2,1,0:T(8,128)(2,1)} %bitcast.23, bf16[128,128,128]{2,1,0:T(8,128)(2,1)} %bitcast.24, ...), custom_call_target="tpu_custom_call" | custom-call | tf_op jit(solution)/shard_map/pallas_call | solution.py:151
  115.2 17.3 %shard_map.98 = f32[4,512,128]{2,1,0:T(8,128)} custom-call(f32[4,512,128]{2,1,0:T(8,128)} %bitcast.33), custom_call_target="tpu_custom_call" | custom-call | tf_op jit(solution)/shard_map/pallas_call | solution.py:82
  132.4 1.3 reduce_sum.18
  133.7 0.3 convolution_add_fusion
  134.1 0.6 fusion.4
  134.6 0.7 fusion.18
  135.3 18.0 %shard_map.99 = (bf16[8,256,128]{2,1,0:T(8,128)(2,1)}, bf16[8,256,128]{2,1,0:T(8,128)(2,1)}) custom-call(bf16[256,128]{1,0:T(8,128)(2,1)} %get-tuple-element.11.refs_0_, bf16[256,128]{1,0:T(8,128)(2,1)} %get-tuple-element.10.refs_1_), custom_call_target="tpu_custom_call" | custom-call | tf_op jit(solution)/shard_map/pallas_call | solution.py:82
  153.3 0.0 all-gather.7.cloned.1.call-update
  153.3 75.5 %shard_map.100 = bf16[8,8,256,128]{3,2,1,0:T(8,128)(2,1)} custom-call(bf16[8,256,128]{2,1,0:T(8,128)(2,1)} %get-tuple-element.9.refs_0_), custom_call_target="tpu_custom_call" | custom-call | tf_op jit(solution)/shard_map/pallas_call | solution.py:82
  228.9 1.1 fusion.5
  230.0 12.7 %shard_map.101 = f32[16,128,128]{2,1,0:T(8,128)} custom-call(s32[16,4]{1,0:T(8,128)} %fusion.15.flag_ref, s32[16,4]{1,0:T(8,128)} %get-tuple-element.15.first_ref, s32[16,4]{1,0:T(8,128)} %get-tuple-element.14.second_ref, bf16[128,128,128]{2,1,0:T(8,128)(2,1)} %bitcast.26, bf16[128,128,128]{2,1,0:T(8,128)(2,1)} %bitcast.27, bf16[128,128,128]{2,1,0:T(8,128)(2,1)} %bitcast.28, ...), custom_call_target="tpu_custom_call" | custom-call | tf_op jit(solution)/shard_map/pallas_call | solution.py:151
  242.7 16.7 %shard_map.102 = f32[4,512,128]{2,1,0:T(8,128)} custom-call(f32[4,512,128]{2,1,0:T(8,128)} %bitcast.32), custom_call_target="tpu_custom_call" | custom-call | tf_op jit(solution)/shard_map/pallas_call | solution.py:82
  259.4 1.3 reduce_sum.19
  260.7 0.7 add_convert_fusion
  (13 shorter events, 0.0 us)
Async XLA Ops:
  7.2 126.6 %copy-start = (bf16[128,512]{1,0:T(8,128)(2,1)S(1)}, bf16[128,512]{1,0:T(8,128)(2,1)}, u32[]{:S(2)}) copy-start(bf16[128,512]{1,0:T(8,128)(2,1)} %param.11) | copy-start | bytes 393220
  7.2 95.1 %all-gather.5.cloned.1.call-start = ((), (), s32[]{:S(2)}) async-start(), calls=%async_computation | async-start | bytes 4718592 | tf_op jit(solution)/shard_map/all_gather | solution.py:100
  29.1 200.9 %all-gather.7.cloned.1.call-start = ((), (), s32[]{:S(2)}) async-start(), calls=%async_computation.1 | async-start | bytes 4718592 | tf_op jit(solution)/shard_map/all_gather | solution.py:100
  102.3 31.4 %copy-start.3 = (f32[512]{0:T(512)S(1)}, f32[512]{0:T(512)}, u32[]{:S(2)}) copy-start(f32[512]{0:T(512)} %param.12) | copy-start | bytes 6148
  115.2 18.9 %copy-start.2 = (bf16[512,128]{1,0:T(8,128)(2,1)S(1)}, bf16[512,128]{1,0:T(8,128)(2,1)}, u32[]{:S(2)}) copy-start(bf16[512,128]{1,0:T(8,128)(2,1)} %param.15) | copy-start | bytes 393220
  115.2 18.9 %copy-start.4 = (bf16[512,128]{1,0:T(8,128)(2,1)S(1)}, bf16[512,128]{1,0:T(8,128)(2,1)}, u32[]{:S(2)}) copy-start(bf16[512,128]{1,0:T(8,128)(2,1)} %param.13) | copy-start | bytes 393220
  134.6 94.2 %copy-start.1 = (bf16[512,128]{1,0:T(8,128)(2,1)S(1)}, bf16[512,128]{1,0:T(8,128)(2,1)}, u32[]{:S(2)}) copy-start(bf16[512,128]{1,0:T(8,128)(2,1)} %param.8) | copy-start | bytes 393220
  134.6 94.2 %copy-start.5 = (f32[128]{0:T(128)S(1)}, f32[128]{0:T(128)}, u32[]{:S(2)}) copy-start(f32[128]{0:T(128)} %param.14) | copy-start | bytes 1540
Sparse Core Ops, SparseCore 0:
  29.2 54.7 all-gather.4
  153.4 52.6 all-gather.6

commit v7 on v6

--- a/solution.py
+++ b/solution.py
@@ -93,12 +93,72 @@
     )(*srcs)
 
 
+def tree_kernel(src_ref, out_ref, send_sem, recv_sem, local_sem):
+    nx, ny = lax.axis_size("x"), lax.axis_size("ylo")
+    x, y = lax.axis_index("x"), lax.axis_index("ylo")
+    right, left, other = lax.rem(x + 1, nx), lax.rem(x + nx - 1, nx), ny - 1 - y
+    to_right, to_left, to_other = {"x": right}, {"x": left}, {"ylo": other}
+    barrier = pltpu.get_barrier_semaphore()
+    for peer in (to_right, to_left, to_other):
+        pl.semaphore_signal(barrier, 1, device_id=peer)
+    pl.semaphore_wait(barrier, 3)
+
+    def send(kind, src, slot, peer):
+        copy = pltpu.make_async_remote_copy(
+            src_ref=src,
+            dst_ref=out_ref.at[slot],
+            send_sem=send_sem.at[kind],
+            recv_sem=recv_sem.at[kind],
+            device_id=peer,
+        )
+        copy.start()
+        return copy
+
+    me = x * ny + y
+    own = pltpu.make_async_copy(src_ref, out_ref.at[me], local_sem)
+    own.start()
+    first_right = send(0, src_ref, me, to_right)
+    first_left = send(1, src_ref, me, to_left)
+    first_other = send(2, src_ref, me, to_other)
+    first_right.wait_recv()
+    from_left = left * ny + y
+    second_right = send(3, out_ref.at[from_left], from_left, to_right)
+    first_other.wait_recv()
+    from_other = x * ny + other
+    other_right = send(4, out_ref.at[from_other], from_other, to_right)
+    other_left = send(5, out_ref.at[from_other], from_other, to_left)
+    other_right.wait_recv()
+    from_left_other = left * ny + other
+    third_right = send(6, out_ref.at[from_left_other], from_left_other, to_right)
+    for copy in (first_left, second_right, other_left, third_right):
+        copy.wait_recv()
+    for copy in (first_right, first_left, first_other, second_right, other_right, other_left, third_right):
+        copy.wait_send()
+    own.wait()
+
+
+def tree_gather(src, cid):
+    n = lax.axis_size("x") * lax.axis_size("ylo")
+    return pl.pallas_call(
+        tree_kernel,
+        out_shape=jax.ShapeDtypeStruct((n, *src.shape), src.dtype),
+        in_specs=[pl.BlockSpec(memory_space=pl.ANY)],
+        out_specs=pl.BlockSpec(memory_space=pl.ANY),
+        scratch_shapes=[
+            pltpu.SemaphoreType.DMA((7,)),
+            pltpu.SemaphoreType.DMA((7,)),
+            pltpu.SemaphoreType.DMA,
+        ],
+        compiler_params=pltpu.CompilerParams(collective_id=cid, has_side_effects=True),
+    )(src)
+
+
 def gather_blk(rows, cid):
     half = rows.shape[0] // 2
     xy = (("x", "ylo"), True)
     first, second = group_exchange((rows[:half], rows[half:]), (xy, (("z",), True)), cid)
     first = lax.all_gather(first, "z", axis=0, tiled=False)
-    (second,) = group_exchange((second,), (xy,), cid + 4)
+    second = tree_gather(second, cid + 4)
     width = rows.shape[1]
     return first.reshape(-1, BLOCK, width), second.reshape(-1, BLOCK, width)
 

time: 270 us -> 226 us (0.84)
  Pallas kernels: 244 us -> 194 us
  waiting for transfers between devices: 0.04 us -> 6.1 us
    pallas_call x6 -> x4, Pallas kernels: 219 us -> 69.9 us  [group_exchange(): pl.pallas_call(functools.partial(exchange_kernel, tuple(jobs)), out_shape...]
    pallas_call x0 -> x2, Pallas kernels: none -> 98.1 us  [tree_gather(): pl.pallas_call(tree_kernel, out_shape=jax.ShapeDtypeStruct((n, *src.shape...]
    all_gather x2, waiting for transfers between devices: 0.01 us -> 6.07 us  [gather_blk(): first = lax.all_gather(first, 'z', axis=0, tiled=False)]
  transfers between devices with their start and end apart: 2 -> 2, of which waited for: 0 -> 2; matrix products, arithmetic and copies ran while one was open for 1% -> 1% of each run, Pallas kernels for 55% -> 44%
where the time goes in v7:
time: 226 us; the launch traced here: 223 us
  Pallas kernels  194 us (86%)
  between operations  14.2 us (6%)
  waiting for transfers between devices  6.1 us (3%)
  other arithmetic  4.52 us (2%)
  local copies, waits for them, and re-layouts  3.02 us (1%)
    pallas_call x2, Pallas kernels, tree_gather(): pl.pallas_call(tree_kernel, out_shape=jax.ShapeDtypeStruct((n, *src.shape...  98.1 us
    pallas_call x4, Pallas kernels, group_exchange(): pl.pallas_call(functools.partial(exchange_kernel, tuple(jobs)), out_shape...  69.9 us
    pallas_call x2, Pallas kernels, tile_products(): pl.pallas_call(products_kernel, out_shape=jax.ShapeDtypeStruct((rows, BLO...  25.6 us
    all_gather x2, waiting for transfers between devices, gather_blk(): first = lax.all_gather(first, 'z', axis=0, tiled=False)  6.07 us
  transfers between devices with their start and end apart: 2, of which 2 were waited for; matrix products, arithmetic and copies ran while one was open for 1% of the time, Pallas kernels for 44%

profile of v7, /device:TPU:9, one launch (start us, length us, event | category | flops | bytes accessed | tf_op | source)
XLA Modules:
  0.0 223.4 jit_solution(8602280827450083620)
XLA Ops:
  7.2 0.0 all-gather.5.cloned.1.call-start
  7.2 1.6 fusion.19
  8.8 20.3 %shard_map.95 = (bf16[8,256,128]{2,1,0:T(8,128)(2,1)}, bf16[8,256,128]{2,1,0:T(8,128)(2,1)}) custom-call(bf16[256,128]{1,0:T(8,128)(2,1)} %get-tuple-element.13.refs_0_, bf16[256,128]{1,0:T(8,128)(2,1)} %get-tuple-element.12.refs_1_), custom_call_target="tpu_custom_call" | custom-call | tf_op jit(solution)/shard_map/pallas_call | solution.py:82
  29.1 0.0 all-gather.5.cloned.1.call-update
  29.1 0.0 all-gather.7.cloned.1.call-start
  29.1 0.8 copy.14
  29.9 47.9 %shard_map.96 = bf16[8,8,256,128]{3,2,1,0:T(8,128)(2,1)} custom-call(bf16[8,256,128]{2,1,0:T(8,128)(2,1)} %get-tuple-element.7.src_ref), custom_call_target="tpu_custom_call" | custom-call | tf_op jit(solution)/shard_map/pallas_call | solution.py:142
  77.8 0.6 fusion.15.flag_ref
  78.4 0.6 select_add_fusion
  79.1 4.9 %all-gather.5.cloned.1.call-done = bf16[64,256,128]{2,1,0:T(8,128)(2,1)} async-done(((bf16[8,256,128]{2,1,0:T(8,128)(2,1)}), bf16[64,256,128]{2,1,0:T(8,128)(2,1)}) %all-gather.5.cloned.1.call-update) | async-done | bytes 4194320 | tf_op jit(solution)/shard_map/all_gather | solution.py:160
  84.0 12.9 %shard_map.97 = f32[16,128,128]{2,1,0:T(8,128)} custom-call(s32[16,4]{1,0:T(8,128)} %fusion.15.flag_ref, s32[16,4]{1,0:T(8,128)} %get-tuple-element.15.first_ref, s32[16,4]{1,0:T(8,128)} %get-tuple-element.14.second_ref, bf16[128,128,128]{2,1,0:T(8,128)(2,1)} %bitcast.22, bf16[128,128,128]{2,1,0:T(8,128)(2,1)} %bitcast.23, bf16[128,128,128]{2,1,0:T(8,128)(2,1)} %bitcast.24, ...), custom_call_target="tpu_custom_call" | custom-call | tf_op jit(solution)/shard_map/pallas_call | solution.py:211
  96.9 16.3 %shard_map.98 = f32[4,512,128]{2,1,0:T(8,128)} custom-call(f32[4,512,128]{2,1,0:T(8,128)} %bitcast.33), custom_call_target="tpu_custom_call" | custom-call | tf_op jit(solution)/shard_map/pallas_call | solution.py:82
  113.2 1.3 reduce_sum.18
  114.5 0.3 convolution_add_fusion
  114.8 0.6 fusion.4
  115.4 0.7 fusion.18
  116.1 16.3 %shard_map.99 = (bf16[8,256,128]{2,1,0:T(8,128)(2,1)}, bf16[8,256,128]{2,1,0:T(8,128)(2,1)}) custom-call(bf16[256,128]{1,0:T(8,128)(2,1)} %get-tuple-element.11.refs_0_, bf16[256,128]{1,0:T(8,128)(2,1)} %get-tuple-element.10.refs_1_), custom_call_target="tpu_custom_call" | custom-call | tf_op jit(solution)/shard_map/pallas_call | solution.py:82
  132.4 50.2 %shard_map.100 = bf16[8,8,256,128]{3,2,1,0:T(8,128)(2,1)} custom-call(bf16[8,256,128]{2,1,0:T(8,128)(2,1)} %get-tuple-element.9.src_ref), custom_call_target="tpu_custom_call" | custom-call | tf_op jit(solution)/shard_map/pallas_call | solution.py:142
  182.6 1.1 fusion.5
  183.7 1.1 all-gather.7.cloned.1.call-done
  184.8 12.7 %shard_map.101 = f32[16,128,128]{2,1,0:T(8,128)} custom-call(s32[16,4]{1,0:T(8,128)} %fusion.15.flag_ref, s32[16,4]{1,0:T(8,128)} %get-tuple-element.15.first_ref, s32[16,4]{1,0:T(8,128)} %get-tuple-element.14.second_ref, bf16[128,128,128]{2,1,0:T(8,128)(2,1)} %bitcast.26, bf16[128,128,128]{2,1,0:T(8,128)(2,1)} %bitcast.27, bf16[128,128,128]{2,1,0:T(8,128)(2,1)} %bitcast.28, ...), custom_call_target="tpu_custom_call" | custom-call | tf_op jit(solution)/shard_map/pallas_call | solution.py:211
  197.5 17.0 %shard_map.102 = f32[4,512,128]{2,1,0:T(8,128)} custom-call(f32[4,512,128]{2,1,0:T(8,128)} %bitcast.32), custom_call_target="tpu_custom_call" | custom-call | tf_op jit(solution)/shard_map/pallas_call | solution.py:82
  214.5 1.3 reduce_sum.19
  215.8 0.7 add_convert_fusion
  (13 shorter events, 0.1 us)
Async XLA Ops:
  7.2 107.3 %copy-start = (bf16[128,512]{1,0:T(8,128)(2,1)S(1)}, bf16[128,512]{1,0:T(8,128)(2,1)}, u32[]{:S(2)}) copy-start(bf16[128,512]{1,0:T(8,128)(2,1)} %param.11) | copy-start | bytes 393220
  7.2 76.8 %all-gather.5.cloned.1.call-start = ((), (), s32[]{:S(2)}) async-start(), calls=%async_computation | async-start | bytes 4718592 | tf_op jit(solution)/shard_map/all_gather | solution.py:160
  29.1 155.7 %all-gather.7.cloned.1.call-start = ((), (), s32[]{:S(2)}) async-start(), calls=%async_computation.1 | async-start | bytes 4718592 | tf_op jit(solution)/shard_map/all_gather | solution.py:160
  84.0 30.5 %copy-start.3 = (f32[512]{0:T(512)S(1)}, f32[512]{0:T(512)}, u32[]{:S(2)}) copy-start(f32[512]{0:T(512)} %param.12) | copy-start | bytes 6148
  96.9 18.0 %copy-start.2 = (bf16[512,128]{1,0:T(8,128)(2,1)S(1)}, bf16[512,128]{1,0:T(8,128)(2,1)}, u32[]{:S(2)}) copy-start(bf16[512,128]{1,0:T(8,128)(2,1)} %param.15) | copy-start | bytes 393220
  96.9 18.0 %copy-start.4 = (bf16[512,128]{1,0:T(8,128)(2,1)S(1)}, bf16[512,128]{1,0:T(8,128)(2,1)}, u32[]{:S(2)}) copy-start(bf16[512,128]{1,0:T(8,128)(2,1)} %param.13) | copy-start | bytes 393220
  115.4 67.2 %copy-start.1 = (bf16[512,128]{1,0:T(8,128)(2,1)S(1)}, bf16[512,128]{1,0:T(8,128)(2,1)}, u32[]{:S(2)}) copy-start(bf16[512,128]{1,0:T(8,128)(2,1)} %param.8) | copy-start | bytes 393220
  115.4 67.2 %copy-start.5 = (f32[128]{0:T(128)S(1)}, f32[128]{0:T(128)}, u32[]{:S(2)}) copy-start(f32[128]{0:T(128)} %param.14) | copy-start | bytes 1540
Sparse Core Ops, SparseCore 0:
  29.2 54.7 all-gather.4
  132.5 52.2 all-gather.6

commit v8 on v7

--- a/solution.py
+++ b/solution.py
@@ -164,9 +164,12 @@
 
 
 def reduce_rep(partial, cid):
-    nrep = lax.axis_size("yhi") * lax.axis_size("core")
-    pieces = partial.reshape(nrep, -1, partial.shape[1])
-    (pieces,) = group_exchange((pieces,), ((REP, False),), cid)
+    ncore = lax.axis_size("core")
+    nyhi = lax.axis_size("yhi")
+    pieces = partial.reshape(ncore, nyhi, -1, partial.shape[1])
+    (pieces,) = group_exchange((pieces,), ((("core",), False),), cid)
+    pieces = jnp.sum(pieces, axis=0)
+    (pieces,) = group_exchange((pieces,), ((("yhi",), False),), cid + 2)
     return jnp.sum(pieces, axis=0)
 
 
@@ -185,47 +188,55 @@
 
 
 def products_kernel(flag_ref, first_ref, second_ref, *refs):
-    kq = len(refs) // 2 - 1
-    firsts, seconds = refs[:kq], refs[kq : 2 * kq]
-    adj_ref, out_ref = refs[2 * kq :]
-    g = pl.program_id(0)
-    acc = jnp.zeros(out_ref.shape[1:], jnp.float32)
-    for k in range(kq):
-        block = jnp.where(flag_ref[g, k] != 0, firsts[k][0], seconds[k][0])
-        acc = acc + jnp.dot(adj_ref[0, k], block, preferred_element_type=jnp.float32)
-    out_ref[0] = acc
-
-
-def tile_products(panels, adj_tiles, index):
+    adj_ref, out_ref = refs[-2:]
+    rows, kq = adj_ref.shape[0], adj_ref.shape[1]
+    firsts, seconds = refs[: rows * kq], refs[rows * kq : 2 * rows * kq]
+    base = pl.program_id(0) * rows
+    for r in range(rows):
+        acc = jnp.zeros(out_ref.shape[1:], jnp.float32)
+        for k in range(kq):
+            at = r * kq + k
+            block = jnp.where(flag_ref[base + r, k] != 0, firsts[at][0], seconds[at][0])
+            acc = acc + jnp.dot(adj_ref[r, k], block, preferred_element_type=jnp.float32)
+        out_ref[r] = acc
+
+
+def tile_products(panels, adj_tiles, index, per_piece):
     flag, first, second = index
     rows, kq = flag.shape
     width = panels[0].shape[2]
     tile = (1, BLOCK, width)
-
-    def pick(table, k):
-        return pl.BlockSpec(tile, lambda g, f, a, b: (table(f, a, b)[g, k], 0, 0))
-
-    specs = [pick(lambda f, a, b: a, k) for k in range(kq)]
-    specs += [pick(lambda f, a, b: b, k) for k in range(kq)]
-    specs.append(pl.BlockSpec((1, kq, BLOCK, BLOCK), lambda g, f, a, b: (g, 0, 0, 0)))
+    ncore = lax.axis_size("core")
+    nyhi = lax.axis_size("yhi")
+
+    def pick(table, r, k):
+        return pl.BlockSpec(tile, lambda g, f, a, b: (table(f, a, b)[g * per_piece + r, k], 0, 0))
+
+    specs = [pick(lambda f, a, b: a, r, k) for r in range(per_piece) for k in range(kq)]
+    specs += [pick(lambda f, a, b: b, r, k) for r in range(per_piece) for k in range(kq)]
+    specs.append(pl.BlockSpec((per_piece, kq, BLOCK, BLOCK), lambda g, f, a, b: (g, 0, 0, 0)))
+    out_spec = pl.BlockSpec(
+        (per_piece, BLOCK, width), lambda g, f, a, b: ((g % ncore) * nyhi + g // ncore, 0, 0)
+    )
     summed = pl.pallas_call(
         products_kernel,
         out_shape=jax.ShapeDtypeStruct((rows, BLOCK, width), jnp.float32),
         grid_spec=pltpu.PrefetchScalarGridSpec(
             num_scalar_prefetch=3,
-            grid=(rows,),
+            grid=(rows // per_piece,),
             in_specs=specs,
-            out_specs=pl.BlockSpec(tile, lambda g, f, a, b: (g, 0, 0)),
+            out_specs=out_spec,
         ),
-    )(flag, first, second, *([panels[0]] * kq), *([panels[1]] * kq), adj_tiles[:, 0])
+    )(flag, first, second, *([panels[0]] * (per_piece * kq)), *([panels[1]] * (per_piece * kq)), adj_tiles[:, 0])
     return summed.reshape(-1, width)
 
 
 def local(node_feats, adj_tiles, col_index, w_in, b_in, w_out, b_out, cot_out):
     per_owner = node_feats.shape[0] // BLOCK
     index = staged_index(col_index[:, 0, :], per_owner)
+    per_piece = per_owner
     panels = gather_blk(node_feats, 0)
-    partial_sum = tile_products(panels, adj_tiles, index)
+    partial_sum = tile_products(panels, adj_tiles, index, per_piece)
     agg = reduce_rep(partial_sum, 8)
     agg_b = agg.astype(jnp.bfloat16)
     pre = jnp.dot(agg_b, w_in, preferred_element_type=jnp.float32) + b_in
@@ -239,7 +250,7 @@
         jnp.bfloat16
     )
     g_panels = gather_blk(g_agg, 1)
-    back_partial = tile_products(g_panels, adj_tiles, index)
+    back_partial = tile_products(g_panels, adj_tiles, index, per_piece)
     back_rows = reduce_rep(back_partial, 9)
     grad_feats = (cot_out.astype(jnp.float32) + back_rows).astype(jnp.bfloat16)
     return (out_feats, grad_feats)

time: 226 us -> 244 us (1.080)
  Pallas kernels: 194 us -> 206 us
  other arithmetic: 4.52 us -> 8.39 us
    pallas_call x4 -> x6, Pallas kernels: 69.9 us -> 94.7 us  [group_exchange(): pl.pallas_call(functools.partial(exchange_kernel, tuple(jobs)), out_shape...]
    pallas_call x2, Pallas kernels: 25.6 us -> 14.1 us  [tile_products(): pl.pallas_call(products_kernel, out_shape=jax.ShapeDtypeStruct((rows, BLO...]
    reduce_sum x0 -> x2, other arithmetic: none -> 4.29 us  [reduce_rep(): pieces = jnp.sum(pieces, axis=0)]
  transfers between devices with their start and end apart: 2 -> 2, of which waited for: 2 -> 2; matrix products, arithmetic and copies ran while one was open for 1% -> 1% of each run, Pallas kernels for 44% -> 40%
where the time goes in v8:
time: 244 us; the launch traced here: 241 us
  Pallas kernels  206 us (84%)
  between operations  14.2 us (6%)
  other arithmetic  8.39 us (3%)
  waiting for transfers between devices  7.56 us (3%)
  local copies, waits for them, and re-layouts  3.03 us (1%)
    pallas_call x2, Pallas kernels, tree_gather(): pl.pallas_call(tree_kernel, out_shape=jax.ShapeDtypeStruct((n, *src.shape...  97.3 us
    pallas_call x6, Pallas kernels, group_exchange(): pl.pallas_call(functools.partial(exchange_kernel, tuple(jobs)), out_shape...  94.7 us
    pallas_call x2, Pallas kernels, tile_products(): pl.pallas_call(products_kernel, out_shape=jax.ShapeDtypeStruct((rows, BLO...  14.1 us
    all_gather x2, waiting for transfers between devices, gather_blk(): first = lax.all_gather(first, 'z', axis=0, tiled=False)  7.53 us
  transfers between devices with their start and end apart: 2, of which 2 were waited for; matrix products, arithmetic and copies ran while one was open for 1% of the time, Pallas kernels for 40%

profile of v8, /device:TPU:9, one launch (start us, length us, event | category | flops | bytes accessed | tf_op | source)
XLA Modules:
  0.0 241.2 jit_solution(13403622720252179132)
XLA Ops:
  7.2 1.6 fusion.19
  8.8 20.3 %shard_map.95 = (bf16[8,256,128]{2,1,0:T(8,128)(2,1)}, bf16[8,256,128]{2,1,0:T(8,128)(2,1)}) custom-call(bf16[256,128]{1,0:T(8,128)(2,1)} %get-tuple-element.13.refs_0_, bf16[256,128]{1,0:T(8,128)(2,1)} %get-tuple-element.12.refs_1_), custom_call_target="tpu_custom_call" | custom-call | tf_op jit(solution)/shard_map/pallas_call | solution.py:82
  29.1 0.8 copy.14
  29.9 47.9 %shard_map.96 = bf16[8,8,256,128]{3,2,1,0:T(8,128)(2,1)} custom-call(bf16[8,256,128]{2,1,0:T(8,128)(2,1)} %get-tuple-element.7.src_ref), custom_call_target="tpu_custom_call" | custom-call | tf_op jit(solution)/shard_map/pallas_call | solution.py:142
  77.8 0.6 fusion.15.flag_ref
  78.4 0.6 select_add_fusion
  79.1 4.9 %all-gather.5.cloned.1.call-done = bf16[64,256,128]{2,1,0:T(8,128)(2,1)} async-done(((bf16[8,256,128]{2,1,0:T(8,128)(2,1)}), bf16[64,256,128]{2,1,0:T(8,128)(2,1)}) %all-gather.5.cloned.1.call-update) | async-done | bytes 4194320 | tf_op jit(solution)/shard_map/all_gather | solution.py:160
  84.0 7.0 %shard_map.97 = f32[16,128,128]{2,1,0:T(8,128)} custom-call(s32[16,4]{1,0:T(8,128)} %fusion.15.flag_ref, s32[16,4]{1,0:T(8,128)} %get-tuple-element.15.first_ref, s32[16,4]{1,0:T(8,128)} %get-tuple-element.14.second_ref, bf16[128,128,128]{2,1,0:T(8,128)(2,1)} %bitcast.46, bf16[128,128,128]{2,1,0:T(8,128)(2,1)} %bitcast.47, bf16[128,128,128]{2,1,0:T(8,128)(2,1)} %bitcast.48, ...), custom_call_target="tpu_custom_call" | custom-call | tf_op jit(solution)/shard_map/pallas_call | solution.py:221
  91.1 17.9 %shard_map.98 = f32[2,2,512,128]{3,2,1,0:T(8,128)} custom-call(f32[2,2,512,128]{3,2,1,0:T(8,128)} %bitcast.81), custom_call_target="tpu_custom_call" | custom-call | tf_op jit(solution)/shard_map/pallas_call | solution.py:82
  108.9 2.1 reduce_sum.36.refs_0_
  111.1 10.9 %shard_map.99 = f32[2,512,128]{2,1,0:T(8,128)} custom-call(f32[2,512,128]{2,1,0:T(8,128)} %reduce_sum.36.refs_0_), custom_call_target="tpu_custom_call" | custom-call | tf_op jit(solution)/shard_map/pallas_call | solution.py:82
  122.0 1.1 reduce_sum.37
  123.4 0.6 fusion.4
  124.0 0.7 fusion.18
  124.6 16.9 %shard_map.100 = (bf16[8,256,128]{2,1,0:T(8,128)(2,1)}, bf16[8,256,128]{2,1,0:T(8,128)(2,1)}) custom-call(bf16[256,128]{1,0:T(8,128)(2,1)} %get-tuple-element.11.refs_0_, bf16[256,128]{1,0:T(8,128)(2,1)} %get-tuple-element.10.refs_1_), custom_call_target="tpu_custom_call" | custom-call | tf_op jit(solution)/shard_map/pallas_call | solution.py:82
  141.6 49.4 %shard_map.101 = bf16[8,8,256,128]{3,2,1,0:T(8,128)(2,1)} custom-call(bf16[8,256,128]{2,1,0:T(8,128)(2,1)} %get-tuple-element.9.src_ref), custom_call_target="tpu_custom_call" | custom-call | tf_op jit(solution)/shard_map/pallas_call | solution.py:142
  191.0 1.1 fusion.5
  192.1 2.6 %all-gather.7.cloned.1.call-done = bf16[64,256,128]{2,1,0:T(8,128)(2,1)} async-done(((bf16[8,256,128]{2,1,0:T(8,128)(2,1)}), bf16[64,256,128]{2,1,0:T(8,128)(2,1)}) %all-gather.7.cloned.1.call-update) | async-done | bytes 4194320 | tf_op jit(solution)/shard_map/all_gather | solution.py:160
  194.6 7.0 %shard_map.102 = f32[16,128,128]{2,1,0:T(8,128)} custom-call(s32[16,4]{1,0:T(8,128)} %fusion.15.flag_ref, s32[16,4]{1,0:T(8,128)} %get-tuple-element.15.first_ref, s32[16,4]{1,0:T(8,128)} %get-tuple-element.14.second_ref, bf16[128,128,128]{2,1,0:T(8,128)(2,1)} %bitcast.62, bf16[128,128,128]{2,1,0:T(8,128)(2,1)} %bitcast.63, bf16[128,128,128]{2,1,0:T(8,128)(2,1)} %bitcast.64, ...), custom_call_target="tpu_custom_call" | custom-call | tf_op jit(solution)/shard_map/pallas_call | solution.py:221
  201.7 17.9 %shard_map.103 = f32[2,2,512,128]{3,2,1,0:T(8,128)} custom-call(f32[2,2,512,128]{3,2,1,0:T(8,128)} %bitcast.80), custom_call_target="tpu_custom_call" | custom-call | tf_op jit(solution)/shard_map/pallas_call | solution.py:82
  219.6 2.1 reduce_sum.38.refs_0_
  221.7 10.9 %shard_map.104 = f32[2,512,128]{2,1,0:T(8,128)} custom-call(f32[2,512,128]{2,1,0:T(8,128)} %reduce_sum.38.refs_0_), custom_call_target="tpu_custom_call" | custom-call | tf_op jit(solution)/shard_map/pallas_call | solution.py:82
  232.6 1.1 reduce_sum.39
  233.7 0.7 add_convert_fusion
  (17 shorter events, 0.4 us)
Async XLA Ops:
  7.2 115.9 %copy-start = (bf16[128,512]{1,0:T(8,128)(2,1)S(1)}, bf16[128,512]{1,0:T(8,128)(2,1)}, u32[]{:S(2)}) copy-start(bf16[128,512]{1,0:T(8,128)(2,1)} %param.11) | copy-start | bytes 393220
  7.2 76.8 %all-gather.5.cloned.1.call-start = ((), (), s32[]{:S(2)}) async-start(), calls=%async_computation | async-start | bytes 4718592 | tf_op jit(solution)/shard_map/all_gather | solution.py:160
  29.1 165.5 %all-gather.7.cloned.1.call-start = ((), (), s32[]{:S(2)}) async-start(), calls=%async_computation.1 | async-start | bytes 4718592 | tf_op jit(solution)/shard_map/all_gather | solution.py:160
  91.0 32.0 %copy-start.3 = (f32[512]{0:T(512)S(1)}, f32[512]{0:T(512)}, u32[]{:S(2)}) copy-start(f32[512]{0:T(512)} %param.12) | copy-start | bytes 6148
  91.1 32.3 %copy-start.2 = (bf16[512,128]{1,0:T(8,128)(2,1)S(1)}, bf16[512,128]{1,0:T(8,128)(2,1)}, u32[]{:S(2)}) copy-start(bf16[512,128]{1,0:T(8,128)(2,1)} %param.15) | copy-start | bytes 393220
  91.1 32.3 %copy-start.4 = (bf16[512,128]{1,0:T(8,128)(2,1)S(1)}, bf16[512,128]{1,0:T(8,128)(2,1)}, u32[]{:S(2)}) copy-start(bf16[512,128]{1,0:T(8,128)(2,1)} %param.13) | copy-start | bytes 393220
  124.0 67.0 %copy-start.1 = (bf16[512,128]{1,0:T(8,128)(2,1)S(1)}, bf16[512,128]{1,0:T(8,128)(2,1)}, u32[]{:S(2)}) copy-start(bf16[512,128]{1,0:T(8,128)(2,1)} %param.8) | copy-start | bytes 393220
  124.0 67.0 %copy-start.5 = (f32[128]{0:T(128)S(1)}, f32[128]{0:T(128)}, u32[]{:S(2)}) copy-start(f32[128]{0:T(128)} %param.14) | copy-start | bytes 1540
Sparse Core Ops, SparseCore 0:
  29.2 54.7 all-gather.4
  141.7 52.9 all-gather.6

commit v9 on v8

--- a/solution.py
+++ b/solution.py
@@ -164,12 +164,9 @@
 
 
 def reduce_rep(partial, cid):
-    ncore = lax.axis_size("core")
-    nyhi = lax.axis_size("yhi")
-    pieces = partial.reshape(ncore, nyhi, -1, partial.shape[1])
-    (pieces,) = group_exchange((pieces,), ((("core",), False),), cid)
-    pieces = jnp.sum(pieces, axis=0)
-    (pieces,) = group_exchange((pieces,), ((("yhi",), False),), cid + 2)
+    nrep = lax.axis_size("yhi") * lax.axis_size("core")
+    pieces = partial.reshape(nrep, -1, partial.shape[1])
+    (pieces,) = group_exchange((pieces,), ((REP, False),), cid)
     return jnp.sum(pieces, axis=0)
 
 
@@ -206,8 +203,6 @@
     rows, kq = flag.shape
     width = panels[0].shape[2]
     tile = (1, BLOCK, width)
-    ncore = lax.axis_size("core")
-    nyhi = lax.axis_size("yhi")
 
     def pick(table, r, k):
         return pl.BlockSpec(tile, lambda g, f, a, b: (table(f, a, b)[g * per_piece + r, k], 0, 0))
@@ -215,9 +210,7 @@
     specs = [pick(lambda f, a, b: a, r, k) for r in range(per_piece) for k in range(kq)]
     specs += [pick(lambda f, a, b: b, r, k) for r in range(per_piece) for k in range(kq)]
     specs.append(pl.BlockSpec((per_piece, kq, BLOCK, BLOCK), lambda g, f, a, b: (g, 0, 0, 0)))
-    out_spec = pl.BlockSpec(
-        (per_piece, BLOCK, width), lambda g, f, a, b: ((g % ncore) * nyhi + g // ncore, 0, 0)
-    )
+    out_spec = pl.BlockSpec((per_piece, BLOCK, width), lambda g, f, a, b: (g, 0, 0))
     summed = pl.pallas_call(
         products_kernel,
         out_shape=jax.ShapeDtypeStruct((rows, BLOCK, width), jnp.float32),

time: 244 us -> 214 us (0.88)
  Pallas kernels: 206 us -> 182 us
  other arithmetic: 8.39 us -> 4.52 us
    pallas_call x6 -> x4, Pallas kernels: 94.7 us -> 70 us  [group_exchange(): pl.pallas_call(functools.partial(exchange_kernel, tuple(jobs)), out_shape...]
    reduce_sum x2 -> x0, other arithmetic: 4.29 us -> none  [reduce_rep(): pieces = jnp.sum(pieces, axis=0)]
  transfers between devices with their start and end apart: 2 -> 2, of which waited for: 2 -> 2; matrix products, arithmetic and copies ran while one was open for 1% -> 1% of each run, Pallas kernels for 40% -> 46%
where the time goes in v9:
time: 214 us; the launch traced here: 212 us
  Pallas kernels  182 us (85%)
  between operations  14.2 us (7%)
  waiting for transfers between devices  6.06 us (3%)
  other arithmetic  4.52 us (2%)
  local copies, waits for them, and re-layouts  3.02 us (1%)
    pallas_call x2, Pallas kernels, tree_gather(): pl.pallas_call(tree_kernel, out_shape=jax.ShapeDtypeStruct((n, *src.shape...  98.2 us
    pallas_call x4, Pallas kernels, group_exchange(): pl.pallas_call(functools.partial(exchange_kernel, tuple(jobs)), out_shape...  70 us
    pallas_call x2, Pallas kernels, tile_products(): pl.pallas_call(products_kernel, out_shape=jax.ShapeDtypeStruct((rows, BLO...  14 us
    all_gather x2, waiting for transfers between devices, gather_blk(): first = lax.all_gather(first, 'z', axis=0, tiled=False)  6.02 us
  transfers between devices with their start and end apart: 2, of which 2 were waited for; matrix products, arithmetic and copies ran while one was open for 1% of the time, Pallas kernels for 46%

profile of v9, /device:TPU:9, one launch (start us, length us, event | category | flops | bytes accessed | tf_op | source)
XLA Modules:
  0.0 212.1 jit_solution(1160452896651232896)
XLA Ops:
  7.2 0.0 all-gather.5.cloned.1.call-start
  7.2 1.6 fusion.19
  8.8 20.3 %shard_map.95 = (bf16[8,256,128]{2,1,0:T(8,128)(2,1)}, bf16[8,256,128]{2,1,0:T(8,128)(2,1)}) custom-call(bf16[256,128]{1,0:T(8,128)(2,1)} %get-tuple-element.13.refs_0_, bf16[256,128]{1,0:T(8,128)(2,1)} %get-tuple-element.12.refs_1_), custom_call_target="tpu_custom_call" | custom-call | tf_op jit(solution)/shard_map/pallas_call | solution.py:82
  29.1 0.0 all-gather.7.cloned.1.call-start
  29.1 0.8 copy.14
  29.9 47.9 %shard_map.96 = bf16[8,8,256,128]{3,2,1,0:T(8,128)(2,1)} custom-call(bf16[8,256,128]{2,1,0:T(8,128)(2,1)} %get-tuple-element.7.src_ref), custom_call_target="tpu_custom_call" | custom-call | tf_op jit(solution)/shard_map/pallas_call | solution.py:142
  77.8 0.6 fusion.15.flag_ref
  78.4 0.6 select_add_fusion
  79.1 4.9 %all-gather.5.cloned.1.call-done = bf16[64,256,128]{2,1,0:T(8,128)(2,1)} async-done(((bf16[8,256,128]{2,1,0:T(8,128)(2,1)}), bf16[64,256,128]{2,1,0:T(8,128)(2,1)}) %all-gather.5.cloned.1.call-update) | async-done | bytes 4194320 | tf_op jit(solution)/shard_map/all_gather | solution.py:160
  84.0 7.1 %shard_map.97 = f32[16,128,128]{2,1,0:T(8,128)} custom-call(s32[16,4]{1,0:T(8,128)} %fusion.15.flag_ref, s32[16,4]{1,0:T(8,128)} %get-tuple-element.15.first_ref, s32[16,4]{1,0:T(8,128)} %get-tuple-element.14.second_ref, bf16[128,128,128]{2,1,0:T(8,128)(2,1)} %bitcast.46, bf16[128,128,128]{2,1,0:T(8,128)(2,1)} %bitcast.47, bf16[128,128,128]{2,1,0:T(8,128)(2,1)} %bitcast.48, ...), custom_call_target="tpu_custom_call" | custom-call | tf_op jit(solution)/shard_map/pallas_call | solution.py:214
  91.1 16.3 %shard_map.98 = f32[4,512,128]{2,1,0:T(8,128)} custom-call(f32[4,512,128]{2,1,0:T(8,128)} %bitcast.81), custom_call_target="tpu_custom_call" | custom-call | tf_op jit(solution)/shard_map/pallas_call | solution.py:82
  107.5 1.3 reduce_sum.18
  108.8 0.3 convolution_add_fusion
  109.1 0.6 fusion.4
  109.7 0.7 fusion.18
  110.3 16.2 %shard_map.99 = (bf16[8,256,128]{2,1,0:T(8,128)(2,1)}, bf16[8,256,128]{2,1,0:T(8,128)(2,1)}) custom-call(bf16[256,128]{1,0:T(8,128)(2,1)} %get-tuple-element.11.refs_0_, bf16[256,128]{1,0:T(8,128)(2,1)} %get-tuple-element.10.refs_1_), custom_call_target="tpu_custom_call" | custom-call | tf_op jit(solution)/shard_map/pallas_call | solution.py:82
  126.5 0.0 all-gather.7.cloned.1.call-update
  126.5 50.3 %shard_map.100 = bf16[8,8,256,128]{3,2,1,0:T(8,128)(2,1)} custom-call(bf16[8,256,128]{2,1,0:T(8,128)(2,1)} %get-tuple-element.9.src_ref), custom_call_target="tpu_custom_call" | custom-call | tf_op jit(solution)/shard_map/pallas_call | solution.py:142
  176.9 1.1 fusion.5
  178.0 1.1 all-gather.7.cloned.1.call-done
  179.0 7.0 %shard_map.101 = f32[16,128,128]{2,1,0:T(8,128)} custom-call(s32[16,4]{1,0:T(8,128)} %fusion.15.flag_ref, s32[16,4]{1,0:T(8,128)} %get-tuple-element.15.first_ref, s32[16,4]{1,0:T(8,128)} %get-tuple-element.14.second_ref, bf16[128,128,128]{2,1,0:T(8,128)(2,1)} %bitcast.62, bf16[128,128,128]{2,1,0:T(8,128)(2,1)} %bitcast.63, bf16[128,128,128]{2,1,0:T(8,128)(2,1)} %bitcast.64, ...), custom_call_target="tpu_custom_call" | custom-call | tf_op jit(solution)/shard_map/pallas_call | solution.py:214
  186.0 17.3 %shard_map.102 = f32[4,512,128]{2,1,0:T(8,128)} custom-call(f32[4,512,128]{2,1,0:T(8,128)} %bitcast.80), custom_call_target="tpu_custom_call" | custom-call | tf_op jit(solution)/shard_map/pallas_call | solution.py:82
  203.3 1.3 reduce_sum.19
  204.6 0.7 add_convert_fusion
  (13 shorter events, 0.1 us)
Async XLA Ops:
  7.2 101.6 %copy-start = (bf16[128,512]{1,0:T(8,128)(2,1)S(1)}, bf16[128,512]{1,0:T(8,128)(2,1)}, u32[]{:S(2)}) copy-start(bf16[128,512]{1,0:T(8,128)(2,1)} %param.11) | copy-start | bytes 393220
  7.2 76.8 %all-gather.5.cloned.1.call-start = ((), (), s32[]{:S(2)}) async-start(), calls=%async_computation | async-start | bytes 4718592 | tf_op jit(solution)/shard_map/all_gather | solution.py:160
  29.1 149.9 %all-gather.7.cloned.1.call-start = ((), (), s32[]{:S(2)}) async-start(), calls=%async_computation.1 | async-start | bytes 4718592 | tf_op jit(solution)/shard_map/all_gather | solution.py:160
  84.0 24.8 %copy-start.3 = (f32[512]{0:T(512)S(1)}, f32[512]{0:T(512)}, u32[]{:S(2)}) copy-start(f32[512]{0:T(512)} %param.12) | copy-start | bytes 6148
  91.1 18.0 %copy-start.2 = (bf16[512,128]{1,0:T(8,128)(2,1)S(1)}, bf16[512,128]{1,0:T(8,128)(2,1)}, u32[]{:S(2)}) copy-start(bf16[512,128]{1,0:T(8,128)(2,1)} %param.15) | copy-start | bytes 393220
  91.1 18.0 %copy-start.4 = (bf16[512,128]{1,0:T(8,128)(2,1)S(1)}, bf16[512,128]{1,0:T(8,128)(2,1)}, u32[]{:S(2)}) copy-start(bf16[512,128]{1,0:T(8,128)(2,1)} %param.13) | copy-start | bytes 393220
  109.6 67.2 %copy-start.1 = (bf16[512,128]{1,0:T(8,128)(2,1)S(1)}, bf16[512,128]{1,0:T(8,128)(2,1)}, u32[]{:S(2)}) copy-start(bf16[512,128]{1,0:T(8,128)(2,1)} %param.8) | copy-start | bytes 393220
  109.6 67.2 %copy-start.5 = (f32[128]{0:T(128)S(1)}, f32[128]{0:T(128)}, u32[]{:S(2)}) copy-start(f32[128]{0:T(128)} %param.14) | copy-start | bytes 1540
Sparse Core Ops, SparseCore 0:
  29.2 54.7 all-gather.4
  126.6 52.3 all-gather.6

commit v10 on v9

--- a/solution.py
+++ b/solution.py
@@ -93,72 +93,98 @@
     )(*srcs)
 
 
-def tree_kernel(src_ref, out_ref, send_sem, recv_sem, local_sem):
-    nx, ny = lax.axis_size("x"), lax.axis_size("ylo")
-    x, y = lax.axis_index("x"), lax.axis_index("ylo")
+def stage_two_kernel(ring_src, tree_src, ring_out, tree_out, send_sem, recv_sem, local_sem):
+    nx, ny, nz = lax.axis_size("x"), lax.axis_size("ylo"), lax.axis_size("z")
+    x, y, z = lax.axis_index("x"), lax.axis_index("ylo"), lax.axis_index("z")
     right, left, other = lax.rem(x + 1, nx), lax.rem(x + nx - 1, nx), ny - 1 - y
     to_right, to_left, to_other = {"x": right}, {"x": left}, {"ylo": other}
+    up, down = {"z": lax.rem(z + 1, nz)}, {"z": lax.rem(z + nz - 1, nz)}
     barrier = pltpu.get_barrier_semaphore()
-    for peer in (to_right, to_left, to_other):
+    for peer in (to_right, to_left, to_other, up, down):
         pl.semaphore_signal(barrier, 1, device_id=peer)
-    pl.semaphore_wait(barrier, 3)
-
-    def send(kind, src, slot, peer):
+    pl.semaphore_wait(barrier, 5)
+
+    def send(kind, src, dst, peer):
         copy = pltpu.make_async_remote_copy(
-            src_ref=src,
-            dst_ref=out_ref.at[slot],
-            send_sem=send_sem.at[kind],
-            recv_sem=recv_sem.at[kind],
-            device_id=peer,
+            src_ref=src, dst_ref=dst, send_sem=send_sem.at[kind], recv_sem=recv_sem.at[kind], device_id=peer
         )
         copy.start()
         return copy
 
     me = x * ny + y
-    own = pltpu.make_async_copy(src_ref, out_ref.at[me], local_sem)
-    own.start()
-    first_right = send(0, src_ref, me, to_right)
-    first_left = send(1, src_ref, me, to_left)
-    first_other = send(2, src_ref, me, to_other)
+    own_tree = pltpu.make_async_copy(tree_src, tree_out.at[me], local_sem.at[0])
+    own_tree.start()
+    own_ring = pltpu.make_async_copy(ring_src, ring_out.at[z], local_sem.at[1])
+    own_ring.start()
+    sent = []
+    first_right = send(0, tree_src, tree_out.at[me], to_right)
+    first_left = send(1, tree_src, tree_out.at[me], to_left)
+    first_other = send(2, tree_src, tree_out.at[me], to_other)
+    steps = nz // 2
+    split = ring_src.shape[0] // 2
+    ups = [send(7, ring_src, ring_out.at[z], up)]
+    downs = [send(7 + steps, ring_src, ring_out.at[z], down)]
+
+    def ring_step(s):
+        below = lax.rem(z + nz - (s - 1), nz)
+        above = lax.rem(z + s - 1, nz)
+        ups[-1].wait_recv()
+        downs[-1].wait_recv()
+        if s < steps:
+            ups.append(send(7 + s - 1, ring_out.at[below], ring_out.at[below], up))
+            downs.append(send(7 + steps + s - 1, ring_out.at[above], ring_out.at[above], down))
+        else:
+            ups.append(send(7 + s - 1, ring_out.at[below, :split], ring_out.at[below, :split], up))
+            downs.append(send(7 + steps + s - 1, ring_out.at[above, split:], ring_out.at[above, split:], down))
+
     first_right.wait_recv()
     from_left = left * ny + y
-    second_right = send(3, out_ref.at[from_left], from_left, to_right)
+    second_right = send(3, tree_out.at[from_left], tree_out.at[from_left], to_right)
+    ring_step(2)
     first_other.wait_recv()
     from_other = x * ny + other
-    other_right = send(4, out_ref.at[from_other], from_other, to_right)
-    other_left = send(5, out_ref.at[from_other], from_other, to_left)
+    other_right = send(4, tree_out.at[from_other], tree_out.at[from_other], to_right)
+    other_left = send(5, tree_out.at[from_other], tree_out.at[from_other], to_left)
+    ring_step(3)
     other_right.wait_recv()
     from_left_other = left * ny + other
-    third_right = send(6, out_ref.at[from_left_other], from_left_other, to_right)
-    for copy in (first_left, second_right, other_left, third_right):
+    third_right = send(6, tree_out.at[from_left_other], tree_out.at[from_left_other], to_right)
+    for s in range(4, steps + 1):
+        ring_step(s)
+    for copy in (first_left, second_right, other_left, third_right, ups[-1], downs[-1]):
         copy.wait_recv()
-    for copy in (first_right, first_left, first_other, second_right, other_right, other_left, third_right):
+    tree = [first_right, first_left, first_other, second_right, other_right, other_left, third_right]
+    for copy in tree + ups + downs:
         copy.wait_send()
-    own.wait()
-
-
-def tree_gather(src, cid):
-    n = lax.axis_size("x") * lax.axis_size("ylo")
+    own_tree.wait()
+    own_ring.wait()
+
+
+def stage_two(ring_src, tree_src, cid):
+    nz = lax.axis_size("z")
+    nxy = lax.axis_size("x") * lax.axis_size("ylo")
     return pl.pallas_call(
-        tree_kernel,
-        out_shape=jax.ShapeDtypeStruct((n, *src.shape), src.dtype),
-        in_specs=[pl.BlockSpec(memory_space=pl.ANY)],
-        out_specs=pl.BlockSpec(memory_space=pl.ANY),
+        stage_two_kernel,
+        out_shape=(
+            jax.ShapeDtypeStruct((nz, *ring_src.shape), ring_src.dtype),
+            jax.ShapeDtypeStruct((nxy, *tree_src.shape), tree_src.dtype),
+        ),
+        in_specs=[pl.BlockSpec(memory_space=pl.ANY)] * 2,
+        out_specs=(pl.BlockSpec(memory_space=pl.ANY), pl.BlockSpec(memory_space=pl.ANY)),
         scratch_shapes=[
-            pltpu.SemaphoreType.DMA((7,)),
-            pltpu.SemaphoreType.DMA((7,)),
-            pltpu.SemaphoreType.DMA,
+            pltpu.SemaphoreType.DMA((7 + nz,)),
+            pltpu.SemaphoreType.DMA((7 + nz,)),
+            pltpu.SemaphoreType.DMA((2,)),
         ],
         compiler_params=pltpu.CompilerParams(collective_id=cid, has_side_effects=True),
-    )(src)
+    )(ring_src, tree_src)
 
 
 def gather_blk(rows, cid):
     half = rows.shape[0] // 2
     xy = (("x", "ylo"), True)
     first, second = group_exchange((rows[:half], rows[half:]), (xy, (("z",), True)), cid)
-    first = lax.all_gather(first, "z", axis=0, tiled=False)
-    second = tree_gather(second, cid + 4)
+    first, second = stage_two(first, second, cid + 4)
     width = rows.shape[1]
     return first.reshape(-1, BLOCK, width), second.reshape(-1, BLOCK, width)
 

time: 214 us -> 199 us (0.930)
  between operations: 14.2 us -> 0.79 us
  waiting for transfers between devices: 6.06 us -> 0 us
  Pallas kernels: 182 us -> 188 us
    all_gather x2 -> x0, waiting for transfers between devices: 6.02 us -> none  [gather_blk(): first = lax.all_gather(first, 'z', axis=0, tiled=False)]
    pallas_call x4, Pallas kernels: 70 us -> 74.6 us  [group_exchange(): pl.pallas_call(functools.partial(exchange_kernel, tuple(jobs)), out_shape...]
  transfers between devices with their start and end apart: 2 -> 0, of which waited for: 2 -> 0; matrix products, arithmetic and copies ran while one was open for 1% -> 0% of each run, Pallas kernels for 46% -> 0%
where the time goes in v10:
time: 199 us; the launch traced here: 198 us
  Pallas kernels  188 us (94%)
  other arithmetic  4.54 us (2%)
  local copies, waits for them, and re-layouts  3.02 us (2%)
    pallas_call x2, Pallas kernels, stage_two(): pl.pallas_call(stage_two_kernel, out_shape=(jax.ShapeDtypeStruct((nz, *ri...  99.3 us
    pallas_call x4, Pallas kernels, group_exchange(): pl.pallas_call(functools.partial(exchange_kernel, tuple(jobs)), out_shape...  74.6 us
    pallas_call x2, Pallas kernels, tile_products(): pl.pallas_call(products_kernel, out_shape=jax.ShapeDtypeStruct((rows, BLO...  14 us

profile of v10, /device:TPU:9, one launch (start us, length us, event | category | flops | bytes accessed | tf_op | source)
XLA Modules:
  0.0 198.3 jit_solution(1619813025646496724)
XLA Ops:
  0.6 0.0 copy-start
  0.6 0.8 copy.10
  1.4 0.6 fusion.15.flag_ref
  2.0 0.6 select_add_fusion
  2.7 1.5 fusion.19
  4.2 20.3 %shard_map.95 = (bf16[8,256,128]{2,1,0:T(8,128)(2,1)}, bf16[8,256,128]{2,1,0:T(8,128)(2,1)}) custom-call(bf16[256,128]{1,0:T(8,128)(2,1)} %get-tuple-element.21.refs_0_, bf16[256,128]{1,0:T(8,128)(2,1)} %get-tuple-element.20.refs_1_), custom_call_target="tpu_custom_call" | custom-call | tf_op jit(solution)/shard_map/pallas_call | solution.py:82
  24.5 49.4 %shard_map.96 = (bf16[8,8,256,128]{3,2,1,0:T(8,128)(2,1)}, bf16[8,8,256,128]{3,2,1,0:T(8,128)(2,1)}) custom-call(bf16[8,256,128]{2,1,0:T(8,128)(2,1)} %get-tuple-element.10.ring_src, bf16[8,256,128]{2,1,0:T(8,128)(2,1)} %get-tuple-element.11.tree_src), custom_call_target="tpu_custom_call" | custom-call | tf_op jit(solution)/shard_map/pallas_call | solution.py:166
  73.9 0.0 copy-start.3
  73.9 7.0 %shard_map.97 = f32[16,128,128]{2,1,0:T(8,128)} custom-call(s32[16,4]{1,0:T(8,128)} %fusion.15.flag_ref, s32[16,4]{1,0:T(8,128)} %get-tuple-element.23.first_ref, s32[16,4]{1,0:T(8,128)} %get-tuple-element.22.second_ref, bf16[128,128,128]{2,1,0:T(8,128)(2,1)} %bitcast.46, bf16[128,128,128]{2,1,0:T(8,128)(2,1)} %bitcast.47, bf16[128,128,128]{2,1,0:T(8,128)(2,1)} %bitcast.48, ...), custom_call_target="tpu_custom_call" | custom-call | tf_op jit(solution)/shard_map/pallas_call | solution.py:240
  80.9 0.0 copy-start.1
  80.9 0.0 copy-start.4
  81.0 0.0 copy-start.5
  81.0 18.7 %shard_map.98 = f32[4,512,128]{2,1,0:T(8,128)} custom-call(f32[4,512,128]{2,1,0:T(8,128)} %bitcast.81), custom_call_target="tpu_custom_call" | custom-call | tf_op jit(solution)/shard_map/pallas_call | solution.py:82
  99.6 1.3 reduce_sum.18
  101.0 0.3 convolution_add_fusion
  101.3 1.1 fusion.5
  102.4 0.6 fusion.4
  103.0 0.7 fusion.18
  103.6 17.7 %shard_map.99 = (bf16[8,256,128]{2,1,0:T(8,128)(2,1)}, bf16[8,256,128]{2,1,0:T(8,128)(2,1)}) custom-call(bf16[256,128]{1,0:T(8,128)(2,1)} %get-tuple-element.19.refs_0_, bf16[256,128]{1,0:T(8,128)(2,1)} %get-tuple-element.18.refs_1_), custom_call_target="tpu_custom_call" | custom-call | tf_op jit(solution)/shard_map/pallas_call | solution.py:82
  121.3 49.9 %shard_map.100 = (bf16[8,8,256,128]{3,2,1,0:T(8,128)(2,1)}, bf16[8,8,256,128]{3,2,1,0:T(8,128)(2,1)}) custom-call(bf16[8,256,128]{2,1,0:T(8,128)(2,1)} %get-tuple-element.14.ring_src, bf16[8,256,128]{2,1,0:T(8,128)(2,1)} %get-tuple-element.15.tree_src), custom_call_target="tpu_custom_call" | custom-call | tf_op jit(solution)/shard_map/pallas_call | solution.py:166
  171.2 7.0 %shard_map.101 = f32[16,128,128]{2,1,0:T(8,128)} custom-call(s32[16,4]{1,0:T(8,128)} %fusion.15.flag_ref, s32[16,4]{1,0:T(8,128)} %get-tuple-element.23.first_ref, s32[16,4]{1,0:T(8,128)} %get-tuple-element.22.second_ref, bf16[128,128,128]{2,1,0:T(8,128)(2,1)} %bitcast.14, bf16[128,128,128]{2,1,0:T(8,128)(2,1)} %bitcast.15, bf16[128,128,128]{2,1,0:T(8,128)(2,1)} %bitcast.16, ...), custom_call_target="tpu_custom_call" | custom-call | tf_op jit(solution)/shard_map/pallas_call | solution.py:240
  178.3 18.0 %shard_map.102 = f32[4,512,128]{2,1,0:T(8,128)} custom-call(f32[4,512,128]{2,1,0:T(8,128)} %bitcast.80), custom_call_target="tpu_custom_call" | custom-call | tf_op jit(solution)/shard_map/pallas_call | solution.py:82
  196.3 1.3 reduce_sum.19
  197.6 0.7 add_convert_fusion
  (7 shorter events, 0.0 us)
Async XLA Ops:
  0.6 100.3 %copy-start = (bf16[128,512]{1,0:T(8,128)(2,1)S(1)}, bf16[128,512]{1,0:T(8,128)(2,1)}, u32[]{:S(2)}) copy-start(bf16[128,512]{1,0:T(8,128)(2,1)} %param.11) | copy-start | bytes 393220
  73.9 27.1 %copy-start.3 = (f32[512]{0:T(512)S(1)}, f32[512]{0:T(512)}, u32[]{:S(2)}) copy-start(f32[512]{0:T(512)} %param.12) | copy-start | bytes 6148
  80.9 20.3 %copy-start.1 = (bf16[512,128]{1,0:T(8,128)(2,1)S(1)}, bf16[512,128]{1,0:T(8,128)(2,1)}, u32[]{:S(2)}) copy-start(bf16[512,128]{1,0:T(8,128)(2,1)} %param.8) | copy-start | bytes 393220
  80.9 20.3 %copy-start.4 = (bf16[512,128]{1,0:T(8,128)(2,1)S(1)}, bf16[512,128]{1,0:T(8,128)(2,1)}, u32[]{:S(2)}) copy-start(bf16[512,128]{1,0:T(8,128)(2,1)} %param.13) | copy-start | bytes 393220
  81.0 20.3 %copy-start.5 = (f32[128]{0:T(128)S(1)}, f32[128]{0:T(128)}, u32[]{:S(2)}) copy-start(f32[128]{0:T(128)} %param.14) | copy-start | bytes 1540
  99.6 2.8 %copy-start.2 = (bf16[512,128]{1,0:T(8,128)(2,1)S(1)}, bf16[512,128]{1,0:T(8,128)(2,1)}, u32[]{:S(2)}) copy-start(bf16[512,128]{1,0:T(8,128)(2,1)} %param.15) | copy-start | bytes 393220

commit v11 on v10

--- a/solution.py
+++ b/solution.py
@@ -182,8 +182,7 @@
 
 def gather_blk(rows, cid):
     half = rows.shape[0] // 2
-    xy = (("x", "ylo"), True)
-    first, second = group_exchange((rows[:half], rows[half:]), (xy, (("z",), True)), cid)
+    second, first = stage_two(rows[half:], rows[:half], cid)
     first, second = stage_two(first, second, cid + 4)
     width = rows.shape[1]
     return first.reshape(-1, BLOCK, width), second.reshape(-1, BLOCK, width)

time: 199 us -> 195 us (0.980)
  Pallas kernels: 188 us -> 182 us
    pallas_call x4 -> x2, Pallas kernels: 74.6 us -> 40.1 us  [group_exchange(): pl.pallas_call(functools.partial(exchange_kernel, tuple(jobs)), out_shape...]
    pallas_call x2 -> x4, Pallas kernels: 99.3 us -> 128 us  [stage_two(): pl.pallas_call(stage_two_kernel, out_shape=(jax.ShapeDtypeStruct((nz, *ri...]
where the time goes in v11:
time: 195 us; the launch traced here: 192 us
  Pallas kernels  182 us (93%)
  other arithmetic  4.54 us (2%)
  local copies, waits for them, and re-layouts  3.02 us (2%)
    pallas_call x4, Pallas kernels, stage_two(): pl.pallas_call(stage_two_kernel, out_shape=(jax.ShapeDtypeStruct((nz, *ri...  128 us
    pallas_call x2, Pallas kernels, group_exchange(): pl.pallas_call(functools.partial(exchange_kernel, tuple(jobs)), out_shape...  40.1 us
    pallas_call x2, Pallas kernels, tile_products(): pl.pallas_call(products_kernel, out_shape=jax.ShapeDtypeStruct((rows, BLO...  14.2 us

profile of v11, /device:TPU:9, one launch (start us, length us, event | category | flops | bytes accessed | tf_op | source)
XLA Modules:
  0.0 192.3 jit_solution(7618747271473272333)
XLA Ops:
  0.6 0.0 copy-start
  0.6 0.8 copy.10
  1.4 0.6 fusion.15.flag_ref
  2.0 0.6 select_add_fusion
  2.7 1.5 fusion.19
  4.2 20.2 %shard_map.95 = (bf16[8,256,128]{2,1,0:T(8,128)(2,1)}, bf16[8,256,128]{2,1,0:T(8,128)(2,1)}) custom-call(bf16[256,128]{1,0:T(8,128)(2,1)} %get-tuple-element.21.ring_src, bf16[256,128]{1,0:T(8,128)(2,1)} %get-tuple-element.20.tree_src), custom_call_target="tpu_custom_call" | custom-call | tf_op jit(solution)/shard_map/pallas_call | solution.py:166
  24.4 45.3 %shard_map.96 = (bf16[8,8,256,128]{3,2,1,0:T(8,128)(2,1)}, bf16[8,8,256,128]{3,2,1,0:T(8,128)(2,1)}) custom-call(bf16[8,256,128]{2,1,0:T(8,128)(2,1)} %get-tuple-element.10.ring_src, bf16[8,256,128]{2,1,0:T(8,128)(2,1)} %get-tuple-element.11.tree_src), custom_call_target="tpu_custom_call" | custom-call | tf_op jit(solution)/shard_map/pallas_call | solution.py:166
  69.7 0.0 copy-start.3
  69.7 7.1 %shard_map.97 = f32[16,128,128]{2,1,0:T(8,128)} custom-call(s32[16,4]{1,0:T(8,128)} %fusion.15.flag_ref, s32[16,4]{1,0:T(8,128)} %get-tuple-element.23.first_ref, s32[16,4]{1,0:T(8,128)} %get-tuple-element.22.second_ref, bf16[128,128,128]{2,1,0:T(8,128)(2,1)} %bitcast.46, bf16[128,128,128]{2,1,0:T(8,128)(2,1)} %bitcast.47, bf16[128,128,128]{2,1,0:T(8,128)(2,1)} %bitcast.48, ...), custom_call_target="tpu_custom_call" | custom-call | tf_op jit(solution)/shard_map/pallas_call | solution.py:239
  76.9 0.0 copy-start.1
  76.9 0.0 copy-start.4
  76.9 20.5 %shard_map.98 = f32[4,512,128]{2,1,0:T(8,128)} custom-call(f32[4,512,128]{2,1,0:T(8,128)} %bitcast.81), custom_call_target="tpu_custom_call" | custom-call | tf_op jit(solution)/shard_map/pallas_call | solution.py:82
  97.4 0.0 copy-start.2
  97.4 1.3 reduce_sum.18
  98.8 0.3 convolution_add_fusion
  99.1 1.1 fusion.5
  100.2 0.6 fusion.4
  100.8 0.7 fusion.18
  101.4 16.0 %shard_map.99 = (bf16[8,256,128]{2,1,0:T(8,128)(2,1)}, bf16[8,256,128]{2,1,0:T(8,128)(2,1)}) custom-call(bf16[256,128]{1,0:T(8,128)(2,1)} %get-tuple-element.19.ring_src, bf16[256,128]{1,0:T(8,128)(2,1)} %get-tuple-element.18.tree_src), custom_call_target="tpu_custom_call" | custom-call | tf_op jit(solution)/shard_map/pallas_call | solution.py:166
  117.4 46.2 %shard_map.100 = (bf16[8,8,256,128]{3,2,1,0:T(8,128)(2,1)}, bf16[8,8,256,128]{3,2,1,0:T(8,128)(2,1)}) custom-call(bf16[8,256,128]{2,1,0:T(8,128)(2,1)} %get-tuple-element.14.ring_src, bf16[8,256,128]{2,1,0:T(8,128)(2,1)} %get-tuple-element.15.tree_src), custom_call_target="tpu_custom_call" | custom-call | tf_op jit(solution)/shard_map/pallas_call | solution.py:166
  163.6 7.1 %shard_map.101 = f32[16,128,128]{2,1,0:T(8,128)} custom-call(s32[16,4]{1,0:T(8,128)} %fusion.15.flag_ref, s32[16,4]{1,0:T(8,128)} %get-tuple-element.23.first_ref, s32[16,4]{1,0:T(8,128)} %get-tuple-element.22.second_ref, bf16[128,128,128]{2,1,0:T(8,128)(2,1)} %bitcast.14, bf16[128,128,128]{2,1,0:T(8,128)(2,1)} %bitcast.15, bf16[128,128,128]{2,1,0:T(8,128)(2,1)} %bitcast.16, ...), custom_call_target="tpu_custom_call" | custom-call | tf_op jit(solution)/shard_map/pallas_call | solution.py:239
  170.8 19.5 %shard_map.102 = f32[4,512,128]{2,1,0:T(8,128)} custom-call(f32[4,512,128]{2,1,0:T(8,128)} %bitcast.80), custom_call_target="tpu_custom_call" | custom-call | tf_op jit(solution)/shard_map/pallas_call | solution.py:82
  190.3 1.3 reduce_sum.19
  191.6 0.7 add_convert_fusion
  (7 shorter events, 0.0 us)
Async XLA Ops:
  0.6 98.1 %copy-start = (bf16[128,512]{1,0:T(8,128)(2,1)S(1)}, bf16[128,512]{1,0:T(8,128)(2,1)}, u32[]{:S(2)}) copy-start(bf16[128,512]{1,0:T(8,128)(2,1)} %param.11) | copy-start | bytes 393220
  69.7 29.1 %copy-start.3 = (f32[512]{0:T(512)S(1)}, f32[512]{0:T(512)}, u32[]{:S(2)}) copy-start(f32[512]{0:T(512)} %param.12) | copy-start | bytes 6148
  76.9 22.2 %copy-start.1 = (bf16[512,128]{1,0:T(8,128)(2,1)S(1)}, bf16[512,128]{1,0:T(8,128)(2,1)}, u32[]{:S(2)}) copy-start(bf16[512,128]{1,0:T(8,128)(2,1)} %param.8) | copy-start | bytes 393220
  76.9 22.2 %copy-start.4 = (bf16[512,128]{1,0:T(8,128)(2,1)S(1)}, bf16[512,128]{1,0:T(8,128)(2,1)}, u32[]{:S(2)}) copy-start(bf16[512,128]{1,0:T(8,128)(2,1)} %param.13) | copy-start | bytes 393220
  76.9 22.2 %copy-start.5 = (f32[128]{0:T(128)S(1)}, f32[128]{0:T(128)}, u32[]{:S(2)}) copy-start(f32[128]{0:T(128)} %param.14) | copy-start | bytes 1540
  97.4 2.8 %copy-start.2 = (bf16[512,128]{1,0:T(8,128)(2,1)S(1)}, bf16[512,128]{1,0:T(8,128)(2,1)}, u32[]{:S(2)}) copy-start(bf16[512,128]{1,0:T(8,128)(2,1)} %param.15) | copy-start | bytes 393220

commit v12 on v11

--- a/solution.py
+++ b/solution.py
@@ -93,7 +93,20 @@
     )(*srcs)
 
 
-def stage_two_kernel(ring_src, tree_src, ring_out, tree_out, send_sem, recv_sem, local_sem):
+def stage_two_kernel(halves, *refs):
+    if halves:
+        rows_ref = refs[0]
+        half = rows_ref.shape[0] // 2
+        ring_src, tree_src = rows_ref.at[pl.ds(half, half)], rows_ref.at[pl.ds(0, half)]
+        refs = refs[1:]
+    else:
+        ring_src, tree_src = refs[:2]
+        refs = refs[2:]
+    ring_out, tree_out, send_sem, recv_sem, local_sem = refs
+    stage_two_body(ring_src, tree_src, ring_out, tree_out, send_sem, recv_sem, local_sem)
+
+
+def stage_two_body(ring_src, tree_src, ring_out, tree_out, send_sem, recv_sem, local_sem):
     nx, ny, nz = lax.axis_size("x"), lax.axis_size("ylo"), lax.axis_size("z")
     x, y, z = lax.axis_index("x"), lax.axis_index("ylo"), lax.axis_index("z")
     right, left, other = lax.rem(x + 1, nx), lax.rem(x + nx - 1, nx), ny - 1 - y
@@ -160,16 +173,22 @@
     own_ring.wait()
 
 
-def stage_two(ring_src, tree_src, cid):
+def stage_two(srcs, cid):
     nz = lax.axis_size("z")
     nxy = lax.axis_size("x") * lax.axis_size("ylo")
+    if len(srcs) == 1:
+        half = srcs[0].shape[0] // 2
+        ring_shape = tree_shape = (half, *srcs[0].shape[1:])
+    else:
+        ring_shape, tree_shape = srcs[0].shape, srcs[1].shape
+    dtype = srcs[0].dtype
     return pl.pallas_call(
-        stage_two_kernel,
+        functools.partial(stage_two_kernel, len(srcs) == 1),
         out_shape=(
-            jax.ShapeDtypeStruct((nz, *ring_src.shape), ring_src.dtype),
-            jax.ShapeDtypeStruct((nxy, *tree_src.shape), tree_src.dtype),
+            jax.ShapeDtypeStruct((nz, *ring_shape), dtype),
+            jax.ShapeDtypeStruct((nxy, *tree_shape), dtype),
         ),
-        in_specs=[pl.BlockSpec(memory_space=pl.ANY)] * 2,
+        in_specs=[pl.BlockSpec(memory_space=pl.ANY)] * len(srcs),
         out_specs=(pl.BlockSpec(memory_space=pl.ANY), pl.BlockSpec(memory_space=pl.ANY)),
         scratch_shapes=[
             pltpu.SemaphoreType.DMA((7 + nz,)),
@@ -177,27 +196,65 @@
             pltpu.SemaphoreType.DMA((2,)),
         ],
         compiler_params=pltpu.CompilerParams(collective_id=cid, has_side_effects=True),
-    )(ring_src, tree_src)
+    )(*srcs)
 
 
 def gather_blk(rows, cid):
-    half = rows.shape[0] // 2
-    second, first = stage_two(rows[half:], rows[:half], cid)
-    first, second = stage_two(first, second, cid + 4)
+    second, first = stage_two((rows,), cid)
+    first, second = stage_two((first, second), cid + 4)
     width = rows.shape[1]
     return first.reshape(-1, BLOCK, width), second.reshape(-1, BLOCK, width)
+
+
+def reduce_kernel(src_ref, out_ref, landed, send_sem, recv_sem, local_sem):
+    me, sizes = group_place(REP)
+    n = landed.shape[0]
+    barrier = pltpu.get_barrier_semaphore()
+    for d in range(1, n):
+        pl.semaphore_signal(barrier, 1, device_id=peer_id(REP, sizes, lax.rem(me + d, n)))
+    pl.semaphore_wait(barrier, n - 1)
+    copies = []
+    for d in range(1, n):
+        p = lax.rem(me + d, n)
+        copy = pltpu.make_async_remote_copy(
+            src_ref=src_ref.at[p],
+            dst_ref=landed.at[me],
+            send_sem=send_sem.at[d],
+            recv_sem=recv_sem.at[d],
+            device_id=peer_id(REP, sizes, p),
+        )
+        copy.start()
+        copies.append(copy)
+    own = pltpu.make_async_copy(src_ref.at[me], landed.at[me], local_sem)
+    own.start()
+    for copy in copies:
+        copy.wait()
+    own.wait()
+    total = landed[0]
+    for slot in range(1, n):
+        total = total + landed[slot]
+    out_ref[...] = total
 
 
 def reduce_rep(partial, cid):
     nrep = lax.axis_size("yhi") * lax.axis_size("core")
     pieces = partial.reshape(nrep, -1, partial.shape[1])
-    (pieces,) = group_exchange((pieces,), ((REP, False),), cid)
-    return jnp.sum(pieces, axis=0)
-
-
-def staged_index(col, per_owner):
-    nz = lax.axis_size("z")
-    nxy = lax.axis_size("x") * lax.axis_size("ylo")
+    return pl.pallas_call(
+        reduce_kernel,
+        out_shape=jax.ShapeDtypeStruct(pieces.shape[1:], pieces.dtype),
+        in_specs=[pl.BlockSpec(memory_space=pl.ANY)],
+        out_specs=pl.BlockSpec(memory_space=pltpu.VMEM),
+        scratch_shapes=[
+            pltpu.VMEM(pieces.shape, pieces.dtype),
+            pltpu.SemaphoreType.DMA((nrep,)),
+            pltpu.SemaphoreType.DMA((nrep,)),
+            pltpu.SemaphoreType.DMA,
+        ],
+        compiler_params=pltpu.CompilerParams(collective_id=cid, has_side_effects=True),
+    )(pieces)
+
+
+def block_of(col, per_owner, nz, nxy):
     half = per_owner // 2
     owner = col // per_owner
     sub = col % per_owner
@@ -206,10 +263,10 @@
     in_first = sub < half
     first = (z * nxy + xy) * half + jnp.where(in_first, sub, 0)
     second = (xy * nz + z) * half + jnp.where(in_first, 0, sub - half)
-    return in_first.astype(jnp.int32), first, second
-
-
-def products_kernel(flag_ref, first_ref, second_ref, *refs):
+    return in_first, first, second
+
+
+def products_kernel(layout, col_ref, *refs):
     adj_ref, out_ref = refs[-2:]
     rows, kq = adj_ref.shape[0], adj_ref.shape[1]
     firsts, seconds = refs[: rows * kq], refs[rows * kq : 2 * rows * kq]
@@ -218,41 +275,43 @@
         acc = jnp.zeros(out_ref.shape[1:], jnp.float32)
         for k in range(kq):
             at = r * kq + k
-            block = jnp.where(flag_ref[base + r, k] != 0, firsts[at][0], seconds[at][0])
+            in_first = block_of(col_ref[base + r, k], *layout)[0]
+            block = jnp.where(in_first, firsts[at][0], seconds[at][0])
             acc = acc + jnp.dot(adj_ref[r, k], block, preferred_element_type=jnp.float32)
         out_ref[r] = acc
 
 
-def tile_products(panels, adj_tiles, index, per_piece):
-    flag, first, second = index
-    rows, kq = flag.shape
+def tile_products(panels, adj_tiles, col, per_piece):
+    rows, kq = col.shape
     width = panels[0].shape[2]
     tile = (1, BLOCK, width)
-
-    def pick(table, r, k):
-        return pl.BlockSpec(tile, lambda g, f, a, b: (table(f, a, b)[g * per_piece + r, k], 0, 0))
-
-    specs = [pick(lambda f, a, b: a, r, k) for r in range(per_piece) for k in range(kq)]
-    specs += [pick(lambda f, a, b: b, r, k) for r in range(per_piece) for k in range(kq)]
-    specs.append(pl.BlockSpec((per_piece, kq, BLOCK, BLOCK), lambda g, f, a, b: (g, 0, 0, 0)))
-    out_spec = pl.BlockSpec((per_piece, BLOCK, width), lambda g, f, a, b: (g, 0, 0))
+    layout = (panels[0].shape[0] * 2 // lax.axis_size(BLK), lax.axis_size("z"),
+              lax.axis_size("x") * lax.axis_size("ylo"))
+
+    def pick(which, r, k):
+        return pl.BlockSpec(
+            tile, lambda g, c: (block_of(c[g * per_piece + r, k], *layout)[which], 0, 0)
+        )
+
+    specs = [pick(1, r, k) for r in range(per_piece) for k in range(kq)]
+    specs += [pick(2, r, k) for r in range(per_piece) for k in range(kq)]
+    specs.append(pl.BlockSpec((per_piece, kq, BLOCK, BLOCK), lambda g, c: (g, 0, 0, 0)))
     summed = pl.pallas_call(
-        products_kernel,
+        functools.partial(products_kernel, layout),
         out_shape=jax.ShapeDtypeStruct((rows, BLOCK, width), jnp.float32),
         grid_spec=pltpu.PrefetchScalarGridSpec(
-            num_scalar_prefetch=3,
+            num_scalar_prefetch=1,
             grid=(rows // per_piece,),
             in_specs=specs,
-            out_specs=out_spec,
+            out_specs=pl.BlockSpec((per_piece, BLOCK, width), lambda g, c: (g, 0, 0)),
         ),
-    )(flag, first, second, *([panels[0]] * (per_piece * kq)), *([panels[1]] * (per_piece * kq)), adj_tiles[:, 0])
+    )(col, *([panels[0]] * (per_piece * kq)), *([panels[1]] * (per_piece * kq)), adj_tiles[:, 0])
     return summed.reshape(-1, width)
 
 
 def local(node_feats, adj_tiles, col_index, w_in, b_in, w_out, b_out, cot_out):
-    per_owner = node_feats.shape[0] // BLOCK
-    index = staged_index(col_index[:, 0, :], per_owner)
-    per_piece = per_owner
+    per_piece = node_feats.shape[0] // BLOCK
+    index = col_index.reshape(col_index.shape[0], -1)
     panels = gather_blk(node_feats, 0)
     partial_sum = tile_products(panels, adj_tiles, index, per_piece)
     agg = reduce_rep(partial_sum, 8)

time: 195 us -> 202 us (1.036)
  Pallas kernels: 182 us -> 192 us
  other arithmetic: 4.54 us -> 1.63 us
    pallas_call x8, Pallas kernels: 182 us -> 192 us  [the longest x4 129 us: stage_two(): pl.pallas_call(functools.partial(stage_two_kernel, len(srcs) == 1), out_s...]
    reduce_sum x2 -> x0, other arithmetic: 2.63 us -> none  [reduce_rep(): return jnp.sum(pieces, axis=0)]
    slice x2 -> x0, local copies, waits for them, and re-layouts: 2.19 us -> none  [gather_blk(): second, first = stage_two(rows[half:], rows[:half], cid)]
where the time goes in v12:
time: 202 us; the launch traced here: 200 us
  Pallas kernels  192 us (95%)
  matrix products  3.54 us (2%)
    pallas_call x4, Pallas kernels, stage_two(): pl.pallas_call(functools.partial(stage_two_kernel, len(srcs) == 1), out_s...  129 us
    pallas_call x2, Pallas kernels, reduce_rep(): pl.pallas_call(reduce_kernel, out_shape=jax.ShapeDtypeStruct(pieces.shape...  40 us
    pallas_call x2, Pallas kernels, tile_products(): pl.pallas_call(functools.partial(products_kernel, layout), out_shape=jax....  23.2 us

profile of v12, /device:TPU:9, one launch (start us, length us, event | category | flops | bytes accessed | tf_op | source)
XLA Modules:
  0.0 199.6 jit_solution(6857436729546972769)
XLA Ops:
  0.6 0.0 copy-start
  0.6 1.4 copy.10.col_ref
  2.0 20.2 %shard_map.95 = (bf16[8,256,128]{2,1,0:T(8,128)(2,1)}, bf16[8,256,128]{2,1,0:T(8,128)(2,1)}) custom-call(bf16[512,128]{1,0:T(8,128)(2,1)} %refs_0_.1), custom_call_target="tpu_custom_call" | custom-call | tf_op jit(solution)/shard_map/pallas_call | solution.py:185
  22.3 45.3 %shard_map.96 = (bf16[8,8,256,128]{3,2,1,0:T(8,128)(2,1)}, bf16[8,8,256,128]{3,2,1,0:T(8,128)(2,1)}) custom-call(bf16[8,256,128]{2,1,0:T(8,128)(2,1)} %get-tuple-element.10.refs_0_, bf16[8,256,128]{2,1,0:T(8,128)(2,1)} %get-tuple-element.11.refs_1_), custom_call_target="tpu_custom_call" | custom-call | tf_op jit(solution)/shard_map/pallas_call | solution.py:185
  67.5 0.0 copy-start.3
  67.6 0.0 copy-start.1
  67.6 0.0 copy-start.4
  67.6 0.0 copy-start.5
  67.6 11.7 %shard_map.97 = f32[16,128,128]{2,1,0:T(8,128)} custom-call(s32[16,4]{1,0:T(8,128)} %copy.10.col_ref, bf16[128,128,128]{2,1,0:T(8,128)(2,1)} %bitcast.45, bf16[128,128,128]{2,1,0:T(8,128)(2,1)} %bitcast.46, bf16[128,128,128]{2,1,0:T(8,128)(2,1)} %bitcast.47, bf16[128,128,128]{2,1,0:T(8,128)(2,1)} %bitcast.48, bf16[128,128,128]{2,1,0:T(8,128)(2,1)} %bitcast.49, ...), custom_call_target="tpu_custom_call" | custom-call | tf_op jit(solution)/shard_map/pallas_call | solution.py:299
  79.3 0.0 copy-start.2
  79.3 21.1 %shard_map.98 = f32[512,128]{1,0:T(8,128)} custom-call(f32[4,512,128]{2,1,0:T(8,128)} %bitcast.80), custom_call_target="tpu_custom_call" | custom-call | tf_op jit(solution)/shard_map/pallas_call | solution.py:242
  100.4 0.0 copy-done
  100.4 0.0 copy-done.3
  100.4 1.2 convolution_add_fusion
  101.6 0.0 copy-done.1
  101.7 0.0 copy-done.4
  101.7 0.0 copy-done.5
  101.7 1.1 fusion.5
  102.8 1.2 fusion.4.refs_0_
  104.0 16.0 %shard_map.99 = (bf16[8,256,128]{2,1,0:T(8,128)(2,1)}, bf16[8,256,128]{2,1,0:T(8,128)(2,1)}) custom-call(bf16[512,128]{1,0:T(8,128)(2,1)} %fusion.4.refs_0_), custom_call_target="tpu_custom_call" | custom-call | tf_op jit(solution)/shard_map/pallas_call | solution.py:185
  120.0 47.5 %shard_map.100 = (bf16[8,8,256,128]{3,2,1,0:T(8,128)(2,1)}, bf16[8,8,256,128]{3,2,1,0:T(8,128)(2,1)}) custom-call(bf16[8,256,128]{2,1,0:T(8,128)(2,1)} %get-tuple-element.14.refs_0_, bf16[8,256,128]{2,1,0:T(8,128)(2,1)} %get-tuple-element.15.refs_1_), custom_call_target="tpu_custom_call" | custom-call | tf_op jit(solution)/shard_map/pallas_call | solution.py:185
  167.5 11.5 %shard_map.101 = f32[16,128,128]{2,1,0:T(8,128)} custom-call(s32[16,4]{1,0:T(8,128)} %copy.10.col_ref, bf16[128,128,128]{2,1,0:T(8,128)(2,1)} %bitcast.13, bf16[128,128,128]{2,1,0:T(8,128)(2,1)} %bitcast.14, bf16[128,128,128]{2,1,0:T(8,128)(2,1)} %bitcast.15, bf16[128,128,128]{2,1,0:T(8,128)(2,1)} %bitcast.16, bf16[128,128,128]{2,1,0:T(8,128)(2,1)} %bitcast.17, ...), custom_call_target="tpu_custom_call" | custom-call | tf_op jit(solution)/shard_map/pallas_call | solution.py:299
  179.0 18.9 %shard_map.102 = f32[512,128]{1,0:T(8,128)} custom-call(f32[4,512,128]{2,1,0:T(8,128)} %bitcast.79), custom_call_target="tpu_custom_call" | custom-call | tf_op jit(solution)/shard_map/pallas_call | solution.py:242
  197.9 1.6 add_convert_fusion
  (1 shorter events, 0.0 us)
Async XLA Ops:
  0.6 99.8 %copy-start = (bf16[128,512]{1,0:T(8,128)(2,1)S(1)}, bf16[128,512]{1,0:T(8,128)(2,1)}, u32[]{:S(2)}) copy-start(bf16[128,512]{1,0:T(8,128)(2,1)} %param.11) | copy-start | bytes 393220
  67.5 32.9 %copy-start.3 = (f32[512]{0:T(512)S(1)}, f32[512]{0:T(512)}, u32[]{:S(2)}) copy-start(f32[512]{0:T(512)} %param.12) | copy-start | bytes 6148
  67.6 34.1 %copy-start.1 = (bf16[512,128]{1,0:T(8,128)(2,1)S(1)}, bf16[512,128]{1,0:T(8,128)(2,1)}, u32[]{:S(2)}) copy-start(bf16[512,128]{1,0:T(8,128)(2,1)} %refs_0_.1) | copy-start | bytes 393220
  67.6 34.1 %copy-start.4 = (bf16[512,128]{1,0:T(8,128)(2,1)S(1)}, bf16[512,128]{1,0:T(8,128)(2,1)}, u32[]{:S(2)}) copy-start(bf16[512,128]{1,0:T(8,128)(2,1)} %param.13) | copy-start | bytes 393220
  67.6 34.1 %copy-start.5 = (f32[128]{0:T(128)S(1)}, f32[128]{0:T(128)}, u32[]{:S(2)}) copy-start(f32[128]{0:T(128)} %param.14) | copy-start | bytes 1540
  79.3 23.5 %copy-start.2 = (bf16[512,128]{1,0:T(8,128)(2,1)S(1)}, bf16[512,128]{1,0:T(8,128)(2,1)}, u32[]{:S(2)}) copy-start(bf16[512,128]{1,0:T(8,128)(2,1)} %param.15) | copy-start | bytes 393220

commit v13 on v12

--- a/solution.py
+++ b/solution.py
@@ -254,7 +254,9 @@
     )(pieces)
 
 
-def block_of(col, per_owner, nz, nxy):
+def staged_index(col, per_owner):
+    nz = lax.axis_size("z")
+    nxy = lax.axis_size("x") * lax.axis_size("ylo")
     half = per_owner // 2
     owner = col // per_owner
     sub = col % per_owner
@@ -263,10 +265,10 @@
     in_first = sub < half
     first = (z * nxy + xy) * half + jnp.where(in_first, sub, 0)
     second = (xy * nz + z) * half + jnp.where(in_first, 0, sub - half)
-    return in_first, first, second
-
-
-def products_kernel(layout, col_ref, *refs):
+    return in_first.astype(jnp.int32), first, second
+
+
+def products_kernel(flag_ref, first_ref, second_ref, *refs):
     adj_ref, out_ref = refs[-2:]
     rows, kq = adj_ref.shape[0], adj_ref.shape[1]
     firsts, seconds = refs[: rows * kq], refs[rows * kq : 2 * rows * kq]
@@ -275,43 +277,40 @@
         acc = jnp.zeros(out_ref.shape[1:], jnp.float32)
         for k in range(kq):
             at = r * kq + k
-            in_first = block_of(col_ref[base + r, k], *layout)[0]
-            block = jnp.where(in_first, firsts[at][0], seconds[at][0])
+            block = jnp.where(flag_ref[base + r, k] != 0, firsts[at][0], seconds[at][0])
             acc = acc + jnp.dot(adj_ref[r, k], block, preferred_element_type=jnp.float32)
         out_ref[r] = acc
 
 
-def tile_products(panels, adj_tiles, col, per_piece):
-    rows, kq = col.shape
+def tile_products(panels, adj_tiles, index, per_piece):
+    flag, first, second = index
+    rows, kq = flag.shape
     width = panels[0].shape[2]
     tile = (1, BLOCK, width)
-    layout = (panels[0].shape[0] * 2 // lax.axis_size(BLK), lax.axis_size("z"),
-              lax.axis_size("x") * lax.axis_size("ylo"))
-
-    def pick(which, r, k):
-        return pl.BlockSpec(
-            tile, lambda g, c: (block_of(c[g * per_piece + r, k], *layout)[which], 0, 0)
-        )
-
-    specs = [pick(1, r, k) for r in range(per_piece) for k in range(kq)]
-    specs += [pick(2, r, k) for r in range(per_piece) for k in range(kq)]
-    specs.append(pl.BlockSpec((per_piece, kq, BLOCK, BLOCK), lambda g, c: (g, 0, 0, 0)))
+
+    def pick(table, r, k):
+        return pl.BlockSpec(tile, lambda g, f, a, b: (table(f, a, b)[g * per_piece + r, k], 0, 0))
+
+    specs = [pick(lambda f, a, b: a, r, k) for r in range(per_piece) for k in range(kq)]
+    specs += [pick(lambda f, a, b: b, r, k) for r in range(per_piece) for k in range(kq)]
+    specs.append(pl.BlockSpec((per_piece, kq, BLOCK, BLOCK), lambda g, f, a, b: (g, 0, 0, 0)))
+    out_spec = pl.BlockSpec((per_piece, BLOCK, width), lambda g, f, a, b: (g, 0, 0))
     summed = pl.pallas_call(
-        functools.partial(products_kernel, layout),
+        products_kernel,
         out_shape=jax.ShapeDtypeStruct((rows, BLOCK, width), jnp.float32),
         grid_spec=pltpu.PrefetchScalarGridSpec(
-            num_scalar_prefetch=1,
+            num_scalar_prefetch=3,
             grid=(rows // per_piece,),
             in_specs=specs,
-            out_specs=pl.BlockSpec((per_piece, BLOCK, width), lambda g, c: (g, 0, 0)),
+            out_specs=out_spec,
         ),
-    )(col, *([panels[0]] * (per_piece * kq)), *([panels[1]] * (per_piece * kq)), adj_tiles[:, 0])
+    )(flag, first, second, *([panels[0]] * (per_piece * kq)), *([panels[1]] * (per_piece * kq)), adj_tiles[:, 0])
     return summed.reshape(-1, width)
 
 
 def local(node_feats, adj_tiles, col_index, w_in, b_in, w_out, b_out, cot_out):
     per_piece = node_feats.shape[0] // BLOCK
-    index = col_index.reshape(col_index.shape[0], -1)
+    index = staged_index(col_index[:, 0, :], per_piece)
     panels = gather_blk(node_feats, 0)
     partial_sum = tile_products(panels, adj_tiles, index, per_piece)
     agg = reduce_rep(partial_sum, 8)

time: 202 us -> 194 us (0.960)
  Pallas kernels: 192 us -> 183 us
    pallas_call x2, Pallas kernels: 23.2 us -> 14.2 us  [tile_products(): pl.pallas_call(products_kernel, out_shape=jax.ShapeDtypeStruct((rows, BLO...]
where the time goes in v13:
time: 194 us; the launch traced here: 191 us
  Pallas kernels  183 us (94%)
  matrix products  3.53 us (2%)
  other arithmetic  2.86 us (1%)
    pallas_call x4, Pallas kernels, stage_two(): pl.pallas_call(functools.partial(stage_two_kernel, len(srcs) == 1), out_s...  129 us
    pallas_call x2, Pallas kernels, reduce_rep(): pl.pallas_call(reduce_kernel, out_shape=jax.ShapeDtypeStruct(pieces.shape...  40.3 us
    pallas_call x2, Pallas kernels, tile_products(): pl.pallas_call(products_kernel, out_shape=jax.ShapeDtypeStruct((rows, BLO...  14.2 us

profile of v13, /device:TPU:9, one launch (start us, length us, event | category | flops | bytes accessed | tf_op | source)
XLA Modules:
  0.0 191.2 jit_solution(15531304303909713452)
XLA Ops:
  0.6 0.0 copy-start
  0.6 0.8 copy.10
  1.4 0.6 fusion.15.flag_ref
  2.0 0.6 select_add_fusion
  2.7 20.2 %shard_map.95 = (bf16[8,256,128]{2,1,0:T(8,128)(2,1)}, bf16[8,256,128]{2,1,0:T(8,128)(2,1)}) custom-call(bf16[512,128]{1,0:T(8,128)(2,1)} %refs_0_.1), custom_call_target="tpu_custom_call" | custom-call | tf_op jit(solution)/shard_map/pallas_call | solution.py:185
  22.9 45.3 %shard_map.96 = (bf16[8,8,256,128]{3,2,1,0:T(8,128)(2,1)}, bf16[8,8,256,128]{3,2,1,0:T(8,128)(2,1)}) custom-call(bf16[8,256,128]{2,1,0:T(8,128)(2,1)} %get-tuple-element.10.refs_0_, bf16[8,256,128]{2,1,0:T(8,128)(2,1)} %get-tuple-element.11.refs_1_), custom_call_target="tpu_custom_call" | custom-call | tf_op jit(solution)/shard_map/pallas_call | solution.py:185
  68.2 0.0 copy-start.3
  68.2 0.0 copy-start.1
  68.2 0.0 copy-start.4
  68.2 0.0 copy-start.5
  68.2 7.2 %shard_map.97 = f32[16,128,128]{2,1,0:T(8,128)} custom-call(s32[16,4]{1,0:T(8,128)} %fusion.15.flag_ref, s32[16,4]{1,0:T(8,128)} %get-tuple-element.19.first_ref, s32[16,4]{1,0:T(8,128)} %get-tuple-element.18.second_ref, bf16[128,128,128]{2,1,0:T(8,128)(2,1)} %bitcast.45, bf16[128,128,128]{2,1,0:T(8,128)(2,1)} %bitcast.46, bf16[128,128,128]{2,1,0:T(8,128)(2,1)} %bitcast.47, ...), custom_call_target="tpu_custom_call" | custom-call | tf_op jit(solution)/shard_map/pallas_call | solution.py:298
  75.4 0.0 copy-start.2
  75.4 21.1 %shard_map.98 = f32[512,128]{1,0:T(8,128)} custom-call(f32[4,512,128]{2,1,0:T(8,128)} %bitcast.80), custom_call_target="tpu_custom_call" | custom-call | tf_op jit(solution)/shard_map/pallas_call | solution.py:242
  96.5 0.0 copy-done
  96.5 0.0 copy-done.3
  96.6 1.2 convolution_add_fusion
  97.8 0.0 copy-done.1
  97.8 1.1 fusion.5
  98.9 1.2 fusion.4.refs_0_
  100.1 16.0 %shard_map.99 = (bf16[8,256,128]{2,1,0:T(8,128)(2,1)}, bf16[8,256,128]{2,1,0:T(8,128)(2,1)}) custom-call(bf16[512,128]{1,0:T(8,128)(2,1)} %fusion.4.refs_0_), custom_call_target="tpu_custom_call" | custom-call | tf_op jit(solution)/shard_map/pallas_call | solution.py:185
  116.1 47.2 %shard_map.100 = (bf16[8,8,256,128]{3,2,1,0:T(8,128)(2,1)}, bf16[8,8,256,128]{3,2,1,0:T(8,128)(2,1)}) custom-call(bf16[8,256,128]{2,1,0:T(8,128)(2,1)} %get-tuple-element.14.refs_0_, bf16[8,256,128]{2,1,0:T(8,128)(2,1)} %get-tuple-element.15.refs_1_), custom_call_target="tpu_custom_call" | custom-call | tf_op jit(solution)/shard_map/pallas_call | solution.py:185
  163.3 7.0 %shard_map.101 = f32[16,128,128]{2,1,0:T(8,128)} custom-call(s32[16,4]{1,0:T(8,128)} %fusion.15.flag_ref, s32[16,4]{1,0:T(8,128)} %get-tuple-element.19.first_ref, s32[16,4]{1,0:T(8,128)} %get-tuple-element.18.second_ref, bf16[128,128,128]{2,1,0:T(8,128)(2,1)} %bitcast.13, bf16[128,128,128]{2,1,0:T(8,128)(2,1)} %bitcast.14, bf16[128,128,128]{2,1,0:T(8,128)(2,1)} %bitcast.15, ...), custom_call_target="tpu_custom_call" | custom-call | tf_op jit(solution)/shard_map/pallas_call | solution.py:298
  170.4 19.2 %shard_map.102 = f32[512,128]{1,0:T(8,128)} custom-call(f32[4,512,128]{2,1,0:T(8,128)} %bitcast.79), custom_call_target="tpu_custom_call" | custom-call | tf_op jit(solution)/shard_map/pallas_call | solution.py:242
  189.6 1.6 add_convert_fusion
  (3 shorter events, 0.0 us)
Async XLA Ops:
  0.6 95.9 %copy-start = (bf16[128,512]{1,0:T(8,128)(2,1)S(1)}, bf16[128,512]{1,0:T(8,128)(2,1)}, u32[]{:S(2)}) copy-start(bf16[128,512]{1,0:T(8,128)(2,1)} %param.11) | copy-start | bytes 393220
  68.2 28.4 %copy-start.3 = (f32[512]{0:T(512)S(1)}, f32[512]{0:T(512)}, u32[]{:S(2)}) copy-start(f32[512]{0:T(512)} %param.12) | copy-start | bytes 6148
  68.2 29.6 %copy-start.1 = (bf16[512,128]{1,0:T(8,128)(2,1)S(1)}, bf16[512,128]{1,0:T(8,128)(2,1)}, u32[]{:S(2)}) copy-start(bf16[512,128]{1,0:T(8,128)(2,1)} %refs_0_.1) | copy-start | bytes 393220
  68.2 29.6 %copy-start.4 = (bf16[512,128]{1,0:T(8,128)(2,1)S(1)}, bf16[512,128]{1,0:T(8,128)(2,1)}, u32[]{:S(2)}) copy-start(bf16[512,128]{1,0:T(8,128)(2,1)} %param.13) | copy-start | bytes 393220
  68.2 29.6 %copy-start.5 = (f32[128]{0:T(128)S(1)}, f32[128]{0:T(128)}, u32[]{:S(2)}) copy-start(f32[128]{0:T(128)} %param.14) | copy-start | bytes 1540
  75.4 23.5 %copy-start.2 = (bf16[512,128]{1,0:T(8,128)(2,1)S(1)}, bf16[512,128]{1,0:T(8,128)(2,1)}, u32[]{:S(2)}) copy-start(bf16[512,128]{1,0:T(8,128)(2,1)} %param.15) | copy-start | bytes 393220

commit v14 on v13

--- a/solution.py
+++ b/solution.py
@@ -30,106 +30,35 @@
     return coords
 
 
-def exchange_kernel(jobs, *refs):
-    count = len(jobs)
-    src_refs, out_refs = refs[:count], refs[count : 2 * count]
-    send_sem, recv_sem, local_sem = refs[2 * count :]
-    places = [group_place(axes) for axes, _ in jobs]
-    barrier = pltpu.get_barrier_semaphore()
-    total = 0
-    for (axes, _), (me, sizes), out_ref in zip(jobs, places, out_refs):
-        n = out_ref.shape[0]
-        total += n - 1
-        for d in range(1, n):
-            p = lax.rem(me + d, n)
-            pl.semaphore_signal(barrier, 1, device_id=peer_id(axes, sizes, p))
-    pl.semaphore_wait(barrier, total)
-    copies = []
-    for j, ((axes, gather), (me, sizes)) in enumerate(zip(jobs, places)):
-        src_ref, out_ref = src_refs[j], out_refs[j]
-        n = out_ref.shape[0]
-        for d in range(1, n):
-            p = lax.rem(me + d, n)
-            copy = pltpu.make_async_remote_copy(
-                src_ref=src_ref if gather else src_ref.at[p],
-                dst_ref=out_ref.at[me],
-                send_sem=send_sem.at[j, d],
-                recv_sem=recv_sem.at[j, d],
-                device_id=peer_id(axes, sizes, p),
-            )
-            copy.start()
-            copies.append(copy)
-        own = pltpu.make_async_copy(
-            src_ref if gather else src_ref.at[me], out_ref.at[me], local_sem.at[j]
-        )
-        own.start()
-        copies.append(own)
-    for copy in copies:
-        copy.wait()
-
-
-def group_exchange(srcs, jobs, cid):
-    shapes = []
-    most = 1
-    for src, (axes, gather) in zip(srcs, jobs):
-        n = 1
-        for a in axes:
-            n *= lax.axis_size(a)
-        most = max(most, n)
-        block = src.shape if gather else src.shape[1:]
-        shapes.append(jax.ShapeDtypeStruct((n, *block), src.dtype))
-    count = len(jobs)
-    return pl.pallas_call(
-        functools.partial(exchange_kernel, tuple(jobs)),
-        out_shape=tuple(shapes),
-        in_specs=[pl.BlockSpec(memory_space=pl.ANY)] * count,
-        out_specs=tuple([pl.BlockSpec(memory_space=pl.ANY)] * count),
-        scratch_shapes=[
-            pltpu.SemaphoreType.DMA((count, most)),
-            pltpu.SemaphoreType.DMA((count, most)),
-            pltpu.SemaphoreType.DMA((count,)),
-        ],
-        compiler_params=pltpu.CompilerParams(collective_id=cid, has_side_effects=True),
-    )(*srcs)
-
-
-def stage_two_kernel(halves, *refs):
-    if halves:
-        rows_ref = refs[0]
-        half = rows_ref.shape[0] // 2
-        ring_src, tree_src = rows_ref.at[pl.ds(half, half)], rows_ref.at[pl.ds(0, half)]
-        refs = refs[1:]
-    else:
-        ring_src, tree_src = refs[:2]
-        refs = refs[2:]
-    ring_out, tree_out, send_sem, recv_sem, local_sem = refs
-    stage_two_body(ring_src, tree_src, ring_out, tree_out, send_sem, recv_sem, local_sem)
-
-
-def stage_two_body(ring_src, tree_src, ring_out, tree_out, send_sem, recv_sem, local_sem):
+def neighbours():
     nx, ny, nz = lax.axis_size("x"), lax.axis_size("ylo"), lax.axis_size("z")
     x, y, z = lax.axis_index("x"), lax.axis_index("ylo"), lax.axis_index("z")
     right, left, other = lax.rem(x + 1, nx), lax.rem(x + nx - 1, nx), ny - 1 - y
-    to_right, to_left, to_other = {"x": right}, {"x": left}, {"ylo": other}
-    up, down = {"z": lax.rem(z + 1, nz)}, {"z": lax.rem(z + nz - 1, nz)}
-    barrier = pltpu.get_barrier_semaphore()
-    for peer in (to_right, to_left, to_other, up, down):
-        pl.semaphore_signal(barrier, 1, device_id=peer)
-    pl.semaphore_wait(barrier, 5)
+    return {"x": right}, {"x": left}, {"ylo": other}, {"z": lax.rem(z + 1, nz)}, {"z": lax.rem(z + nz - 1, nz)}
+
+
+def gather_phase(phase, ring_src, tree_src, ring_out, tree_out, send_sem, recv_sem, local_sem):
+    nx, ny, nz = lax.axis_size("x"), lax.axis_size("ylo"), lax.axis_size("z")
+    x, y, z = lax.axis_index("x"), lax.axis_index("ylo"), lax.axis_index("z")
+    left, other = lax.rem(x + nx - 1, nx), ny - 1 - y
+    to_right, to_left, to_other, up, down = neighbours()
 
     def send(kind, src, dst, peer):
         copy = pltpu.make_async_remote_copy(
-            src_ref=src, dst_ref=dst, send_sem=send_sem.at[kind], recv_sem=recv_sem.at[kind], device_id=peer
+            src_ref=src,
+            dst_ref=dst,
+            send_sem=send_sem.at[phase, kind],
+            recv_sem=recv_sem.at[phase, kind],
+            device_id=peer,
         )
         copy.start()
         return copy
 
     me = x * ny + y
-    own_tree = pltpu.make_async_copy(tree_src, tree_out.at[me], local_sem.at[0])
+    own_tree = pltpu.make_async_copy(tree_src, tree_out.at[me], local_sem.at[phase, 0])
     own_tree.start()
-    own_ring = pltpu.make_async_copy(ring_src, ring_out.at[z], local_sem.at[1])
+    own_ring = pltpu.make_async_copy(ring_src, ring_out.at[z], local_sem.at[phase, 1])
     own_ring.start()
-    sent = []
     first_right = send(0, tree_src, tree_out.at[me], to_right)
     first_left = send(1, tree_src, tree_out.at[me], to_left)
     first_other = send(2, tree_src, tree_out.at[me], to_other)
@@ -167,42 +96,51 @@
     for copy in (first_left, second_right, other_left, third_right, ups[-1], downs[-1]):
         copy.wait_recv()
     tree = [first_right, first_left, first_other, second_right, other_right, other_left, third_right]
-    for copy in tree + ups + downs:
+    return tree + ups + downs, [own_tree, own_ring]
+
+
+def gather_kernel(rows_ref, mid_ring, mid_tree, ring_out, tree_out, send_sem, recv_sem, local_sem):
+    barrier = pltpu.get_barrier_semaphore()
+    peers = neighbours()
+    for peer in peers:
+        pl.semaphore_signal(barrier, 1, device_id=peer)
+    pl.semaphore_wait(barrier, len(peers))
+    half = rows_ref.shape[0] // 2
+    ring_src, tree_src = rows_ref.at[pl.ds(half, half)], rows_ref.at[pl.ds(0, half)]
+    sends, local = gather_phase(0, ring_src, tree_src, mid_ring, mid_tree, send_sem, recv_sem, local_sem)
+    for copy in local:
+        copy.wait()
+    more, local = gather_phase(1, mid_tree, mid_ring, ring_out, tree_out, send_sem, recv_sem, local_sem)
+    for copy in sends + more:
         copy.wait_send()
-    own_tree.wait()
-    own_ring.wait()
-
-
-def stage_two(srcs, cid):
+    for copy in local:
+        copy.wait()
+
+
+def gather_blk(rows, cid):
     nz = lax.axis_size("z")
     nxy = lax.axis_size("x") * lax.axis_size("ylo")
-    if len(srcs) == 1:
-        half = srcs[0].shape[0] // 2
-        ring_shape = tree_shape = (half, *srcs[0].shape[1:])
-    else:
-        ring_shape, tree_shape = srcs[0].shape, srcs[1].shape
-    dtype = srcs[0].dtype
-    return pl.pallas_call(
-        functools.partial(stage_two_kernel, len(srcs) == 1),
+    half = rows.shape[0] // 2
+    width = rows.shape[1]
+    piece = (half, width)
+    any_space = pl.BlockSpec(memory_space=pl.ANY)
+    _, _, first, second = pl.pallas_call(
+        gather_kernel,
         out_shape=(
-            jax.ShapeDtypeStruct((nz, *ring_shape), dtype),
-            jax.ShapeDtypeStruct((nxy, *tree_shape), dtype),
+            jax.ShapeDtypeStruct((nz, *piece), rows.dtype),
+            jax.ShapeDtypeStruct((nxy, *piece), rows.dtype),
+            jax.ShapeDtypeStruct((nz, nxy, *piece), rows.dtype),
+            jax.ShapeDtypeStruct((nxy, nz, *piece), rows.dtype),
         ),
-        in_specs=[pl.BlockSpec(memory_space=pl.ANY)] * len(srcs),
-        out_specs=(pl.BlockSpec(memory_space=pl.ANY), pl.BlockSpec(memory_space=pl.ANY)),
+        in_specs=[any_space],
+        out_specs=(any_space,) * 4,
         scratch_shapes=[
-            pltpu.SemaphoreType.DMA((7 + nz,)),
-            pltpu.SemaphoreType.DMA((7 + nz,)),
-            pltpu.SemaphoreType.DMA((2,)),
+            pltpu.SemaphoreType.DMA((2, 7 + nz)),
+            pltpu.SemaphoreType.DMA((2, 7 + nz)),
+            pltpu.SemaphoreType.DMA((2, 2)),
         ],
         compiler_params=pltpu.CompilerParams(collective_id=cid, has_side_effects=True),
-    )(*srcs)
-
-
-def gather_blk(rows, cid):
-    second, first = stage_two((rows,), cid)
-    first, second = stage_two((first, second), cid + 4)
-    width = rows.shape[1]
+    )(rows)
     return first.reshape(-1, BLOCK, width), second.reshape(-1, BLOCK, width)
 
 

time: 194 us -> 192 us (0.990)
  Pallas kernels: 183 us -> 180 us
    pallas_call x4 -> x2, Pallas kernels: 129 us -> 123 us  [gather_blk(): pl.pallas_call(gather_kernel, out_shape=(jax.ShapeDtypeStruct((nz, *piece...]
    pallas_call x2, Pallas kernels: 40.3 us -> 43 us  [reduce_rep(): pl.pallas_call(reduce_kernel, out_shape=jax.ShapeDtypeStruct(pieces.shape...]
where the time goes in v14:
time: 192 us; the launch traced here: 188 us
  Pallas kernels  180 us (94%)
  matrix products  3.53 us (2%)
  other arithmetic  2.86 us (1%)
    pallas_call x2, Pallas kernels, gather_blk(): pl.pallas_call(gather_kernel, out_shape=(jax.ShapeDtypeStruct((nz, *piece...  123 us
    pallas_call x2, Pallas kernels, reduce_rep(): pl.pallas_call(reduce_kernel, out_shape=jax.ShapeDtypeStruct(pieces.shape...  43 us
    pallas_call x2, Pallas kernels, tile_products(): pl.pallas_call(products_kernel, out_shape=jax.ShapeDtypeStruct((rows, BLO...  14.2 us

profile of v14, /device:TPU:9, one launch (start us, length us, event | category | flops | bytes accessed | tf_op | source)
XLA Modules:
  0.0 188.1 jit_solution(15480451113704587903)
XLA Ops:
  0.6 0.0 copy-start
  0.6 0.8 copy.10
  1.4 0.6 fusion.15.flag_ref
  2.0 0.6 select_add_fusion
  2.7 62.2 %shard_map.95 = (bf16[8,256,128]{2,1,0:T(8,128)(2,1)}, bf16[8,256,128]{2,1,0:T(8,128)(2,1)}, bf16[8,8,256,128]{3,2,1,0:T(8,128)(2,1)}, bf16[8,8,256,128]{3,2,1,0:T(8,128)(2,1)}) custom-call(bf16[512,128]{1,0:T(8,128)(2,1)} %rows_ref.1), custom_call_target="tpu_custom_call" | custom-call | tf_op jit(solution)/shard_map/pallas_call | solution.py:127
  64.9 0.0 copy-start.3
  64.9 0.0 copy-start.1
  64.9 0.0 copy-start.4
  64.9 0.0 copy-start.5
  64.9 7.1 %shard_map.96 = f32[16,128,128]{2,1,0:T(8,128)} custom-call(s32[16,4]{1,0:T(8,128)} %fusion.15.flag_ref, s32[16,4]{1,0:T(8,128)} %get-tuple-element.11.first_ref, s32[16,4]{1,0:T(8,128)} %get-tuple-element.10.second_ref, bf16[128,128,128]{2,1,0:T(8,128)(2,1)} %bitcast.45, bf16[128,128,128]{2,1,0:T(8,128)(2,1)} %bitcast.46, bf16[128,128,128]{2,1,0:T(8,128)(2,1)} %bitcast.47, ...), custom_call_target="tpu_custom_call" | custom-call | tf_op jit(solution)/shard_map/pallas_call | solution.py:236
  72.1 0.0 copy-start.2
  72.1 23.5 %shard_map.97 = f32[512,128]{1,0:T(8,128)} custom-call(f32[4,512,128]{2,1,0:T(8,128)} %bitcast.80), custom_call_target="tpu_custom_call" | custom-call | tf_op jit(solution)/shard_map/pallas_call | solution.py:180
  95.6 0.0 copy-done
  95.6 0.0 copy-done.3
  95.6 1.2 convolution_add_fusion
  96.9 0.0 copy-done.1
  96.9 0.0 copy-done.4
  96.9 0.0 copy-done.5
  96.9 1.1 fusion.5
  98.0 1.2 fusion.4.rows_ref
  99.2 60.7 %shard_map.98 = (bf16[8,256,128]{2,1,0:T(8,128)(2,1)}, bf16[8,256,128]{2,1,0:T(8,128)(2,1)}, bf16[8,8,256,128]{3,2,1,0:T(8,128)(2,1)}, bf16[8,8,256,128]{3,2,1,0:T(8,128)(2,1)}) custom-call(bf16[512,128]{1,0:T(8,128)(2,1)} %fusion.4.rows_ref), custom_call_target="tpu_custom_call" | custom-call | tf_op jit(solution)/shard_map/pallas_call | solution.py:127
  159.9 7.0 %shard_map.99 = f32[16,128,128]{2,1,0:T(8,128)} custom-call(s32[16,4]{1,0:T(8,128)} %fusion.15.flag_ref, s32[16,4]{1,0:T(8,128)} %get-tuple-element.11.first_ref, s32[16,4]{1,0:T(8,128)} %get-tuple-element.10.second_ref, bf16[128,128,128]{2,1,0:T(8,128)(2,1)} %bitcast.13, bf16[128,128,128]{2,1,0:T(8,128)(2,1)} %bitcast.14, bf16[128,128,128]{2,1,0:T(8,128)(2,1)} %bitcast.15, ...), custom_call_target="tpu_custom_call" | custom-call | tf_op jit(solution)/shard_map/pallas_call | solution.py:236
  166.9 19.5 %shard_map.100 = f32[512,128]{1,0:T(8,128)} custom-call(f32[4,512,128]{2,1,0:T(8,128)} %bitcast.79), custom_call_target="tpu_custom_call" | custom-call | tf_op jit(solution)/shard_map/pallas_call | solution.py:180
  186.5 1.6 add_convert_fusion
  (1 shorter events, 0.0 us)
Async XLA Ops:
  0.6 95.0 %copy-start = (bf16[128,512]{1,0:T(8,128)(2,1)S(1)}, bf16[128,512]{1,0:T(8,128)(2,1)}, u32[]{:S(2)}) copy-start(bf16[128,512]{1,0:T(8,128)(2,1)} %param.11) | copy-start | bytes 393220
  64.9 30.8 %copy-start.3 = (f32[512]{0:T(512)S(1)}, f32[512]{0:T(512)}, u32[]{:S(2)}) copy-start(f32[512]{0:T(512)} %param.12) | copy-start | bytes 6148
  64.9 32.0 %copy-start.1 = (bf16[512,128]{1,0:T(8,128)(2,1)S(1)}, bf16[512,128]{1,0:T(8,128)(2,1)}, u32[]{:S(2)}) copy-start(bf16[512,128]{1,0:T(8,128)(2,1)} %rows_ref.1) | copy-start | bytes 393220
  64.9 32.0 %copy-start.4 = (bf16[512,128]{1,0:T(8,128)(2,1)S(1)}, bf16[512,128]{1,0:T(8,128)(2,1)}, u32[]{:S(2)}) copy-start(bf16[512,128]{1,0:T(8,128)(2,1)} %param.13) | copy-start | bytes 393220
  64.9 32.0 %copy-start.5 = (f32[128]{0:T(128)S(1)}, f32[128]{0:T(128)}, u32[]{:S(2)}) copy-start(f32[128]{0:T(128)} %param.14) | copy-start | bytes 1540
  72.1 25.9 %copy-start.2 = (bf16[512,128]{1,0:T(8,128)(2,1)S(1)}, bf16[512,128]{1,0:T(8,128)(2,1)}, u32[]{:S(2)}) copy-start(bf16[512,128]{1,0:T(8,128)(2,1)} %param.15) | copy-start | bytes 393220

commit v15 on v14

--- a/solution.py
+++ b/solution.py
@@ -250,7 +250,7 @@
     per_piece = node_feats.shape[0] // BLOCK
     index = staged_index(col_index[:, 0, :], per_piece)
     panels = gather_blk(node_feats, 0)
-    partial_sum = tile_products(panels, adj_tiles, index, per_piece)
+    partial_sum = tile_products(panels, adj_tiles, index, 2 * per_piece)
     agg = reduce_rep(partial_sum, 8)
     agg_b = agg.astype(jnp.bfloat16)
     pre = jnp.dot(agg_b, w_in, preferred_element_type=jnp.float32) + b_in
@@ -264,7 +264,7 @@
         jnp.bfloat16
     )
     g_panels = gather_blk(g_agg, 1)
-    back_partial = tile_products(g_panels, adj_tiles, index, per_piece)
+    back_partial = tile_products(g_panels, adj_tiles, index, 2 * per_piece)
     back_rows = reduce_rep(back_partial, 9)
     grad_feats = (cot_out.astype(jnp.float32) + back_rows).astype(jnp.bfloat16)
     return (out_feats, grad_feats)

time: 192 us -> 191 us (level)
  no operation moved by 1% of the time
where the time goes in v15:
time: 191 us; the launch traced here: 188 us
  Pallas kernels  180 us (94%)
  matrix products  3.53 us (2%)
  other arithmetic  2.86 us (1%)
    pallas_call x2, Pallas kernels, gather_blk(): pl.pallas_call(gather_kernel, out_shape=(jax.ShapeDtypeStruct((nz, *piece...  123 us
    pallas_call x2, Pallas kernels, reduce_rep(): pl.pallas_call(reduce_kernel, out_shape=jax.ShapeDtypeStruct(pieces.shape...  42.9 us
    pallas_call x2, Pallas kernels, tile_products(): pl.pallas_call(products_kernel, out_shape=jax.ShapeDtypeStruct((rows, BLO...  13.2 us

profile of v15, /device:TPU:9, one launch (start us, length us, event | category | flops | bytes accessed | tf_op | source)
XLA Modules:
  0.0 187.5 jit_solution(8101700472483987325)
XLA Ops:
  0.6 0.0 copy-start
  0.6 0.8 copy.10
  1.4 0.6 fusion.15.flag_ref
  2.0 0.6 select_add_fusion
  2.7 62.2 %shard_map.95 = (bf16[8,256,128]{2,1,0:T(8,128)(2,1)}, bf16[8,256,128]{2,1,0:T(8,128)(2,1)}, bf16[8,8,256,128]{3,2,1,0:T(8,128)(2,1)}, bf16[8,8,256,128]{3,2,1,0:T(8,128)(2,1)}) custom-call(bf16[512,128]{1,0:T(8,128)(2,1)} %rows_ref.1), custom_call_target="tpu_custom_call" | custom-call | tf_op jit(solution)/shard_map/pallas_call | solution.py:127
  64.9 0.0 copy-start.3
  64.9 0.0 copy-start.1
  64.9 0.0 copy-start.4
  64.9 0.0 copy-start.5
  64.9 6.6 %shard_map.96 = f32[16,128,128]{2,1,0:T(8,128)} custom-call(s32[16,4]{1,0:T(8,128)} %fusion.15.flag_ref, s32[16,4]{1,0:T(8,128)} %get-tuple-element.11.first_ref, s32[16,4]{1,0:T(8,128)} %get-tuple-element.10.second_ref, bf16[128,128,128]{2,1,0:T(8,128)(2,1)} %bitcast.92, bf16[128,128,128]{2,1,0:T(8,128)(2,1)} %bitcast.108, bf16[128,128,128]{2,1,0:T(8,128)(2,1)} %bitcast.79, ...), custom_call_target="tpu_custom_call" | custom-call | tf_op jit(solution)/shard_map/pallas_call | solution.py:236
  71.5 0.0 copy-start.2
  71.5 23.5 %shard_map.97 = f32[512,128]{1,0:T(8,128)} custom-call(f32[4,512,128]{2,1,0:T(8,128)} %bitcast.144), custom_call_target="tpu_custom_call" | custom-call | tf_op jit(solution)/shard_map/pallas_call | solution.py:180
  95.1 0.0 copy-done
  95.1 0.0 copy-done.3
  95.1 1.2 convolution_add_fusion
  96.3 0.0 copy-done.1
  96.3 0.0 copy-done.4
  96.3 1.1 fusion.5
  97.4 0.0 copy-done.2
  97.4 1.2 fusion.4.rows_ref
  98.6 61.3 %shard_map.98 = (bf16[8,256,128]{2,1,0:T(8,128)(2,1)}, bf16[8,256,128]{2,1,0:T(8,128)(2,1)}, bf16[8,8,256,128]{3,2,1,0:T(8,128)(2,1)}, bf16[8,8,256,128]{3,2,1,0:T(8,128)(2,1)}) custom-call(bf16[512,128]{1,0:T(8,128)(2,1)} %fusion.4.rows_ref), custom_call_target="tpu_custom_call" | custom-call | tf_op jit(solution)/shard_map/pallas_call | solution.py:127
  159.9 6.6 %shard_map.99 = f32[16,128,128]{2,1,0:T(8,128)} custom-call(s32[16,4]{1,0:T(8,128)} %fusion.15.flag_ref, s32[16,4]{1,0:T(8,128)} %get-tuple-element.11.first_ref, s32[16,4]{1,0:T(8,128)} %get-tuple-element.10.second_ref, bf16[128,128,128]{2,1,0:T(8,128)(2,1)} %bitcast.28, bf16[128,128,128]{2,1,0:T(8,128)(2,1)} %bitcast.44, bf16[128,128,128]{2,1,0:T(8,128)(2,1)} %bitcast.15, ...), custom_call_target="tpu_custom_call" | custom-call | tf_op jit(solution)/shard_map/pallas_call | solution.py:236
  166.5 19.4 %shard_map.100 = f32[512,128]{1,0:T(8,128)} custom-call(f32[4,512,128]{2,1,0:T(8,128)} %bitcast.143), custom_call_target="tpu_custom_call" | custom-call | tf_op jit(solution)/shard_map/pallas_call | solution.py:180
  185.9 1.6 add_convert_fusion
  (1 shorter events, 0.0 us)
Async XLA Ops:
  0.6 94.4 %copy-start = (bf16[128,512]{1,0:T(8,128)(2,1)S(1)}, bf16[128,512]{1,0:T(8,128)(2,1)}, u32[]{:S(2)}) copy-start(bf16[128,512]{1,0:T(8,128)(2,1)} %param.11) | copy-start | bytes 393220
  64.9 30.2 %copy-start.3 = (f32[512]{0:T(512)S(1)}, f32[512]{0:T(512)}, u32[]{:S(2)}) copy-start(f32[512]{0:T(512)} %param.12) | copy-start | bytes 6148
  64.9 31.4 %copy-start.1 = (bf16[512,128]{1,0:T(8,128)(2,1)S(1)}, bf16[512,128]{1,0:T(8,128)(2,1)}, u32[]{:S(2)}) copy-start(bf16[512,128]{1,0:T(8,128)(2,1)} %rows_ref.1) | copy-start | bytes 393220
  64.9 31.4 %copy-start.4 = (bf16[512,128]{1,0:T(8,128)(2,1)S(1)}, bf16[512,128]{1,0:T(8,128)(2,1)}, u32[]{:S(2)}) copy-start(bf16[512,128]{1,0:T(8,128)(2,1)} %param.13) | copy-start | bytes 393220
  64.9 31.4 %copy-start.5 = (f32[128]{0:T(128)S(1)}, f32[128]{0:T(128)}, u32[]{:S(2)}) copy-start(f32[128]{0:T(128)} %param.14) | copy-start | bytes 1540
  71.5 25.9 %copy-start.2 = (bf16[512,128]{1,0:T(8,128)(2,1)S(1)}, bf16[512,128]{1,0:T(8,128)(2,1)}, u32[]{:S(2)}) copy-start(bf16[512,128]{1,0:T(8,128)(2,1)} %param.15) | copy-start | bytes 393220

commit v16 on v15

--- a/solution.py
+++ b/solution.py
@@ -99,15 +99,63 @@
     return tree + ups + downs, [own_tree, own_ring]
 
 
+def phase_one(ring_src, tree_src, ring_out, tree_out, send_sem, recv_sem, local_sem):
+    nx, ny, nz = lax.axis_size("x"), lax.axis_size("ylo"), lax.axis_size("z")
+    x, y, z = lax.axis_index("x"), lax.axis_index("ylo"), lax.axis_index("z")
+
+    def send(kind, src, dst, peer):
+        copy = pltpu.make_async_remote_copy(
+            src_ref=src, dst_ref=dst, send_sem=send_sem.at[0, kind], recv_sem=recv_sem.at[0, kind], device_id=peer
+        )
+        copy.start()
+        return copy
+
+    def on_z(step):
+        return {"z": lax.rem(z + nz + step, nz)}
+
+    me = x * ny + y
+    own_tree = pltpu.make_async_copy(tree_src, tree_out.at[me], local_sem.at[0, 0])
+    own_tree.start()
+    own_ring = pltpu.make_async_copy(ring_src, ring_out.at[z], local_sem.at[0, 1])
+    own_ring.start()
+    n = nx * ny
+    sends = []
+    for d in range(1, n):
+        p = lax.rem(me + d, n)
+        sends.append(send(d - 1, tree_src, tree_out.at[me], {"x": p // ny, "ylo": p % ny}))
+    kind = n - 1
+    up_one = send(kind, ring_src, ring_out.at[z], on_z(1))
+    down_one = send(kind + 1, ring_src, ring_out.at[z], on_z(-1))
+    up_two = send(kind + 2, ring_src, ring_out.at[z], on_z(2))
+    down_two = send(kind + 3, ring_src, ring_out.at[z], on_z(-2))
+    split = ring_src.shape[0] // 2
+    up_two.wait_recv()
+    below = lax.rem(z + nz - 2, nz)
+    fwd_up_one = send(kind + 4, ring_out.at[below], ring_out.at[below], on_z(1))
+    fwd_up_two = send(kind + 5, ring_out.at[below, :split], ring_out.at[below, :split], on_z(2))
+    down_two.wait_recv()
+    above = lax.rem(z + 2, nz)
+    fwd_down_one = send(kind + 6, ring_out.at[above], ring_out.at[above], on_z(-1))
+    fwd_down_two = send(kind + 7, ring_out.at[above, split:], ring_out.at[above, split:], on_z(-2))
+    ring = [up_one, down_one, up_two, down_two, fwd_up_one, fwd_up_two, fwd_down_one, fwd_down_two]
+    for copy in sends + [up_one, down_one, fwd_up_one, fwd_up_two, fwd_down_one, fwd_down_two]:
+        copy.wait_recv()
+    return sends + ring, [own_tree, own_ring]
+
+
 def gather_kernel(rows_ref, mid_ring, mid_tree, ring_out, tree_out, send_sem, recv_sem, local_sem):
+    nx, ny, nz = lax.axis_size("x"), lax.axis_size("ylo"), lax.axis_size("z")
+    x, y, z = lax.axis_index("x"), lax.axis_index("ylo"), lax.axis_index("z")
+    me = x * ny + y
+    peers = [{"x": lax.rem(me + d, nx * ny) // ny, "ylo": lax.rem(me + d, nx * ny) % ny} for d in range(1, nx * ny)]
+    peers += [{"z": lax.rem(z + nz + step, nz)} for step in (1, -1, 2, -2)]
     barrier = pltpu.get_barrier_semaphore()
-    peers = neighbours()
     for peer in peers:
         pl.semaphore_signal(barrier, 1, device_id=peer)
     pl.semaphore_wait(barrier, len(peers))
     half = rows_ref.shape[0] // 2
     ring_src, tree_src = rows_ref.at[pl.ds(half, half)], rows_ref.at[pl.ds(0, half)]
-    sends, local = gather_phase(0, ring_src, tree_src, mid_ring, mid_tree, send_sem, recv_sem, local_sem)
+    sends, local = phase_one(ring_src, tree_src, mid_ring, mid_tree, send_sem, recv_sem, local_sem)
     for copy in local:
         copy.wait()
     more, local = gather_phase(1, mid_tree, mid_ring, ring_out, tree_out, send_sem, recv_sem, local_sem)

time: 191 us -> 186 us (0.974)
  Pallas kernels: 180 us -> 175 us
    pallas_call x2, Pallas kernels: 42.9 us -> 39.9 us  [reduce_rep(): pl.pallas_call(reduce_kernel, out_shape=jax.ShapeDtypeStruct(pieces.shape...]
where the time goes in v16:
time: 186 us; the launch traced here: 183 us
  Pallas kernels  175 us (94%)
  matrix products  3.54 us (2%)
  other arithmetic  2.86 us (2%)
    pallas_call x2, Pallas kernels, gather_blk(): pl.pallas_call(gather_kernel, out_shape=(jax.ShapeDtypeStruct((nz, *piece...  122 us
    pallas_call x2, Pallas kernels, reduce_rep(): pl.pallas_call(reduce_kernel, out_shape=jax.ShapeDtypeStruct(pieces.shape...  39.9 us
    pallas_call x2, Pallas kernels, tile_products(): pl.pallas_call(products_kernel, out_shape=jax.ShapeDtypeStruct((rows, BLO...  13.2 us

profile of v16, /device:TPU:9, one launch (start us, length us, event | category | flops | bytes accessed | tf_op | source)
XLA Modules:
  0.0 183.1 jit_solution(1324559203902277025)
XLA Ops:
  0.6 0.0 copy-start
  0.6 0.8 copy.10
  1.4 0.6 fusion.15.flag_ref
  2.0 0.6 select_add_fusion
  2.7 60.1 %shard_map.95 = (bf16[8,256,128]{2,1,0:T(8,128)(2,1)}, bf16[8,256,128]{2,1,0:T(8,128)(2,1)}, bf16[8,8,256,128]{3,2,1,0:T(8,128)(2,1)}, bf16[8,8,256,128]{3,2,1,0:T(8,128)(2,1)}) custom-call(bf16[512,128]{1,0:T(8,128)(2,1)} %rows_ref.1), custom_call_target="tpu_custom_call" | custom-call | tf_op jit(solution)/shard_map/pallas_call | solution.py:175
  62.8 0.0 copy-start.3
  62.8 0.0 copy-start.1
  62.8 0.0 copy-start.4
  62.8 0.0 copy-start.5
  62.8 6.6 %shard_map.96 = f32[16,128,128]{2,1,0:T(8,128)} custom-call(s32[16,4]{1,0:T(8,128)} %fusion.15.flag_ref, s32[16,4]{1,0:T(8,128)} %get-tuple-element.11.first_ref, s32[16,4]{1,0:T(8,128)} %get-tuple-element.10.second_ref, bf16[128,128,128]{2,1,0:T(8,128)(2,1)} %bitcast.92, bf16[128,128,128]{2,1,0:T(8,128)(2,1)} %bitcast.108, bf16[128,128,128]{2,1,0:T(8,128)(2,1)} %bitcast.79, ...), custom_call_target="tpu_custom_call" | custom-call | tf_op jit(solution)/shard_map/pallas_call | solution.py:284
  69.4 0.0 copy-start.2
  69.4 20.6 %shard_map.97 = f32[512,128]{1,0:T(8,128)} custom-call(f32[4,512,128]{2,1,0:T(8,128)} %bitcast.144), custom_call_target="tpu_custom_call" | custom-call | tf_op jit(solution)/shard_map/pallas_call | solution.py:228
  90.1 0.0 copy-done
  90.1 0.0 copy-done.3
  90.1 1.2 convolution_add_fusion
  91.3 0.0 copy-done.1
  91.3 0.0 copy-done.4
  91.3 1.1 fusion.5
  92.4 0.0 copy-done.2
  92.4 1.2 fusion.4.rows_ref
  93.7 61.9 %shard_map.98 = (bf16[8,256,128]{2,1,0:T(8,128)(2,1)}, bf16[8,256,128]{2,1,0:T(8,128)(2,1)}, bf16[8,8,256,128]{3,2,1,0:T(8,128)(2,1)}, bf16[8,8,256,128]{3,2,1,0:T(8,128)(2,1)}) custom-call(bf16[512,128]{1,0:T(8,128)(2,1)} %fusion.4.rows_ref), custom_call_target="tpu_custom_call" | custom-call | tf_op jit(solution)/shard_map/pallas_call | solution.py:175
  155.6 6.6 %shard_map.99 = f32[16,128,128]{2,1,0:T(8,128)} custom-call(s32[16,4]{1,0:T(8,128)} %fusion.15.flag_ref, s32[16,4]{1,0:T(8,128)} %get-tuple-element.11.first_ref, s32[16,4]{1,0:T(8,128)} %get-tuple-element.10.second_ref, bf16[128,128,128]{2,1,0:T(8,128)(2,1)} %bitcast.28, bf16[128,128,128]{2,1,0:T(8,128)(2,1)} %bitcast.44, bf16[128,128,128]{2,1,0:T(8,128)(2,1)} %bitcast.15, ...), custom_call_target="tpu_custom_call" | custom-call | tf_op jit(solution)/shard_map/pallas_call | solution.py:284
  162.2 19.3 %shard_map.100 = f32[512,128]{1,0:T(8,128)} custom-call(f32[4,512,128]{2,1,0:T(8,128)} %bitcast.143), custom_call_target="tpu_custom_call" | custom-call | tf_op jit(solution)/shard_map/pallas_call | solution.py:228
  181.5 1.6 add_convert_fusion
  (1 shorter events, 0.0 us)
Async XLA Ops:
  0.6 89.4 %copy-start = (bf16[128,512]{1,0:T(8,128)(2,1)S(1)}, bf16[128,512]{1,0:T(8,128)(2,1)}, u32[]{:S(2)}) copy-start(bf16[128,512]{1,0:T(8,128)(2,1)} %param.11) | copy-start | bytes 393220
  62.8 27.3 %copy-start.3 = (f32[512]{0:T(512)S(1)}, f32[512]{0:T(512)}, u32[]{:S(2)}) copy-start(f32[512]{0:T(512)} %param.12) | copy-start | bytes 6148
  62.8 28.5 %copy-start.1 = (bf16[512,128]{1,0:T(8,128)(2,1)S(1)}, bf16[512,128]{1,0:T(8,128)(2,1)}, u32[]{:S(2)}) copy-start(bf16[512,128]{1,0:T(8,128)(2,1)} %rows_ref.1) | copy-start | bytes 393220
  62.8 28.5 %copy-start.4 = (bf16[512,128]{1,0:T(8,128)(2,1)S(1)}, bf16[512,128]{1,0:T(8,128)(2,1)}, u32[]{:S(2)}) copy-start(bf16[512,128]{1,0:T(8,128)(2,1)} %param.13) | copy-start | bytes 393220
  62.8 28.5 %copy-start.5 = (f32[128]{0:T(128)S(1)}, f32[128]{0:T(128)}, u32[]{:S(2)}) copy-start(f32[128]{0:T(128)} %param.14) | copy-start | bytes 1540
  69.4 23.0 %copy-start.2 = (bf16[512,128]{1,0:T(8,128)(2,1)S(1)}, bf16[512,128]{1,0:T(8,128)(2,1)}, u32[]{:S(2)}) copy-start(bf16[512,128]{1,0:T(8,128)(2,1)} %param.15) | copy-start | bytes 393220

commit v17 on v16

--- a/solution.py
+++ b/solution.py
@@ -40,7 +40,7 @@
 def gather_phase(phase, ring_src, tree_src, ring_out, tree_out, send_sem, recv_sem, local_sem):
     nx, ny, nz = lax.axis_size("x"), lax.axis_size("ylo"), lax.axis_size("z")
     x, y, z = lax.axis_index("x"), lax.axis_index("ylo"), lax.axis_index("z")
-    left, other = lax.rem(x + nx - 1, nx), ny - 1 - y
+    right, left, other = lax.rem(x + 1, nx), lax.rem(x + nx - 1, nx), ny - 1 - y
     to_right, to_left, to_other, up, down = neighbours()
 
     def send(kind, src, dst, peer):
@@ -64,8 +64,8 @@
     first_other = send(2, tree_src, tree_out.at[me], to_other)
     steps = nz // 2
     split = ring_src.shape[0] // 2
-    ups = [send(7, ring_src, ring_out.at[z], up)]
-    downs = [send(7 + steps, ring_src, ring_out.at[z], down)]
+    ups = [send(9, ring_src, ring_out.at[z], up)]
+    downs = [send(9 + steps, ring_src, ring_out.at[z], down)]
 
     def ring_step(s):
         below = lax.rem(z + nz - (s - 1), nz)
@@ -73,15 +73,19 @@
         ups[-1].wait_recv()
         downs[-1].wait_recv()
         if s < steps:
-            ups.append(send(7 + s - 1, ring_out.at[below], ring_out.at[below], up))
-            downs.append(send(7 + steps + s - 1, ring_out.at[above], ring_out.at[above], down))
+            ups.append(send(9 + s - 1, ring_out.at[below], ring_out.at[below], up))
+            downs.append(send(9 + steps + s - 1, ring_out.at[above], ring_out.at[above], down))
         else:
-            ups.append(send(7 + s - 1, ring_out.at[below, :split], ring_out.at[below, :split], up))
-            downs.append(send(7 + steps + s - 1, ring_out.at[above, split:], ring_out.at[above, split:], down))
-
+            ups.append(send(9 + s - 1, ring_out.at[below, :split], ring_out.at[below, :split], up))
+            downs.append(send(9 + steps + s - 1, ring_out.at[above, split:], ring_out.at[above, split:], down))
+
+    tree_split = tree_src.shape[0] // 2
     first_right.wait_recv()
     from_left = left * ny + y
-    second_right = send(3, tree_out.at[from_left], tree_out.at[from_left], to_right)
+    second_right = send(3, tree_out.at[from_left, :tree_split], tree_out.at[from_left, :tree_split], to_right)
+    first_left.wait_recv()
+    from_right = right * ny + y
+    second_left = send(7, tree_out.at[from_right, tree_split:], tree_out.at[from_right, tree_split:], to_left)
     ring_step(2)
     first_other.wait_recv()
     from_other = x * ny + other
@@ -90,12 +94,20 @@
     ring_step(3)
     other_right.wait_recv()
     from_left_other = left * ny + other
-    third_right = send(6, tree_out.at[from_left_other], tree_out.at[from_left_other], to_right)
+    third_right = send(
+        6, tree_out.at[from_left_other, :tree_split], tree_out.at[from_left_other, :tree_split], to_right
+    )
+    other_left.wait_recv()
+    from_right_other = right * ny + other
+    third_left = send(
+        8, tree_out.at[from_right_other, tree_split:], tree_out.at[from_right_other, tree_split:], to_left
+    )
     for s in range(4, steps + 1):
         ring_step(s)
-    for copy in (first_left, second_right, other_left, third_right, ups[-1], downs[-1]):
+    for copy in (second_right, second_left, third_right, third_left, ups[-1], downs[-1]):
         copy.wait_recv()
-    tree = [first_right, first_left, first_other, second_right, other_right, other_left, third_right]
+    tree = [first_right, first_left, first_other, second_right, second_left]
+    tree += [other_right, other_left, third_right, third_left]
     return tree + ups + downs, [own_tree, own_ring]
 
 
@@ -183,8 +195,8 @@
         in_specs=[any_space],
         out_specs=(any_space,) * 4,
         scratch_shapes=[
-            pltpu.SemaphoreType.DMA((2, 7 + nz)),
-            pltpu.SemaphoreType.DMA((2, 7 + nz)),
+            pltpu.SemaphoreType.DMA((2, 9 + nz)),
+            pltpu.SemaphoreType.DMA((2, 9 + nz)),
             pltpu.SemaphoreType.DMA((2, 2)),
         ],
         compiler_params=pltpu.CompilerParams(collective_id=cid, has_side_effects=True),

time: 186 us -> 183 us (0.984); the launches traced: 183 us -> 182 us
    pallas_call x2, Pallas kernels: 122 us -> 119 us  [gather_blk(): pl.pallas_call(gather_kernel, out_shape=(jax.ShapeDtypeStruct((nz, *piece...]
where the time goes in v17:
time: 183 us; the launch traced here: 182 us
  Pallas kernels  174 us (95%)
  matrix products  3.54 us (2%)
  other arithmetic  2.86 us (2%)
    pallas_call x2, Pallas kernels, gather_blk(): pl.pallas_call(gather_kernel, out_shape=(jax.ShapeDtypeStruct((nz, *piece...  119 us
    pallas_call x2, Pallas kernels, reduce_rep(): pl.pallas_call(reduce_kernel, out_shape=jax.ShapeDtypeStruct(pieces.shape...  40.7 us
    pallas_call x2, Pallas kernels, tile_products(): pl.pallas_call(products_kernel, out_shape=jax.ShapeDtypeStruct((rows, BLO...  14 us

profile of v17, /device:TPU:9, one launch (start us, length us, event | category | flops | bytes accessed | tf_op | source)
XLA Modules:
  0.0 182.0 jit_solution(6171449093588806432)
XLA Ops:
  0.6 0.0 copy-start
  0.6 0.8 copy.10
  1.4 0.6 fusion.15.flag_ref
  2.0 0.6 select_add_fusion
  2.7 57.0 %shard_map.95 = (bf16[8,256,128]{2,1,0:T(8,128)(2,1)}, bf16[8,256,128]{2,1,0:T(8,128)(2,1)}, bf16[8,8,256,128]{3,2,1,0:T(8,128)(2,1)}, bf16[8,8,256,128]{3,2,1,0:T(8,128)(2,1)}) custom-call(bf16[512,128]{1,0:T(8,128)(2,1)} %rows_ref.1), custom_call_target="tpu_custom_call" | custom-call | tf_op jit(solution)/shard_map/pallas_call | solution.py:187
  59.6 0.0 copy-start.3
  59.6 0.0 copy-start.1
  59.7 0.0 copy-start.4
  59.7 0.0 copy-start.5
  59.7 7.0 %shard_map.96 = f32[16,128,128]{2,1,0:T(8,128)} custom-call(s32[16,4]{1,0:T(8,128)} %fusion.15.flag_ref, s32[16,4]{1,0:T(8,128)} %get-tuple-element.11.first_ref, s32[16,4]{1,0:T(8,128)} %get-tuple-element.10.second_ref, bf16[128,128,128]{2,1,0:T(8,128)(2,1)} %bitcast.92, bf16[128,128,128]{2,1,0:T(8,128)(2,1)} %bitcast.108, bf16[128,128,128]{2,1,0:T(8,128)(2,1)} %bitcast.79, ...), custom_call_target="tpu_custom_call" | custom-call | tf_op jit(solution)/shard_map/pallas_call | solution.py:296
  66.7 0.0 copy-start.2
  66.7 22.1 %shard_map.97 = f32[512,128]{1,0:T(8,128)} custom-call(f32[4,512,128]{2,1,0:T(8,128)} %bitcast.144), custom_call_target="tpu_custom_call" | custom-call | tf_op jit(solution)/shard_map/pallas_call | solution.py:240
  88.8 0.0 copy-done
  88.8 0.0 copy-done.3
  88.8 1.2 convolution_add_fusion
  90.1 0.0 copy-done.1
  90.1 0.0 copy-done.4
  90.1 0.0 copy-done.5
  90.1 1.1 fusion.5
  91.2 1.2 fusion.4.rows_ref
  92.4 62.4 %shard_map.98 = (bf16[8,256,128]{2,1,0:T(8,128)(2,1)}, bf16[8,256,128]{2,1,0:T(8,128)(2,1)}, bf16[8,8,256,128]{3,2,1,0:T(8,128)(2,1)}, bf16[8,8,256,128]{3,2,1,0:T(8,128)(2,1)}) custom-call(bf16[512,128]{1,0:T(8,128)(2,1)} %fusion.4.rows_ref), custom_call_target="tpu_custom_call" | custom-call | tf_op jit(solution)/shard_map/pallas_call | solution.py:187
  154.8 7.0 %shard_map.99 = f32[16,128,128]{2,1,0:T(8,128)} custom-call(s32[16,4]{1,0:T(8,128)} %fusion.15.flag_ref, s32[16,4]{1,0:T(8,128)} %get-tuple-element.11.first_ref, s32[16,4]{1,0:T(8,128)} %get-tuple-element.10.second_ref, bf16[128,128,128]{2,1,0:T(8,128)(2,1)} %bitcast.28, bf16[128,128,128]{2,1,0:T(8,128)(2,1)} %bitcast.44, bf16[128,128,128]{2,1,0:T(8,128)(2,1)} %bitcast.15, ...), custom_call_target="tpu_custom_call" | custom-call | tf_op jit(solution)/shard_map/pallas_call | solution.py:296
  161.8 18.5 %shard_map.100 = f32[512,128]{1,0:T(8,128)} custom-call(f32[4,512,128]{2,1,0:T(8,128)} %bitcast.143), custom_call_target="tpu_custom_call" | custom-call | tf_op jit(solution)/shard_map/pallas_call | solution.py:240
  180.4 1.6 add_convert_fusion
  (1 shorter events, 0.0 us)
Async XLA Ops:
  0.6 88.2 %copy-start = (bf16[128,512]{1,0:T(8,128)(2,1)S(1)}, bf16[128,512]{1,0:T(8,128)(2,1)}, u32[]{:S(2)}) copy-start(bf16[128,512]{1,0:T(8,128)(2,1)} %param.11) | copy-start | bytes 393220
  59.6 29.2 %copy-start.3 = (f32[512]{0:T(512)S(1)}, f32[512]{0:T(512)}, u32[]{:S(2)}) copy-start(f32[512]{0:T(512)} %param.12) | copy-start | bytes 6148
  59.6 30.4 %copy-start.1 = (bf16[512,128]{1,0:T(8,128)(2,1)S(1)}, bf16[512,128]{1,0:T(8,128)(2,1)}, u32[]{:S(2)}) copy-start(bf16[512,128]{1,0:T(8,128)(2,1)} %rows_ref.1) | copy-start | bytes 393220
  59.7 30.4 %copy-start.4 = (bf16[512,128]{1,0:T(8,128)(2,1)S(1)}, bf16[512,128]{1,0:T(8,128)(2,1)}, u32[]{:S(2)}) copy-start(bf16[512,128]{1,0:T(8,128)(2,1)} %param.13) | copy-start | bytes 393220
  59.7 30.4 %copy-start.5 = (f32[128]{0:T(128)S(1)}, f32[128]{0:T(128)}, u32[]{:S(2)}) copy-start(f32[128]{0:T(128)} %param.14) | copy-start | bytes 1540
  66.7 24.5 %copy-start.2 = (bf16[512,128]{1,0:T(8,128)(2,1)S(1)}, bf16[512,128]{1,0:T(8,128)(2,1)}, u32[]{:S(2)}) copy-start(bf16[512,128]{1,0:T(8,128)(2,1)} %param.15) | copy-start | bytes 393220

commit v18 on v17

--- a/solution.py
+++ b/solution.py
@@ -204,49 +204,66 @@
     return first.reshape(-1, BLOCK, width), second.reshape(-1, BLOCK, width)
 
 
-def reduce_kernel(src_ref, out_ref, landed, send_sem, recv_sem, local_sem):
-    me, sizes = group_place(REP)
-    n = landed.shape[0]
+def reduce_kernel(src_ref, out_ref, own, landed, mid, last, send_sem, recv_sem, local_sem):
+    nyhi, ncore = lax.axis_size("yhi"), lax.axis_size("core")
+    yhi, core = lax.axis_index("yhi"), lax.axis_index("core")
+    other_core, other_yhi = ncore - 1 - core, nyhi - 1 - yhi
+    to_core, to_yhi = {"core": other_core}, {"yhi": other_yhi}
     barrier = pltpu.get_barrier_semaphore()
-    for d in range(1, n):
-        pl.semaphore_signal(barrier, 1, device_id=peer_id(REP, sizes, lax.rem(me + d, n)))
-    pl.semaphore_wait(barrier, n - 1)
-    copies = []
-    for d in range(1, n):
-        p = lax.rem(me + d, n)
+    for peer in (to_core, to_yhi):
+        pl.semaphore_signal(barrier, 1, device_id=peer)
+    pl.semaphore_wait(barrier, 2)
+    copies, locals_ = [], []
+    for h in range(nyhi):
         copy = pltpu.make_async_remote_copy(
-            src_ref=src_ref.at[p],
-            dst_ref=landed.at[me],
-            send_sem=send_sem.at[d],
-            recv_sem=recv_sem.at[d],
-            device_id=peer_id(REP, sizes, p),
+            src_ref=src_ref.at[h * ncore + other_core],
+            dst_ref=landed.at[h],
+            send_sem=send_sem.at[h],
+            recv_sem=recv_sem.at[h],
+            device_id=to_core,
         )
         copy.start()
         copies.append(copy)
-    own = pltpu.make_async_copy(src_ref.at[me], landed.at[me], local_sem)
-    own.start()
+        keep = pltpu.make_async_copy(src_ref.at[h * ncore + core], own.at[h], local_sem.at[h])
+        keep.start()
+        locals_.append(keep)
     for copy in copies:
-        copy.wait()
-    own.wait()
-    total = landed[0]
-    for slot in range(1, n):
-        total = total + landed[slot]
-    out_ref[...] = total
+        copy.wait_recv()
+    for keep in locals_:
+        keep.wait()
+    mid[...] = own[...] + landed[...]
+    cross = pltpu.make_async_remote_copy(
+        src_ref=mid.at[other_yhi],
+        dst_ref=last,
+        send_sem=send_sem.at[nyhi],
+        recv_sem=recv_sem.at[nyhi],
+        device_id=to_yhi,
+    )
+    cross.start()
+    cross.wait_recv()
+    out_ref[...] = mid[yhi] + last[...]
+    for copy in copies:
+        copy.wait_send()
+    cross.wait_send()
 
 
 def reduce_rep(partial, cid):
-    nrep = lax.axis_size("yhi") * lax.axis_size("core")
-    pieces = partial.reshape(nrep, -1, partial.shape[1])
+    nyhi, ncore = lax.axis_size("yhi"), lax.axis_size("core")
+    pieces = partial.reshape(nyhi * ncore, -1, partial.shape[1])
+    piece = pieces.shape[1:]
     return pl.pallas_call(
         reduce_kernel,
-        out_shape=jax.ShapeDtypeStruct(pieces.shape[1:], pieces.dtype),
+        out_shape=jax.ShapeDtypeStruct(piece, pieces.dtype),
         in_specs=[pl.BlockSpec(memory_space=pl.ANY)],
         out_specs=pl.BlockSpec(memory_space=pltpu.VMEM),
         scratch_shapes=[
-            pltpu.VMEM(pieces.shape, pieces.dtype),
-            pltpu.SemaphoreType.DMA((nrep,)),
-            pltpu.SemaphoreType.DMA((nrep,)),
-            pltpu.SemaphoreType.DMA,
+            pltpu.VMEM((nyhi, *piece), pieces.dtype),
+            pltpu.VMEM((nyhi, *piece), pieces.dtype),
+            pltpu.VMEM((nyhi, *piece), pieces.dtype),
+            pltpu.VMEM(piece, pieces.dtype),
+            pltpu.SemaphoreType.DMA((nyhi + 1,)),
+            pltpu.SemaphoreType.DMA((nyhi + 1,)),
+            pltpu.SemaphoreType.DMA((nyhi,)),
         ],
         compiler_params=pltpu.CompilerParams(collective_id=cid, has_side_effects=True),
     )(pieces)

time: 183 us -> 173 us (0.945)
  Pallas kernels: 174 us -> 164 us
    pallas_call x2, Pallas kernels: 40.7 us -> 33.9 us  [reduce_rep(): pl.pallas_call(reduce_kernel, out_shape=jax.ShapeDtypeStruct(piece, piece...]
    pallas_call x2, Pallas kernels: 119 us -> 116 us  [gather_blk(): pl.pallas_call(gather_kernel, out_shape=(jax.ShapeDtypeStruct((nz, *piece...]
where the time goes in v18:
time: 173 us; the launch traced here: 172 us
  Pallas kernels  164 us (95%)
  matrix products  3.54 us (2%)
  other arithmetic  2.86 us (2%)
    pallas_call x2, Pallas kernels, gather_blk(): pl.pallas_call(gather_kernel, out_shape=(jax.ShapeDtypeStruct((nz, *piece...  116 us
    pallas_call x2, Pallas kernels, reduce_rep(): pl.pallas_call(reduce_kernel, out_shape=jax.ShapeDtypeStruct(piece, piece...  33.9 us
    pallas_call x2, Pallas kernels, tile_products(): pl.pallas_call(products_kernel, out_shape=jax.ShapeDtypeStruct((rows, BLO...  13.9 us

profile of v18, /device:TPU:9, one launch (start us, length us, event | category | flops | bytes accessed | tf_op | source)
XLA Modules:
  0.0 172.1 jit_solution(14327987258644658698)
XLA Ops:
  0.6 0.0 copy-start
  0.6 0.8 copy.10
  1.4 0.6 fusion.15.flag_ref
  2.0 0.6 select_add_fusion
  2.7 57.0 %shard_map.95 = (bf16[8,256,128]{2,1,0:T(8,128)(2,1)}, bf16[8,256,128]{2,1,0:T(8,128)(2,1)}, bf16[8,8,256,128]{3,2,1,0:T(8,128)(2,1)}, bf16[8,8,256,128]{3,2,1,0:T(8,128)(2,1)}) custom-call(bf16[512,128]{1,0:T(8,128)(2,1)} %rows_ref.1), custom_call_target="tpu_custom_call" | custom-call | tf_op jit(solution)/shard_map/pallas_call | solution.py:187
  59.6 0.0 copy-start.3
  59.6 0.0 copy-start.1
  59.7 0.0 copy-start.4
  59.7 0.0 copy-start.5
  59.7 6.9 %shard_map.96 = f32[16,128,128]{2,1,0:T(8,128)} custom-call(s32[16,4]{1,0:T(8,128)} %fusion.15.flag_ref, s32[16,4]{1,0:T(8,128)} %get-tuple-element.11.first_ref, s32[16,4]{1,0:T(8,128)} %get-tuple-element.10.second_ref, bf16[128,128,128]{2,1,0:T(8,128)(2,1)} %bitcast.92, bf16[128,128,128]{2,1,0:T(8,128)(2,1)} %bitcast.108, bf16[128,128,128]{2,1,0:T(8,128)(2,1)} %bitcast.79, ...), custom_call_target="tpu_custom_call" | custom-call | tf_op jit(solution)/shard_map/pallas_call | solution.py:313
  66.6 0.0 copy-start.2
  66.6 17.9 %shard_map.97 = f32[512,128]{1,0:T(8,128)} custom-call(f32[4,512,128]{2,1,0:T(8,128)} %bitcast.144), custom_call_target="tpu_custom_call" | custom-call | tf_op jit(solution)/shard_map/pallas_call | solution.py:254
  84.6 0.0 copy-done
  84.6 0.0 copy-done.3
  84.6 1.2 convolution_add_fusion
  85.8 0.0 copy-done.1
  85.8 0.0 copy-done.4
  85.8 0.0 copy-done.5
  85.8 1.1 fusion.5
  86.9 1.2 fusion.4.rows_ref
  88.2 59.3 %shard_map.98 = (bf16[8,256,128]{2,1,0:T(8,128)(2,1)}, bf16[8,256,128]{2,1,0:T(8,128)(2,1)}, bf16[8,8,256,128]{3,2,1,0:T(8,128)(2,1)}, bf16[8,8,256,128]{3,2,1,0:T(8,128)(2,1)}) custom-call(bf16[512,128]{1,0:T(8,128)(2,1)} %fusion.4.rows_ref), custom_call_target="tpu_custom_call" | custom-call | tf_op jit(solution)/shard_map/pallas_call | solution.py:187
  147.5 6.9 %shard_map.99 = f32[16,128,128]{2,1,0:T(8,128)} custom-call(s32[16,4]{1,0:T(8,128)} %fusion.15.flag_ref, s32[16,4]{1,0:T(8,128)} %get-tuple-element.11.first_ref, s32[16,4]{1,0:T(8,128)} %get-tuple-element.10.second_ref, bf16[128,128,128]{2,1,0:T(8,128)(2,1)} %bitcast.28, bf16[128,128,128]{2,1,0:T(8,128)(2,1)} %bitcast.44, bf16[128,128,128]{2,1,0:T(8,128)(2,1)} %bitcast.15, ...), custom_call_target="tpu_custom_call" | custom-call | tf_op jit(solution)/shard_map/pallas_call | solution.py:313
  154.5 16.0 %shard_map.100 = f32[512,128]{1,0:T(8,128)} custom-call(f32[4,512,128]{2,1,0:T(8,128)} %bitcast.143), custom_call_target="tpu_custom_call" | custom-call | tf_op jit(solution)/shard_map/pallas_call | solution.py:254
  170.4 1.6 add_convert_fusion
  (1 shorter events, 0.0 us)
Async XLA Ops:
  0.6 83.9 %copy-start = (bf16[128,512]{1,0:T(8,128)(2,1)S(1)}, bf16[128,512]{1,0:T(8,128)(2,1)}, u32[]{:S(2)}) copy-start(bf16[128,512]{1,0:T(8,128)(2,1)} %param.11) | copy-start | bytes 393220
  59.6 24.9 %copy-start.3 = (f32[512]{0:T(512)S(1)}, f32[512]{0:T(512)}, u32[]{:S(2)}) copy-start(f32[512]{0:T(512)} %param.12) | copy-start | bytes 6148
  59.6 26.2 %copy-start.1 = (bf16[512,128]{1,0:T(8,128)(2,1)S(1)}, bf16[512,128]{1,0:T(8,128)(2,1)}, u32[]{:S(2)}) copy-start(bf16[512,128]{1,0:T(8,128)(2,1)} %rows_ref.1) | copy-start | bytes 393220
  59.7 26.2 %copy-start.4 = (bf16[512,128]{1,0:T(8,128)(2,1)S(1)}, bf16[512,128]{1,0:T(8,128)(2,1)}, u32[]{:S(2)}) copy-start(bf16[512,128]{1,0:T(8,128)(2,1)} %param.13) | copy-start | bytes 393220
  59.7 26.2 %copy-start.5 = (f32[128]{0:T(128)S(1)}, f32[128]{0:T(128)}, u32[]{:S(2)}) copy-start(f32[128]{0:T(128)} %param.14) | copy-start | bytes 1540
  66.6 20.3 %copy-start.2 = (bf16[512,128]{1,0:T(8,128)(2,1)S(1)}, bf16[512,128]{1,0:T(8,128)(2,1)}, u32[]{:S(2)}) copy-start(bf16[512,128]{1,0:T(8,128)(2,1)} %param.15) | copy-start | bytes 393220

commit v19 on v18

--- a/solution.py
+++ b/solution.py
@@ -231,7 +231,8 @@
         copy.wait_recv()
     for keep in locals_:
         keep.wait()
-    mid[...] = own[...] + landed[...]
+    mid[other_yhi] = own[other_yhi] + landed[other_yhi]
+    mid[yhi] = own[yhi] + landed[yhi]
     cross = pltpu.make_async_remote_copy(
         src_ref=mid.at[other_yhi],
         dst_ref=last,

time: 173 us -> 173 us (level)
  no operation moved by 1% of the time
where the time goes in v19:
time: 173 us; the launch traced here: 171 us
  Pallas kernels  163 us (94%)
  matrix products  3.53 us (2%)
  other arithmetic  2.86 us (2%)
    pallas_call x2, Pallas kernels, gather_blk(): pl.pallas_call(gather_kernel, out_shape=(jax.ShapeDtypeStruct((nz, *piece...  115 us
    pallas_call x2, Pallas kernels, reduce_rep(): pl.pallas_call(reduce_kernel, out_shape=jax.ShapeDtypeStruct(piece, piece...  33.6 us
    pallas_call x2, Pallas kernels, tile_products(): pl.pallas_call(products_kernel, out_shape=jax.ShapeDtypeStruct((rows, BLO...  14.4 us

profile of v19, /device:TPU:9, one launch (start us, length us, event | category | flops | bytes accessed | tf_op | source)
XLA Modules:
  0.0 170.9 jit_solution(16667632447664283042)
XLA Ops:
  0.6 0.0 copy-start
  0.6 0.8 copy.10
  1.4 0.6 fusion.15.flag_ref
  2.0 0.6 select_add_fusion
  2.7 57.0 %shard_map.95 = (bf16[8,256,128]{2,1,0:T(8,128)(2,1)}, bf16[8,256,128]{2,1,0:T(8,128)(2,1)}, bf16[8,8,256,128]{3,2,1,0:T(8,128)(2,1)}, bf16[8,8,256,128]{3,2,1,0:T(8,128)(2,1)}) custom-call(bf16[512,128]{1,0:T(8,128)(2,1)} %rows_ref.1), custom_call_target="tpu_custom_call" | custom-call | tf_op jit(solution)/shard_map/pallas_call | solution.py:187
  59.6 0.0 copy-start.3
  59.6 0.0 copy-start.1
  59.7 0.0 copy-start.4
  59.7 0.0 copy-start.5
  59.7 7.2 %shard_map.96 = f32[16,128,128]{2,1,0:T(8,128)} custom-call(s32[16,4]{1,0:T(8,128)} %fusion.15.flag_ref, s32[16,4]{1,0:T(8,128)} %get-tuple-element.11.first_ref, s32[16,4]{1,0:T(8,128)} %get-tuple-element.10.second_ref, bf16[128,128,128]{2,1,0:T(8,128)(2,1)} %bitcast.92, bf16[128,128,128]{2,1,0:T(8,128)(2,1)} %bitcast.108, bf16[128,128,128]{2,1,0:T(8,128)(2,1)} %bitcast.79, ...), custom_call_target="tpu_custom_call" | custom-call | tf_op jit(solution)/shard_map/pallas_call | solution.py:314
  66.9 0.0 copy-start.2
  66.9 17.7 %shard_map.97 = f32[512,128]{1,0:T(8,128)} custom-call(f32[4,512,128]{2,1,0:T(8,128)} %bitcast.144), custom_call_target="tpu_custom_call" | custom-call | tf_op jit(solution)/shard_map/pallas_call | solution.py:255
  84.6 0.0 copy-done
  84.6 0.0 copy-done.3
  84.6 1.2 convolution_add_fusion
  85.8 0.0 copy-done.1
  85.8 0.0 copy-done.4
  85.8 0.0 copy-done.5
  85.8 1.1 fusion.5
  86.9 1.2 fusion.4.rows_ref
  88.2 58.0 %shard_map.98 = (bf16[8,256,128]{2,1,0:T(8,128)(2,1)}, bf16[8,256,128]{2,1,0:T(8,128)(2,1)}, bf16[8,8,256,128]{3,2,1,0:T(8,128)(2,1)}, bf16[8,8,256,128]{3,2,1,0:T(8,128)(2,1)}) custom-call(bf16[512,128]{1,0:T(8,128)(2,1)} %fusion.4.rows_ref), custom_call_target="tpu_custom_call" | custom-call | tf_op jit(solution)/shard_map/pallas_call | solution.py:187
  146.2 7.2 %shard_map.99 = f32[16,128,128]{2,1,0:T(8,128)} custom-call(s32[16,4]{1,0:T(8,128)} %fusion.15.flag_ref, s32[16,4]{1,0:T(8,128)} %get-tuple-element.11.first_ref, s32[16,4]{1,0:T(8,128)} %get-tuple-element.10.second_ref, bf16[128,128,128]{2,1,0:T(8,128)(2,1)} %bitcast.28, bf16[128,128,128]{2,1,0:T(8,128)(2,1)} %bitcast.44, bf16[128,128,128]{2,1,0:T(8,128)(2,1)} %bitcast.15, ...), custom_call_target="tpu_custom_call" | custom-call | tf_op jit(solution)/shard_map/pallas_call | solution.py:314
  153.4 15.9 %shard_map.100 = f32[512,128]{1,0:T(8,128)} custom-call(f32[4,512,128]{2,1,0:T(8,128)} %bitcast.143), custom_call_target="tpu_custom_call" | custom-call | tf_op jit(solution)/shard_map/pallas_call | solution.py:255
  169.3 1.6 add_convert_fusion
  (1 shorter events, 0.0 us)
Async XLA Ops:
  0.6 83.9 %copy-start = (bf16[128,512]{1,0:T(8,128)(2,1)S(1)}, bf16[128,512]{1,0:T(8,128)(2,1)}, u32[]{:S(2)}) copy-start(bf16[128,512]{1,0:T(8,128)(2,1)} %param.11) | copy-start | bytes 393220
  59.6 24.9 %copy-start.3 = (f32[512]{0:T(512)S(1)}, f32[512]{0:T(512)}, u32[]{:S(2)}) copy-start(f32[512]{0:T(512)} %param.12) | copy-start | bytes 6148
  59.6 26.2 %copy-start.1 = (bf16[512,128]{1,0:T(8,128)(2,1)S(1)}, bf16[512,128]{1,0:T(8,128)(2,1)}, u32[]{:S(2)}) copy-start(bf16[512,128]{1,0:T(8,128)(2,1)} %rows_ref.1) | copy-start | bytes 393220
  59.7 26.2 %copy-start.4 = (bf16[512,128]{1,0:T(8,128)(2,1)S(1)}, bf16[512,128]{1,0:T(8,128)(2,1)}, u32[]{:S(2)}) copy-start(bf16[512,128]{1,0:T(8,128)(2,1)} %param.13) | copy-start | bytes 393220
  59.7 26.2 %copy-start.5 = (f32[128]{0:T(128)S(1)}, f32[128]{0:T(128)}, u32[]{:S(2)}) copy-start(f32[128]{0:T(128)} %param.14) | copy-start | bytes 1540
  66.9 20.1 %copy-start.2 = (bf16[512,128]{1,0:T(8,128)(2,1)S(1)}, bf16[512,128]{1,0:T(8,128)(2,1)}, u32[]{:S(2)}) copy-start(bf16[512,128]{1,0:T(8,128)(2,1)} %param.15) | copy-start | bytes 393220

commit v20 on v19

--- a/solution.py
+++ b/solution.py
@@ -63,21 +63,33 @@
     first_left = send(1, tree_src, tree_out.at[me], to_left)
     first_other = send(2, tree_src, tree_out.at[me], to_other)
     steps = nz // 2
-    split = ring_src.shape[0] // 2
-    ups = [send(9, ring_src, ring_out.at[z], up)]
-    downs = [send(9 + steps, ring_src, ring_out.at[z], down)]
+    slots = ring_src.shape[0]
+    miss = slots // 4
+    keep = slots - miss
+    lo = miss * y
+    ups = [send(9, ring_src.at[pl.ds(lo, keep)], ring_out.at[z, pl.ds(lo, keep)], up)]
+    downs = [send(9 + steps, ring_src.at[pl.ds(lo, keep)], ring_out.at[z, pl.ds(lo, keep)], down)]
+    handed = []
+
+    def hand(origin):
+        part = pl.ds(keep * y, miss)
+        handed.append(send(9 + 2 * steps + len(handed), ring_out.at[origin, part], ring_out.at[origin, part], to_other))
 
     def ring_step(s):
         below = lax.rem(z + nz - (s - 1), nz)
         above = lax.rem(z + s - 1, nz)
         ups[-1].wait_recv()
         downs[-1].wait_recv()
+        hand(below)
+        hand(above)
         if s < steps:
-            ups.append(send(9 + s - 1, ring_out.at[below], ring_out.at[below], up))
-            downs.append(send(9 + steps + s - 1, ring_out.at[above], ring_out.at[above], down))
+            part = pl.ds(lo, keep)
+            ups.append(send(9 + s - 1, ring_out.at[below, part], ring_out.at[below, part], up))
+            downs.append(send(9 + steps + s - 1, ring_out.at[above, part], ring_out.at[above, part], down))
         else:
-            ups.append(send(9 + s - 1, ring_out.at[below, :split], ring_out.at[below, :split], up))
-            downs.append(send(9 + steps + s - 1, ring_out.at[above, split:], ring_out.at[above, split:], down))
+            first, second = pl.ds(lo, keep // 2), pl.ds(lo + keep // 2, keep - keep // 2)
+            ups.append(send(9 + s - 1, ring_out.at[below, first], ring_out.at[below, first], up))
+            downs.append(send(9 + steps + s - 1, ring_out.at[above, second], ring_out.at[above, second], down))
 
     tree_split = tree_src.shape[0] // 2
     first_right.wait_recv()
@@ -104,11 +116,14 @@
     )
     for s in range(4, steps + 1):
         ring_step(s)
-    for copy in (second_right, second_left, third_right, third_left, ups[-1], downs[-1]):
+    ups[-1].wait_recv()
+    downs[-1].wait_recv()
+    hand(lax.rem(z + steps, nz))
+    for copy in [second_right, second_left, third_right, third_left] + handed:
         copy.wait_recv()
     tree = [first_right, first_left, first_other, second_right, second_left]
     tree += [other_right, other_left, third_right, third_left]
-    return tree + ups + downs, [own_tree, own_ring]
+    return tree + ups + downs + handed, [own_tree, own_ring]
 
 
 def phase_one(ring_src, tree_src, ring_out, tree_out, send_sem, recv_sem, local_sem):
@@ -195,8 +210,8 @@
         in_specs=[any_space],
         out_specs=(any_space,) * 4,
         scratch_shapes=[
-            pltpu.SemaphoreType.DMA((2, 9 + nz)),
-            pltpu.SemaphoreType.DMA((2, 9 + nz)),
+            pltpu.SemaphoreType.DMA((2, 9 + 2 * nz)),
+            pltpu.SemaphoreType.DMA((2, 9 + 2 * nz)),
             pltpu.SemaphoreType.DMA((2, 2)),
         ],
         compiler_params=pltpu.CompilerParams(collective_id=cid, has_side_effects=True),

time: 173 us -> 173 us (level)
    pallas_call x2, Pallas kernels: 115 us -> 113 us  [gather_blk(): pl.pallas_call(gather_kernel, out_shape=(jax.ShapeDtypeStruct((nz, *piece...]
where the time goes in v20:
time: 173 us; the launch traced here: 170 us
  Pallas kernels  162 us (94%)
  matrix products  3.54 us (2%)
  other arithmetic  2.86 us (2%)
    pallas_call x2, Pallas kernels, gather_blk(): pl.pallas_call(gather_kernel, out_shape=(jax.ShapeDtypeStruct((nz, *piece...  113 us
    pallas_call x2, Pallas kernels, reduce_rep(): pl.pallas_call(reduce_kernel, out_shape=jax.ShapeDtypeStruct(piece, piece...  34.5 us
    pallas_call x2, Pallas kernels, tile_products(): pl.pallas_call(products_kernel, out_shape=jax.ShapeDtypeStruct((rows, BLO...  14.1 us

profile of v20, /device:TPU:9, one launch (start us, length us, event | category | flops | bytes accessed | tf_op | source)
XLA Modules:
  0.0 169.6 jit_solution(5970580059740916729)
XLA Ops:
  0.6 0.0 copy-start
  0.6 0.8 copy.10
  1.4 0.6 fusion.15.flag_ref
  2.0 0.6 select_add_fusion
  2.7 56.7 %shard_map.95 = (bf16[8,256,128]{2,1,0:T(8,128)(2,1)}, bf16[8,256,128]{2,1,0:T(8,128)(2,1)}, bf16[8,8,256,128]{3,2,1,0:T(8,128)(2,1)}, bf16[8,8,256,128]{3,2,1,0:T(8,128)(2,1)}) custom-call(bf16[512,128]{1,0:T(8,128)(2,1)} %rows_ref.1), custom_call_target="tpu_custom_call" | custom-call | tf_op jit(solution)/shard_map/pallas_call | solution.py:202
  59.4 0.0 copy-start.3
  59.4 0.0 copy-start.1
  59.4 0.0 copy-start.4
  59.4 0.0 copy-start.5
  59.5 7.1 %shard_map.96 = f32[16,128,128]{2,1,0:T(8,128)} custom-call(s32[16,4]{1,0:T(8,128)} %fusion.15.flag_ref, s32[16,4]{1,0:T(8,128)} %get-tuple-element.11.first_ref, s32[16,4]{1,0:T(8,128)} %get-tuple-element.10.second_ref, bf16[128,128,128]{2,1,0:T(8,128)(2,1)} %bitcast.92, bf16[128,128,128]{2,1,0:T(8,128)(2,1)} %bitcast.108, bf16[128,128,128]{2,1,0:T(8,128)(2,1)} %bitcast.79, ...), custom_call_target="tpu_custom_call" | custom-call | tf_op jit(solution)/shard_map/pallas_call | solution.py:329
  66.5 0.0 copy-start.2
  66.5 18.8 %shard_map.97 = f32[512,128]{1,0:T(8,128)} custom-call(f32[4,512,128]{2,1,0:T(8,128)} %bitcast.144), custom_call_target="tpu_custom_call" | custom-call | tf_op jit(solution)/shard_map/pallas_call | solution.py:270
  85.3 0.0 copy-done
  85.3 0.0 copy-done.3
  85.3 1.2 convolution_add_fusion
  86.6 0.0 copy-done.1
  86.6 0.0 copy-done.4
  86.6 0.0 copy-done.5
  86.6 1.1 fusion.5
  87.7 1.2 fusion.4.rows_ref
  88.9 56.2 %shard_map.98 = (bf16[8,256,128]{2,1,0:T(8,128)(2,1)}, bf16[8,256,128]{2,1,0:T(8,128)(2,1)}, bf16[8,8,256,128]{3,2,1,0:T(8,128)(2,1)}, bf16[8,8,256,128]{3,2,1,0:T(8,128)(2,1)}) custom-call(bf16[512,128]{1,0:T(8,128)(2,1)} %fusion.4.rows_ref), custom_call_target="tpu_custom_call" | custom-call | tf_op jit(solution)/shard_map/pallas_call | solution.py:202
  145.1 7.1 %shard_map.99 = f32[16,128,128]{2,1,0:T(8,128)} custom-call(s32[16,4]{1,0:T(8,128)} %fusion.15.flag_ref, s32[16,4]{1,0:T(8,128)} %get-tuple-element.11.first_ref, s32[16,4]{1,0:T(8,128)} %get-tuple-element.10.second_ref, bf16[128,128,128]{2,1,0:T(8,128)(2,1)} %bitcast.28, bf16[128,128,128]{2,1,0:T(8,128)(2,1)} %bitcast.44, bf16[128,128,128]{2,1,0:T(8,128)(2,1)} %bitcast.15, ...), custom_call_target="tpu_custom_call" | custom-call | tf_op jit(solution)/shard_map/pallas_call | solution.py:329
  152.2 15.7 %shard_map.100 = f32[512,128]{1,0:T(8,128)} custom-call(f32[4,512,128]{2,1,0:T(8,128)} %bitcast.143), custom_call_target="tpu_custom_call" | custom-call | tf_op jit(solution)/shard_map/pallas_call | solution.py:270
  167.9 1.6 add_convert_fusion
  (1 shorter events, 0.0 us)
Async XLA Ops:
  0.6 84.7 %copy-start = (bf16[128,512]{1,0:T(8,128)(2,1)S(1)}, bf16[128,512]{1,0:T(8,128)(2,1)}, u32[]{:S(2)}) copy-start(bf16[128,512]{1,0:T(8,128)(2,1)} %param.11) | copy-start | bytes 393220
  59.4 25.9 %copy-start.3 = (f32[512]{0:T(512)S(1)}, f32[512]{0:T(512)}, u32[]{:S(2)}) copy-start(f32[512]{0:T(512)} %param.12) | copy-start | bytes 6148
  59.4 27.1 %copy-start.1 = (bf16[512,128]{1,0:T(8,128)(2,1)S(1)}, bf16[512,128]{1,0:T(8,128)(2,1)}, u32[]{:S(2)}) copy-start(bf16[512,128]{1,0:T(8,128)(2,1)} %rows_ref.1) | copy-start | bytes 393220
  59.4 27.1 %copy-start.4 = (bf16[512,128]{1,0:T(8,128)(2,1)S(1)}, bf16[512,128]{1,0:T(8,128)(2,1)}, u32[]{:S(2)}) copy-start(bf16[512,128]{1,0:T(8,128)(2,1)} %param.13) | copy-start | bytes 393220
  59.4 27.1 %copy-start.5 = (f32[128]{0:T(128)S(1)}, f32[128]{0:T(128)}, u32[]{:S(2)}) copy-start(f32[128]{0:T(128)} %param.14) | copy-start | bytes 1540
  66.5 21.2 %copy-start.2 = (bf16[512,128]{1,0:T(8,128)(2,1)S(1)}, bf16[512,128]{1,0:T(8,128)(2,1)}, u32[]{:S(2)}) copy-start(bf16[512,128]{1,0:T(8,128)(2,1)} %param.15) | copy-start | bytes 393220

commit v21 on v19

--- a/solution.py
+++ b/solution.py
@@ -63,21 +63,26 @@
     first_left = send(1, tree_src, tree_out.at[me], to_left)
     first_other = send(2, tree_src, tree_out.at[me], to_other)
     steps = nz // 2
-    split = ring_src.shape[0] // 2
-    ups = [send(9, ring_src, ring_out.at[z], up)]
-    downs = [send(9 + steps, ring_src, ring_out.at[z], down)]
+    half = ring_src.shape[0] // 2
+    chunks = (pl.ds(0, half), pl.ds(half, half))
+    ups = [[send(9 + c, ring_src.at[part], ring_out.at[z, part], up)] for c, part in enumerate(chunks)]
+    downs = [
+        [send(9 + 4 * steps + c, ring_src.at[part], ring_out.at[z, part], down)]
+        for c, part in enumerate(chunks)
+    ]
 
     def ring_step(s):
         below = lax.rem(z + nz - (s - 1), nz)
         above = lax.rem(z + s - 1, nz)
-        ups[-1].wait_recv()
-        downs[-1].wait_recv()
-        if s < steps:
-            ups.append(send(9 + s - 1, ring_out.at[below], ring_out.at[below], up))
-            downs.append(send(9 + steps + s - 1, ring_out.at[above], ring_out.at[above], down))
-        else:
-            ups.append(send(9 + s - 1, ring_out.at[below, :split], ring_out.at[below, :split], up))
-            downs.append(send(9 + steps + s - 1, ring_out.at[above, split:], ring_out.at[above, split:], down))
+        for c, part in enumerate(chunks):
+            ups[c][-1].wait_recv()
+            if s < steps or c == 0:
+                ups[c].append(send(9 + 2 * (s - 1) + c, ring_out.at[below, part], ring_out.at[below, part], up))
+            downs[c][-1].wait_recv()
+            if s < steps or c == 1:
+                downs[c].append(
+                    send(9 + 4 * steps + 2 * (s - 1) + c, ring_out.at[above, part], ring_out.at[above, part], down)
+                )
 
     tree_split = tree_src.shape[0] // 2
     first_right.wait_recv()
@@ -104,11 +109,11 @@
     )
     for s in range(4, steps + 1):
         ring_step(s)
-    for copy in (second_right, second_left, third_right, third_left, ups[-1], downs[-1]):
+    for copy in (second_right, second_left, third_right, third_left, ups[0][-1], downs[1][-1]):
         copy.wait_recv()
     tree = [first_right, first_left, first_other, second_right, second_left]
     tree += [other_right, other_left, third_right, third_left]
-    return tree + ups + downs, [own_tree, own_ring]
+    return tree + ups[0] + ups[1] + downs[0] + downs[1], [own_tree, own_ring]
 
 
 def phase_one(ring_src, tree_src, ring_out, tree_out, send_sem, recv_sem, local_sem):
@@ -195,8 +200,8 @@
         in_specs=[any_space],
         out_specs=(any_space,) * 4,
         scratch_shapes=[
-            pltpu.SemaphoreType.DMA((2, 9 + nz)),
-            pltpu.SemaphoreType.DMA((2, 9 + nz)),
+            pltpu.SemaphoreType.DMA((2, 9 + 4 * nz)),
+            pltpu.SemaphoreType.DMA((2, 9 + 4 * nz)),
             pltpu.SemaphoreType.DMA((2, 2)),
         ],
         compiler_params=pltpu.CompilerParams(collective_id=cid, has_side_effects=True),

time: 173 us -> 173 us (level)
  no operation moved by 1% of the time
where the time goes in v21:
time: 173 us; the launch traced here: 171 us
  Pallas kernels  163 us (94%)
  matrix products  3.54 us (2%)
  other arithmetic  2.86 us (2%)
    pallas_call x2, Pallas kernels, gather_blk(): pl.pallas_call(gather_kernel, out_shape=(jax.ShapeDtypeStruct((nz, *piece...  115 us
    pallas_call x2, Pallas kernels, reduce_rep(): pl.pallas_call(reduce_kernel, out_shape=jax.ShapeDtypeStruct(piece, piece...  33.8 us
    pallas_call x2, Pallas kernels, tile_products(): pl.pallas_call(products_kernel, out_shape=jax.ShapeDtypeStruct((rows, BLO...  13.9 us

profile of v21, /device:TPU:9, one launch (start us, length us, event | category | flops | bytes accessed | tf_op | source)
XLA Modules:
  0.0 171.0 jit_solution(4266654627645177696)
XLA Ops:
  0.6 0.0 copy-start
  0.6 0.8 copy.10
  1.4 0.6 fusion.15.flag_ref
  2.0 0.6 select_add_fusion
  2.7 57.1 %shard_map.95 = (bf16[8,256,128]{2,1,0:T(8,128)(2,1)}, bf16[8,256,128]{2,1,0:T(8,128)(2,1)}, bf16[8,8,256,128]{3,2,1,0:T(8,128)(2,1)}, bf16[8,8,256,128]{3,2,1,0:T(8,128)(2,1)}) custom-call(bf16[512,128]{1,0:T(8,128)(2,1)} %rows_ref.1), custom_call_target="tpu_custom_call" | custom-call | tf_op jit(solution)/shard_map/pallas_call | solution.py:192
  59.8 0.0 copy-start.3
  59.8 0.0 copy-start.1
  59.8 0.0 copy-start.4
  59.8 0.0 copy-start.5
  59.8 6.9 %shard_map.96 = f32[16,128,128]{2,1,0:T(8,128)} custom-call(s32[16,4]{1,0:T(8,128)} %fusion.15.flag_ref, s32[16,4]{1,0:T(8,128)} %get-tuple-element.11.first_ref, s32[16,4]{1,0:T(8,128)} %get-tuple-element.10.second_ref, bf16[128,128,128]{2,1,0:T(8,128)(2,1)} %bitcast.92, bf16[128,128,128]{2,1,0:T(8,128)(2,1)} %bitcast.108, bf16[128,128,128]{2,1,0:T(8,128)(2,1)} %bitcast.79, ...), custom_call_target="tpu_custom_call" | custom-call | tf_op jit(solution)/shard_map/pallas_call | solution.py:319
  66.8 0.0 copy-start.2
  66.8 18.1 %shard_map.97 = f32[512,128]{1,0:T(8,128)} custom-call(f32[4,512,128]{2,1,0:T(8,128)} %bitcast.144), custom_call_target="tpu_custom_call" | custom-call | tf_op jit(solution)/shard_map/pallas_call | solution.py:260
  84.9 0.0 copy-done
  84.9 0.0 copy-done.3
  84.9 1.2 convolution_add_fusion
  86.1 0.0 copy-done.1
  86.1 0.0 copy-done.4
  86.1 0.0 copy-done.5
  86.1 1.1 fusion.5
  87.2 1.2 fusion.4.rows_ref
  88.5 58.3 %shard_map.98 = (bf16[8,256,128]{2,1,0:T(8,128)(2,1)}, bf16[8,256,128]{2,1,0:T(8,128)(2,1)}, bf16[8,8,256,128]{3,2,1,0:T(8,128)(2,1)}, bf16[8,8,256,128]{3,2,1,0:T(8,128)(2,1)}) custom-call(bf16[512,128]{1,0:T(8,128)(2,1)} %fusion.4.rows_ref), custom_call_target="tpu_custom_call" | custom-call | tf_op jit(solution)/shard_map/pallas_call | solution.py:192
  146.7 6.9 %shard_map.99 = f32[16,128,128]{2,1,0:T(8,128)} custom-call(s32[16,4]{1,0:T(8,128)} %fusion.15.flag_ref, s32[16,4]{1,0:T(8,128)} %get-tuple-element.11.first_ref, s32[16,4]{1,0:T(8,128)} %get-tuple-element.10.second_ref, bf16[128,128,128]{2,1,0:T(8,128)(2,1)} %bitcast.28, bf16[128,128,128]{2,1,0:T(8,128)(2,1)} %bitcast.44, bf16[128,128,128]{2,1,0:T(8,128)(2,1)} %bitcast.15, ...), custom_call_target="tpu_custom_call" | custom-call | tf_op jit(solution)/shard_map/pallas_call | solution.py:319
  153.7 15.7 %shard_map.100 = f32[512,128]{1,0:T(8,128)} custom-call(f32[4,512,128]{2,1,0:T(8,128)} %bitcast.143), custom_call_target="tpu_custom_call" | custom-call | tf_op jit(solution)/shard_map/pallas_call | solution.py:260
  169.4 1.6 add_convert_fusion
  (1 shorter events, 0.0 us)
Async XLA Ops:
  0.6 84.2 %copy-start = (bf16[128,512]{1,0:T(8,128)(2,1)S(1)}, bf16[128,512]{1,0:T(8,128)(2,1)}, u32[]{:S(2)}) copy-start(bf16[128,512]{1,0:T(8,128)(2,1)} %param.11) | copy-start | bytes 393220
  59.8 25.1 %copy-start.3 = (f32[512]{0:T(512)S(1)}, f32[512]{0:T(512)}, u32[]{:S(2)}) copy-start(f32[512]{0:T(512)} %param.12) | copy-start | bytes 6148
  59.8 26.3 %copy-start.1 = (bf16[512,128]{1,0:T(8,128)(2,1)S(1)}, bf16[512,128]{1,0:T(8,128)(2,1)}, u32[]{:S(2)}) copy-start(bf16[512,128]{1,0:T(8,128)(2,1)} %rows_ref.1) | copy-start | bytes 393220
  59.8 26.3 %copy-start.4 = (bf16[512,128]{1,0:T(8,128)(2,1)S(1)}, bf16[512,128]{1,0:T(8,128)(2,1)}, u32[]{:S(2)}) copy-start(bf16[512,128]{1,0:T(8,128)(2,1)} %param.13) | copy-start | bytes 393220
  59.8 26.3 %copy-start.5 = (f32[128]{0:T(128)S(1)}, f32[128]{0:T(128)}, u32[]{:S(2)}) copy-start(f32[128]{0:T(128)} %param.14) | copy-start | bytes 1540
  66.8 20.5 %copy-start.2 = (bf16[512,128]{1,0:T(8,128)(2,1)S(1)}, bf16[512,128]{1,0:T(8,128)(2,1)}, u32[]{:S(2)}) copy-start(bf16[512,128]{1,0:T(8,128)(2,1)} %param.15) | copy-start | bytes 393220

commit v22 on v21

--- a/solution.py
+++ b/solution.py
@@ -37,7 +37,7 @@
     return {"x": right}, {"x": left}, {"ylo": other}, {"z": lax.rem(z + 1, nz)}, {"z": lax.rem(z + nz - 1, nz)}
 
 
-def gather_phase(phase, ring_src, tree_src, ring_out, tree_out, send_sem, recv_sem, local_sem):
+def gather_phase(phase, ring_src, tree_src, ring_out, tree_out, send_sem, recv_sem, local_sem, ready):
     nx, ny, nz = lax.axis_size("x"), lax.axis_size("ylo"), lax.axis_size("z")
     x, y, z = lax.axis_index("x"), lax.axis_index("ylo"), lax.axis_index("z")
     right, left, other = lax.rem(x + 1, nx), lax.rem(x + nx - 1, nx), ny - 1 - y
@@ -55,13 +55,8 @@
         return copy
 
     me = x * ny + y
-    own_tree = pltpu.make_async_copy(tree_src, tree_out.at[me], local_sem.at[phase, 0])
-    own_tree.start()
     own_ring = pltpu.make_async_copy(ring_src, ring_out.at[z], local_sem.at[phase, 1])
     own_ring.start()
-    first_right = send(0, tree_src, tree_out.at[me], to_right)
-    first_left = send(1, tree_src, tree_out.at[me], to_left)
-    first_other = send(2, tree_src, tree_out.at[me], to_other)
     steps = nz // 2
     half = ring_src.shape[0] // 2
     chunks = (pl.ds(0, half), pl.ds(half, half))
@@ -70,6 +65,13 @@
         [send(9 + 4 * steps + c, ring_src.at[part], ring_out.at[z, part], down)]
         for c, part in enumerate(chunks)
     ]
+
+    ready()
+    own_tree = pltpu.make_async_copy(tree_src, tree_out.at[me], local_sem.at[phase, 0])
+    own_tree.start()
+    first_right = send(0, tree_src, tree_out.at[me], to_right)
+    first_left = send(1, tree_src, tree_out.at[me], to_left)
+    first_other = send(2, tree_src, tree_out.at[me], to_other)
 
     def ring_step(s):
         below = lax.rem(z + nz - (s - 1), nz)
@@ -155,9 +157,16 @@
     fwd_down_one = send(kind + 6, ring_out.at[above], ring_out.at[above], on_z(-1))
     fwd_down_two = send(kind + 7, ring_out.at[above, split:], ring_out.at[above, split:], on_z(-2))
     ring = [up_one, down_one, up_two, down_two, fwd_up_one, fwd_up_two, fwd_down_one, fwd_down_two]
-    for copy in sends + [up_one, down_one, fwd_up_one, fwd_up_two, fwd_down_one, fwd_down_two]:
+    for copy in sends:
         copy.wait_recv()
-    return sends + ring, [own_tree, own_ring]
+    own_tree.wait()
+
+    def ring_landed():
+        for copy in (up_one, down_one, fwd_up_one, fwd_up_two, fwd_down_one, fwd_down_two):
+            copy.wait_recv()
+        own_ring.wait()
+
+    return sends + ring, ring_landed
 
 
 def gather_kernel(rows_ref, mid_ring, mid_tree, ring_out, tree_out, send_sem, recv_sem, local_sem):
@@ -172,10 +181,10 @@
     pl.semaphore_wait(barrier, len(peers))
     half = rows_ref.shape[0] // 2
     ring_src, tree_src = rows_ref.at[pl.ds(half, half)], rows_ref.at[pl.ds(0, half)]
-    sends, local = phase_one(ring_src, tree_src, mid_ring, mid_tree, send_sem, recv_sem, local_sem)
-    for copy in local:
-        copy.wait()
-    more, local = gather_phase(1, mid_tree, mid_ring, ring_out, tree_out, send_sem, recv_sem, local_sem)
+    sends, ring_landed = phase_one(ring_src, tree_src, mid_ring, mid_tree, send_sem, recv_sem, local_sem)
+    more, local = gather_phase(
+        1, mid_tree, mid_ring, ring_out, tree_out, send_sem, recv_sem, local_sem, ring_landed
+    )
     for copy in sends + more:
         copy.wait_send()
     for copy in local:

time: 173 us -> 172 us (level)
  Pallas kernels: 163 us -> 161 us
    pallas_call x2, Pallas kernels: 115 us -> 110 us  [gather_blk(): pl.pallas_call(gather_kernel, out_shape=(jax.ShapeDtypeStruct((nz, *piece...]
    pallas_call x2, Pallas kernels: 33.8 us -> 37 us  [reduce_rep(): pl.pallas_call(reduce_kernel, out_shape=jax.ShapeDtypeStruct(piece, piece...]
where the time goes in v22:
time: 172 us; the launch traced here: 169 us
  Pallas kernels  161 us (94%)
  matrix products  3.53 us (2%)
  other arithmetic  2.86 us (2%)
    pallas_call x2, Pallas kernels, gather_blk(): pl.pallas_call(gather_kernel, out_shape=(jax.ShapeDtypeStruct((nz, *piece...  110 us
    pallas_call x2, Pallas kernels, reduce_rep(): pl.pallas_call(reduce_kernel, out_shape=jax.ShapeDtypeStruct(piece, piece...  37 us
    pallas_call x2, Pallas kernels, tile_products(): pl.pallas_call(products_kernel, out_shape=jax.ShapeDtypeStruct((rows, BLO...  13.9 us

profile of v22, /device:TPU:9, one launch (start us, length us, event | category | flops | bytes accessed | tf_op | source)
XLA Modules:
  0.0 169.0 jit_solution(4304477076392085885)
XLA Ops:
  0.6 0.0 copy-start
  0.6 0.8 copy.10
  1.4 0.6 fusion.15.flag_ref
  2.0 0.6 select_add_fusion
  2.7 55.8 %shard_map.95 = (bf16[8,256,128]{2,1,0:T(8,128)(2,1)}, bf16[8,256,128]{2,1,0:T(8,128)(2,1)}, bf16[8,8,256,128]{3,2,1,0:T(8,128)(2,1)}, bf16[8,8,256,128]{3,2,1,0:T(8,128)(2,1)}) custom-call(bf16[512,128]{1,0:T(8,128)(2,1)} %rows_ref.1), custom_call_target="tpu_custom_call" | custom-call | tf_op jit(solution)/shard_map/pallas_call | solution.py:201
  58.4 0.0 copy-start.3
  58.5 0.0 copy-start.1
  58.5 0.0 copy-start.4
  58.5 0.0 copy-start.5
  58.5 6.9 %shard_map.96 = f32[16,128,128]{2,1,0:T(8,128)} custom-call(s32[16,4]{1,0:T(8,128)} %fusion.15.flag_ref, s32[16,4]{1,0:T(8,128)} %get-tuple-element.11.first_ref, s32[16,4]{1,0:T(8,128)} %get-tuple-element.10.second_ref, bf16[128,128,128]{2,1,0:T(8,128)(2,1)} %bitcast.92, bf16[128,128,128]{2,1,0:T(8,128)(2,1)} %bitcast.108, bf16[128,128,128]{2,1,0:T(8,128)(2,1)} %bitcast.79, ...), custom_call_target="tpu_custom_call" | custom-call | tf_op jit(solution)/shard_map/pallas_call | solution.py:328
  65.4 0.0 copy-start.2
  65.5 18.6 %shard_map.97 = f32[512,128]{1,0:T(8,128)} custom-call(f32[4,512,128]{2,1,0:T(8,128)} %bitcast.144), custom_call_target="tpu_custom_call" | custom-call | tf_op jit(solution)/shard_map/pallas_call | solution.py:269
  84.0 0.0 copy-done
  84.0 0.0 copy-done.3
  84.0 1.2 convolution_add_fusion
  85.3 0.0 copy-done.1
  85.3 0.0 copy-done.4
  85.3 0.0 copy-done.5
  85.3 1.1 fusion.5
  86.4 1.2 fusion.4.rows_ref
  87.6 54.4 %shard_map.98 = (bf16[8,256,128]{2,1,0:T(8,128)(2,1)}, bf16[8,256,128]{2,1,0:T(8,128)(2,1)}, bf16[8,8,256,128]{3,2,1,0:T(8,128)(2,1)}, bf16[8,8,256,128]{3,2,1,0:T(8,128)(2,1)}) custom-call(bf16[512,128]{1,0:T(8,128)(2,1)} %fusion.4.rows_ref), custom_call_target="tpu_custom_call" | custom-call | tf_op jit(solution)/shard_map/pallas_call | solution.py:201
  142.0 6.9 %shard_map.99 = f32[16,128,128]{2,1,0:T(8,128)} custom-call(s32[16,4]{1,0:T(8,128)} %fusion.15.flag_ref, s32[16,4]{1,0:T(8,128)} %get-tuple-element.11.first_ref, s32[16,4]{1,0:T(8,128)} %get-tuple-element.10.second_ref, bf16[128,128,128]{2,1,0:T(8,128)(2,1)} %bitcast.28, bf16[128,128,128]{2,1,0:T(8,128)(2,1)} %bitcast.44, bf16[128,128,128]{2,1,0:T(8,128)(2,1)} %bitcast.15, ...), custom_call_target="tpu_custom_call" | custom-call | tf_op jit(solution)/shard_map/pallas_call | solution.py:328
  148.9 18.4 %shard_map.100 = f32[512,128]{1,0:T(8,128)} custom-call(f32[4,512,128]{2,1,0:T(8,128)} %bitcast.143), custom_call_target="tpu_custom_call" | custom-call | tf_op jit(solution)/shard_map/pallas_call | solution.py:269
  167.3 1.6 add_convert_fusion
  (1 shorter events, 0.0 us)
Async XLA Ops:
  0.6 83.4 %copy-start = (bf16[128,512]{1,0:T(8,128)(2,1)S(1)}, bf16[128,512]{1,0:T(8,128)(2,1)}, u32[]{:S(2)}) copy-start(bf16[128,512]{1,0:T(8,128)(2,1)} %param.11) | copy-start | bytes 393220
  58.4 25.6 %copy-start.3 = (f32[512]{0:T(512)S(1)}, f32[512]{0:T(512)}, u32[]{:S(2)}) copy-start(f32[512]{0:T(512)} %param.12) | copy-start | bytes 6148
  58.5 26.8 %copy-start.1 = (bf16[512,128]{1,0:T(8,128)(2,1)S(1)}, bf16[512,128]{1,0:T(8,128)(2,1)}, u32[]{:S(2)}) copy-start(bf16[512,128]{1,0:T(8,128)(2,1)} %rows_ref.1) | copy-start | bytes 393220
  58.5 26.8 %copy-start.4 = (bf16[512,128]{1,0:T(8,128)(2,1)S(1)}, bf16[512,128]{1,0:T(8,128)(2,1)}, u32[]{:S(2)}) copy-start(bf16[512,128]{1,0:T(8,128)(2,1)} %param.13) | copy-start | bytes 393220
  58.5 26.8 %copy-start.5 = (f32[128]{0:T(128)S(1)}, f32[128]{0:T(128)}, u32[]{:S(2)}) copy-start(f32[128]{0:T(128)} %param.14) | copy-start | bytes 1540
  65.4 21.0 %copy-start.2 = (bf16[512,128]{1,0:T(8,128)(2,1)S(1)}, bf16[512,128]{1,0:T(8,128)(2,1)}, u32[]{:S(2)}) copy-start(bf16[512,128]{1,0:T(8,128)(2,1)} %param.15) | copy-start | bytes 393220

commit v23 on v22

--- a/solution.py
+++ b/solution.py
@@ -227,39 +227,44 @@
     for peer in (to_core, to_yhi):
         pl.semaphore_signal(barrier, 1, device_id=peer)
     pl.semaphore_wait(barrier, 2)
+    rows = last.shape[0] // 2
+    parts = (pl.ds(0, rows), pl.ds(rows, rows))
     copies, locals_ = [], []
-    for h in range(nyhi):
-        copy = pltpu.make_async_remote_copy(
-            src_ref=src_ref.at[h * ncore + other_core],
-            dst_ref=landed.at[h],
-            send_sem=send_sem.at[h],
-            recv_sem=recv_sem.at[h],
-            device_id=to_core,
+    for k, part in enumerate(parts):
+        for h in range(nyhi):
+            copy = pltpu.make_async_remote_copy(
+                src_ref=src_ref.at[h * ncore + other_core, part],
+                dst_ref=landed.at[h, part],
+                send_sem=send_sem.at[k, h],
+                recv_sem=recv_sem.at[k, h],
+                device_id=to_core,
+            )
+            copy.start()
+            copies.append(copy)
+            keep = pltpu.make_async_copy(src_ref.at[h * ncore + core, part], own.at[h, part], local_sem.at[k, h])
+            keep.start()
+            locals_.append(keep)
+    crosses = []
+    for k, part in enumerate(parts):
+        for h in range(nyhi):
+            copies[k * nyhi + h].wait_recv()
+            locals_[k * nyhi + h].wait()
+        mid[other_yhi, part] = own[other_yhi, part] + landed[other_yhi, part]
+        mid[yhi, part] = own[yhi, part] + landed[yhi, part]
+        cross = pltpu.make_async_remote_copy(
+            src_ref=mid.at[other_yhi, part],
+            dst_ref=last.at[part],
+            send_sem=send_sem.at[k, nyhi],
+            recv_sem=recv_sem.at[k, nyhi],
+            device_id=to_yhi,
         )
-        copy.start()
-        copies.append(copy)
-        keep = pltpu.make_async_copy(src_ref.at[h * ncore + core], own.at[h], local_sem.at[h])
-        keep.start()
-        locals_.append(keep)
-    for copy in copies:
-        copy.wait_recv()
-    for keep in locals_:
-        keep.wait()
-    mid[other_yhi] = own[other_yhi] + landed[other_yhi]
-    mid[yhi] = own[yhi] + landed[yhi]
-    cross = pltpu.make_async_remote_copy(
-        src_ref=mid.at[other_yhi],
-        dst_ref=last,
-        send_sem=send_sem.at[nyhi],
-        recv_sem=recv_sem.at[nyhi],
-        device_id=to_yhi,
-    )
-    cross.start()
-    cross.wait_recv()
-    out_ref[...] = mid[yhi] + last[...]
-    for copy in copies:
+        cross.start()
+        crosses.append(cross)
+    for k, part in enumerate(parts):
+        crosses[k].wait_recv()
+        out_ref[part] = mid[yhi, part] + last[part]
+    for copy in copies + crosses:
         copy.wait_send()
-    cross.wait_send()
 
 
 def reduce_rep(partial, cid):
@@ -276,9 +281,9 @@
             pltpu.VMEM((nyhi, *piece), pieces.dtype),
             pltpu.VMEM((nyhi, *piece), pieces.dtype),
             pltpu.VMEM(piece, pieces.dtype),
-            pltpu.SemaphoreType.DMA((nyhi + 1,)),
-            pltpu.SemaphoreType.DMA((nyhi + 1,)),
-            pltpu.SemaphoreType.DMA((nyhi,)),
+            pltpu.SemaphoreType.DMA((2, nyhi + 1)),
+            pltpu.SemaphoreType.DMA((2, nyhi + 1)),
+            pltpu.SemaphoreType.DMA((2, nyhi)),
         ],
         compiler_params=pltpu.CompilerParams(collective_id=cid, has_side_effects=True),
     )(pieces)

time: 172 us -> 172 us (level)
  no operation moved by 1% of the time
where the time goes in v23:
time: 172 us; the launch traced here: 170 us
  Pallas kernels  162 us (94%)
  matrix products  3.54 us (2%)
  other arithmetic  2.86 us (2%)
    pallas_call x2, Pallas kernels, gather_blk(): pl.pallas_call(gather_kernel, out_shape=(jax.ShapeDtypeStruct((nz, *piece...  110 us
    pallas_call x2, Pallas kernels, reduce_rep(): pl.pallas_call(reduce_kernel, out_shape=jax.ShapeDtypeStruct(piece, piece...  37.8 us
    pallas_call x2, Pallas kernels, tile_products(): pl.pallas_call(products_kernel, out_shape=jax.ShapeDtypeStruct((rows, BLO...  13.3 us

profile of v23, /device:TPU:9, one launch (start us, length us, event | category | flops | bytes accessed | tf_op | source)
XLA Modules:
  0.0 169.6 jit_solution(1995639808601416815)
XLA Ops:
  0.6 0.0 copy-start
  0.6 0.8 copy.10
  1.4 0.6 fusion.15.flag_ref
  2.0 0.6 select_add_fusion
  2.7 55.8 %shard_map.95 = (bf16[8,256,128]{2,1,0:T(8,128)(2,1)}, bf16[8,256,128]{2,1,0:T(8,128)(2,1)}, bf16[8,8,256,128]{3,2,1,0:T(8,128)(2,1)}, bf16[8,8,256,128]{3,2,1,0:T(8,128)(2,1)}) custom-call(bf16[512,128]{1,0:T(8,128)(2,1)} %rows_ref.1), custom_call_target="tpu_custom_call" | custom-call | tf_op jit(solution)/shard_map/pallas_call | solution.py:201
  58.4 0.0 copy-start.3
  58.5 0.0 copy-start.1
  58.5 0.0 copy-start.4
  58.5 0.0 copy-start.5
  58.5 6.7 %shard_map.96 = f32[16,128,128]{2,1,0:T(8,128)} custom-call(s32[16,4]{1,0:T(8,128)} %fusion.15.flag_ref, s32[16,4]{1,0:T(8,128)} %get-tuple-element.11.first_ref, s32[16,4]{1,0:T(8,128)} %get-tuple-element.10.second_ref, bf16[128,128,128]{2,1,0:T(8,128)(2,1)} %bitcast.92, bf16[128,128,128]{2,1,0:T(8,128)(2,1)} %bitcast.108, bf16[128,128,128]{2,1,0:T(8,128)(2,1)} %bitcast.79, ...), custom_call_target="tpu_custom_call" | custom-call | tf_op jit(solution)/shard_map/pallas_call | solution.py:333
  65.2 0.0 copy-start.2
  65.2 19.0 %shard_map.97 = f32[512,128]{1,0:T(8,128)} custom-call(f32[4,512,128]{2,1,0:T(8,128)} %bitcast.144), custom_call_target="tpu_custom_call" | custom-call | tf_op jit(solution)/shard_map/pallas_call | solution.py:274
  84.2 0.0 copy-done
  84.2 0.0 copy-done.3
  84.2 1.2 convolution_add_fusion
  85.4 0.0 copy-done.1
  85.5 0.0 copy-done.4
  85.5 1.1 fusion.5
  86.6 0.0 copy-done.2
  86.6 1.2 fusion.4.rows_ref
  87.8 54.7 %shard_map.98 = (bf16[8,256,128]{2,1,0:T(8,128)(2,1)}, bf16[8,256,128]{2,1,0:T(8,128)(2,1)}, bf16[8,8,256,128]{3,2,1,0:T(8,128)(2,1)}, bf16[8,8,256,128]{3,2,1,0:T(8,128)(2,1)}) custom-call(bf16[512,128]{1,0:T(8,128)(2,1)} %fusion.4.rows_ref), custom_call_target="tpu_custom_call" | custom-call | tf_op jit(solution)/shard_map/pallas_call | solution.py:201
  142.5 6.7 %shard_map.99 = f32[16,128,128]{2,1,0:T(8,128)} custom-call(s32[16,4]{1,0:T(8,128)} %fusion.15.flag_ref, s32[16,4]{1,0:T(8,128)} %get-tuple-element.11.first_ref, s32[16,4]{1,0:T(8,128)} %get-tuple-element.10.second_ref, bf16[128,128,128]{2,1,0:T(8,128)(2,1)} %bitcast.28, bf16[128,128,128]{2,1,0:T(8,128)(2,1)} %bitcast.44, bf16[128,128,128]{2,1,0:T(8,128)(2,1)} %bitcast.15, ...), custom_call_target="tpu_custom_call" | custom-call | tf_op jit(solution)/shard_map/pallas_call | solution.py:333
  149.1 18.8 %shard_map.100 = f32[512,128]{1,0:T(8,128)} custom-call(f32[4,512,128]{2,1,0:T(8,128)} %bitcast.143), custom_call_target="tpu_custom_call" | custom-call | tf_op jit(solution)/shard_map/pallas_call | solution.py:274
  167.9 1.6 add_convert_fusion
  (1 shorter events, 0.0 us)
Async XLA Ops:
  0.6 83.6 %copy-start = (bf16[128,512]{1,0:T(8,128)(2,1)S(1)}, bf16[128,512]{1,0:T(8,128)(2,1)}, u32[]{:S(2)}) copy-start(bf16[128,512]{1,0:T(8,128)(2,1)} %param.11) | copy-start | bytes 393220
  58.4 25.8 %copy-start.3 = (f32[512]{0:T(512)S(1)}, f32[512]{0:T(512)}, u32[]{:S(2)}) copy-start(f32[512]{0:T(512)} %param.12) | copy-start | bytes 6148
  58.5 27.0 %copy-start.1 = (bf16[512,128]{1,0:T(8,128)(2,1)S(1)}, bf16[512,128]{1,0:T(8,128)(2,1)}, u32[]{:S(2)}) copy-start(bf16[512,128]{1,0:T(8,128)(2,1)} %rows_ref.1) | copy-start | bytes 393220
  58.5 27.0 %copy-start.4 = (bf16[512,128]{1,0:T(8,128)(2,1)S(1)}, bf16[512,128]{1,0:T(8,128)(2,1)}, u32[]{:S(2)}) copy-start(bf16[512,128]{1,0:T(8,128)(2,1)} %param.13) | copy-start | bytes 393220
  58.5 27.0 %copy-start.5 = (f32[128]{0:T(128)S(1)}, f32[128]{0:T(128)}, u32[]{:S(2)}) copy-start(f32[128]{0:T(128)} %param.14) | copy-start | bytes 1540
  65.2 21.4 %copy-start.2 = (bf16[512,128]{1,0:T(8,128)(2,1)S(1)}, bf16[512,128]{1,0:T(8,128)(2,1)}, u32[]{:S(2)}) copy-start(bf16[512,128]{1,0:T(8,128)(2,1)} %param.15) | copy-start | bytes 393220

commit v24 on v23

--- a/solution.py
+++ b/solution.py
@@ -71,7 +71,13 @@
     own_tree.start()
     first_right = send(0, tree_src, tree_out.at[me], to_right)
     first_left = send(1, tree_src, tree_out.at[me], to_left)
-    first_other = send(2, tree_src, tree_out.at[me], to_other)
+    tree_split = tree_src.shape[0] // 2
+    tree_parts = (pl.ds(0, tree_split), pl.ds(tree_split, tree_split))
+    extra = 9 + 4 * nz
+    first_other = [
+        send(2 if c == 0 else extra, tree_src.at[part], tree_out.at[me, part], to_other)
+        for c, part in enumerate(tree_parts)
+    ]
 
     def ring_step(s):
         below = lax.rem(z + nz - (s - 1), nz)
@@ -86,7 +92,6 @@
                     send(9 + 4 * steps + 2 * (s - 1) + c, ring_out.at[above, part], ring_out.at[above, part], down)
                 )
 
-    tree_split = tree_src.shape[0] // 2
     first_right.wait_recv()
     from_left = left * ny + y
     second_right = send(3, tree_out.at[from_left, :tree_split], tree_out.at[from_left, :tree_split], to_right)
@@ -94,17 +99,20 @@
     from_right = right * ny + y
     second_left = send(7, tree_out.at[from_right, tree_split:], tree_out.at[from_right, tree_split:], to_left)
     ring_step(2)
-    first_other.wait_recv()
     from_other = x * ny + other
-    other_right = send(4, tree_out.at[from_other], tree_out.at[from_other], to_right)
-    other_left = send(5, tree_out.at[from_other], tree_out.at[from_other], to_left)
+    other_right, other_left = [], []
+    for c, part in enumerate(tree_parts):
+        first_other[c].wait_recv()
+        src = tree_out.at[from_other, part]
+        other_right.append(send(4 if c == 0 else extra + 1, src, src, to_right))
+        other_left.append(send(5 if c == 0 else extra + 2, src, src, to_left))
     ring_step(3)
-    other_right.wait_recv()
+    other_right[0].wait_recv()
     from_left_other = left * ny + other
     third_right = send(
         6, tree_out.at[from_left_other, :tree_split], tree_out.at[from_left_other, :tree_split], to_right
     )
-    other_left.wait_recv()
+    other_left[1].wait_recv()
     from_right_other = right * ny + other
     third_left = send(
         8, tree_out.at[from_right_other, tree_split:], tree_out.at[from_right_other, tree_split:], to_left
@@ -113,8 +121,10 @@
         ring_step(s)
     for copy in (second_right, second_left, third_right, third_left, ups[0][-1], downs[1][-1]):
         copy.wait_recv()
-    tree = [first_right, first_left, first_other, second_right, second_left]
-    tree += [other_right, other_left, third_right, third_left]
+    other_right[1].wait_recv()
+    other_left[0].wait_recv()
+    tree = [first_right, first_left, *first_other, second_right, second_left]
+    tree += [*other_right, *other_left, third_right, third_left]
     return tree + ups[0] + ups[1] + downs[0] + downs[1], [own_tree, own_ring]
 
 
@@ -209,8 +219,8 @@
         in_specs=[any_space],
         out_specs=(any_space,) * 4,
         scratch_shapes=[
-            pltpu.SemaphoreType.DMA((2, 9 + 4 * nz)),
-            pltpu.SemaphoreType.DMA((2, 9 + 4 * nz)),
+            pltpu.SemaphoreType.DMA((2, 12 + 4 * nz)),
+            pltpu.SemaphoreType.DMA((2, 12 + 4 * nz)),
             pltpu.SemaphoreType.DMA((2, 2)),
         ],
         compiler_params=pltpu.CompilerParams(collective_id=cid, has_side_effects=True),

time: 172 us -> 172 us (level)
    pallas_call x2, Pallas kernels: 110 us -> 113 us  [gather_blk(): pl.pallas_call(gather_kernel, out_shape=(jax.ShapeDtypeStruct((nz, *piece...]
    pallas_call x2, Pallas kernels: 37.8 us -> 36 us  [reduce_rep(): pl.pallas_call(reduce_kernel, out_shape=jax.ShapeDtypeStruct(piece, piece...]
where the time goes in v24:
time: 172 us; the launch traced here: 170 us
  Pallas kernels  162 us (94%)
  matrix products  3.53 us (2%)
  other arithmetic  2.86 us (2%)
    pallas_call x2, Pallas kernels, gather_blk(): pl.pallas_call(gather_kernel, out_shape=(jax.ShapeDtypeStruct((nz, *piece...  113 us
    pallas_call x2, Pallas kernels, reduce_rep(): pl.pallas_call(reduce_kernel, out_shape=jax.ShapeDtypeStruct(piece, piece...  36 us
    pallas_call x2, Pallas kernels, tile_products(): pl.pallas_call(products_kernel, out_shape=jax.ShapeDtypeStruct((rows, BLO...  13.2 us

profile of v24, /device:TPU:9, one launch (start us, length us, event | category | flops | bytes accessed | tf_op | source)
XLA Modules:
  0.0 170.4 jit_solution(8736189726385569226)
XLA Ops:
  0.6 0.0 copy-start
  0.6 0.8 copy.10
  1.4 0.6 fusion.15.flag_ref
  2.0 0.6 select_add_fusion
  2.7 55.9 %shard_map.95 = (bf16[8,256,128]{2,1,0:T(8,128)(2,1)}, bf16[8,256,128]{2,1,0:T(8,128)(2,1)}, bf16[8,8,256,128]{3,2,1,0:T(8,128)(2,1)}, bf16[8,8,256,128]{3,2,1,0:T(8,128)(2,1)}) custom-call(bf16[512,128]{1,0:T(8,128)(2,1)} %rows_ref.1), custom_call_target="tpu_custom_call" | custom-call | tf_op jit(solution)/shard_map/pallas_call | solution.py:211
  58.6 0.0 copy-start.3
  58.6 0.0 copy-start.1
  58.6 0.0 copy-start.4
  58.6 0.0 copy-start.5
  58.6 6.6 %shard_map.96 = f32[16,128,128]{2,1,0:T(8,128)} custom-call(s32[16,4]{1,0:T(8,128)} %fusion.15.flag_ref, s32[16,4]{1,0:T(8,128)} %get-tuple-element.11.first_ref, s32[16,4]{1,0:T(8,128)} %get-tuple-element.10.second_ref, bf16[128,128,128]{2,1,0:T(8,128)(2,1)} %bitcast.92, bf16[128,128,128]{2,1,0:T(8,128)(2,1)} %bitcast.108, bf16[128,128,128]{2,1,0:T(8,128)(2,1)} %bitcast.79, ...), custom_call_target="tpu_custom_call" | custom-call | tf_op jit(solution)/shard_map/pallas_call | solution.py:343
  65.2 0.0 copy-start.2
  65.2 19.1 %shard_map.97 = f32[512,128]{1,0:T(8,128)} custom-call(f32[4,512,128]{2,1,0:T(8,128)} %bitcast.144), custom_call_target="tpu_custom_call" | custom-call | tf_op jit(solution)/shard_map/pallas_call | solution.py:284
  84.3 0.0 copy-done
  84.3 0.0 copy-done.3
  84.3 1.2 convolution_add_fusion
  85.6 0.0 copy-done.1
  85.6 0.0 copy-done.4
  85.6 1.1 fusion.5
  86.7 0.0 copy-done.2
  86.7 1.2 fusion.4.rows_ref
  87.9 57.3 %shard_map.98 = (bf16[8,256,128]{2,1,0:T(8,128)(2,1)}, bf16[8,256,128]{2,1,0:T(8,128)(2,1)}, bf16[8,8,256,128]{3,2,1,0:T(8,128)(2,1)}, bf16[8,8,256,128]{3,2,1,0:T(8,128)(2,1)}) custom-call(bf16[512,128]{1,0:T(8,128)(2,1)} %fusion.4.rows_ref), custom_call_target="tpu_custom_call" | custom-call | tf_op jit(solution)/shard_map/pallas_call | solution.py:211
  145.3 6.6 %shard_map.99 = f32[16,128,128]{2,1,0:T(8,128)} custom-call(s32[16,4]{1,0:T(8,128)} %fusion.15.flag_ref, s32[16,4]{1,0:T(8,128)} %get-tuple-element.11.first_ref, s32[16,4]{1,0:T(8,128)} %get-tuple-element.10.second_ref, bf16[128,128,128]{2,1,0:T(8,128)(2,1)} %bitcast.28, bf16[128,128,128]{2,1,0:T(8,128)(2,1)} %bitcast.44, bf16[128,128,128]{2,1,0:T(8,128)(2,1)} %bitcast.15, ...), custom_call_target="tpu_custom_call" | custom-call | tf_op jit(solution)/shard_map/pallas_call | solution.py:343
  151.9 16.9 %shard_map.100 = f32[512,128]{1,0:T(8,128)} custom-call(f32[4,512,128]{2,1,0:T(8,128)} %bitcast.143), custom_call_target="tpu_custom_call" | custom-call | tf_op jit(solution)/shard_map/pallas_call | solution.py:284
  168.8 1.6 add_convert_fusion
  (1 shorter events, 0.0 us)
Async XLA Ops:
  0.6 83.7 %copy-start = (bf16[128,512]{1,0:T(8,128)(2,1)S(1)}, bf16[128,512]{1,0:T(8,128)(2,1)}, u32[]{:S(2)}) copy-start(bf16[128,512]{1,0:T(8,128)(2,1)} %param.11) | copy-start | bytes 393220
  58.6 25.8 %copy-start.3 = (f32[512]{0:T(512)S(1)}, f32[512]{0:T(512)}, u32[]{:S(2)}) copy-start(f32[512]{0:T(512)} %param.12) | copy-start | bytes 6148
  58.6 27.0 %copy-start.1 = (bf16[512,128]{1,0:T(8,128)(2,1)S(1)}, bf16[512,128]{1,0:T(8,128)(2,1)}, u32[]{:S(2)}) copy-start(bf16[512,128]{1,0:T(8,128)(2,1)} %rows_ref.1) | copy-start | bytes 393220
  58.6 27.0 %copy-start.4 = (bf16[512,128]{1,0:T(8,128)(2,1)S(1)}, bf16[512,128]{1,0:T(8,128)(2,1)}, u32[]{:S(2)}) copy-start(bf16[512,128]{1,0:T(8,128)(2,1)} %param.13) | copy-start | bytes 393220
  58.6 27.0 %copy-start.5 = (f32[128]{0:T(128)S(1)}, f32[128]{0:T(128)}, u32[]{:S(2)}) copy-start(f32[128]{0:T(128)} %param.14) | copy-start | bytes 1540
  65.2 21.5 %copy-start.2 = (bf16[512,128]{1,0:T(8,128)(2,1)S(1)}, bf16[512,128]{1,0:T(8,128)(2,1)}, u32[]{:S(2)}) copy-start(bf16[512,128]{1,0:T(8,128)(2,1)} %param.15) | copy-start | bytes 393220

commit v25 on v23

--- a/solution.py
+++ b/solution.py
@@ -69,9 +69,16 @@
     ready()
     own_tree = pltpu.make_async_copy(tree_src, tree_out.at[me], local_sem.at[phase, 0])
     own_tree.start()
-    first_right = send(0, tree_src, tree_out.at[me], to_right)
-    first_left = send(1, tree_src, tree_out.at[me], to_left)
-    first_other = send(2, tree_src, tree_out.at[me], to_other)
+    quarter = tree_src.shape[0] // 4
+    p_all, p_lo, p_hi = pl.ds(0, 2 * quarter), pl.ds(0, quarter), pl.ds(quarter, quarter)
+    q_all, q_lo, q_hi = pl.ds(2 * quarter, 2 * quarter), pl.ds(2 * quarter, quarter), pl.ds(3 * quarter, quarter)
+    extra = 9 + 4 * nz
+    first_right = send(0, tree_src.at[p_all], tree_out.at[me, p_all], to_right)
+    first_left = send(1, tree_src.at[p_all], tree_out.at[me, p_all], to_left)
+    first_other = send(2, tree_src.at[p_all], tree_out.at[me, p_all], to_other)
+    q_right = send(extra, tree_src.at[q_all], tree_out.at[me, q_all], to_right)
+    q_left = send(extra + 1, tree_src.at[q_all], tree_out.at[me, q_all], to_left)
+    q_own = send(extra + 2, tree_src.at[q_all], tree_out.at[me, q_all], to_other)
 
     def ring_step(s):
         below = lax.rem(z + nz - (s - 1), nz)
@@ -86,35 +93,43 @@
                     send(9 + 4 * steps + 2 * (s - 1) + c, ring_out.at[above, part], ring_out.at[above, part], down)
                 )
 
-    tree_split = tree_src.shape[0] // 2
     first_right.wait_recv()
     from_left = left * ny + y
-    second_right = send(3, tree_out.at[from_left, :tree_split], tree_out.at[from_left, :tree_split], to_right)
+    second_right = send(3, tree_out.at[from_left, p_lo], tree_out.at[from_left, p_lo], to_right)
+    q_right.wait_recv()
+    q_second_right = send(extra + 3, tree_out.at[from_left, q_lo], tree_out.at[from_left, q_lo], to_right)
+    q_from_left = send(extra + 4, tree_out.at[from_left, q_all], tree_out.at[from_left, q_all], to_other)
     first_left.wait_recv()
     from_right = right * ny + y
-    second_left = send(7, tree_out.at[from_right, tree_split:], tree_out.at[from_right, tree_split:], to_left)
+    second_left = send(7, tree_out.at[from_right, p_hi], tree_out.at[from_right, p_hi], to_left)
+    q_left.wait_recv()
+    q_second_left = send(extra + 5, tree_out.at[from_right, q_hi], tree_out.at[from_right, q_hi], to_left)
+    q_from_right = send(extra + 6, tree_out.at[from_right, q_all], tree_out.at[from_right, q_all], to_other)
     ring_step(2)
     first_other.wait_recv()
     from_other = x * ny + other
-    other_right = send(4, tree_out.at[from_other], tree_out.at[from_other], to_right)
-    other_left = send(5, tree_out.at[from_other], tree_out.at[from_other], to_left)
+    other_right = send(4, tree_out.at[from_other, p_all], tree_out.at[from_other, p_all], to_right)
+    other_left = send(5, tree_out.at[from_other, p_all], tree_out.at[from_other, p_all], to_left)
     ring_step(3)
     other_right.wait_recv()
     from_left_other = left * ny + other
-    third_right = send(
-        6, tree_out.at[from_left_other, :tree_split], tree_out.at[from_left_other, :tree_split], to_right
-    )
+    third_right = send(6, tree_out.at[from_left_other, p_lo], tree_out.at[from_left_other, p_lo], to_right)
     other_left.wait_recv()
     from_right_other = right * ny + other
-    third_left = send(
-        8, tree_out.at[from_right_other, tree_split:], tree_out.at[from_right_other, tree_split:], to_left
-    )
+    third_left = send(8, tree_out.at[from_right_other, p_hi], tree_out.at[from_right_other, p_hi], to_left)
+    q_second_right.wait_recv()
+    q_second_left.wait_recv()
+    from_far = lax.rem(x + 2, nx) * ny + y
+    q_from_far = send(extra + 7, tree_out.at[from_far, q_all], tree_out.at[from_far, q_all], to_other)
     for s in range(4, steps + 1):
         ring_step(s)
     for copy in (second_right, second_left, third_right, third_left, ups[0][-1], downs[1][-1]):
         copy.wait_recv()
+    for copy in (q_own, q_from_left, q_from_right, q_from_far):
+        copy.wait_recv()
     tree = [first_right, first_left, first_other, second_right, second_left]
     tree += [other_right, other_left, third_right, third_left]
+    tree += [q_right, q_left, q_own, q_second_right, q_from_left, q_second_left, q_from_right, q_from_far]
     return tree + ups[0] + ups[1] + downs[0] + downs[1], [own_tree, own_ring]
 
 
@@ -209,8 +224,8 @@
         in_specs=[any_space],
         out_specs=(any_space,) * 4,
         scratch_shapes=[
-            pltpu.SemaphoreType.DMA((2, 9 + 4 * nz)),
-            pltpu.SemaphoreType.DMA((2, 9 + 4 * nz)),
+            pltpu.SemaphoreType.DMA((2, 17 + 4 * nz)),
+            pltpu.SemaphoreType.DMA((2, 17 + 4 * nz)),
             pltpu.SemaphoreType.DMA((2, 2)),
         ],
         compiler_params=pltpu.CompilerParams(collective_id=cid, has_side_effects=True),

time: 172 us -> 172 us (level)
  no operation moved by 1% of the time
where the time goes in v25:
time: 172 us; the launch traced here: 170 us
  Pallas kernels  162 us (94%)
  matrix products  3.53 us (2%)
  other arithmetic  2.86 us (2%)
    pallas_call x2, Pallas kernels, gather_blk(): pl.pallas_call(gather_kernel, out_shape=(jax.ShapeDtypeStruct((nz, *piece...  110 us
    pallas_call x2, Pallas kernels, reduce_rep(): pl.pallas_call(reduce_kernel, out_shape=jax.ShapeDtypeStruct(piece, piece...  38.5 us
    pallas_call x2, Pallas kernels, tile_products(): pl.pallas_call(products_kernel, out_shape=jax.ShapeDtypeStruct((rows, BLO...  13.2 us

profile of v25, /device:TPU:9, one launch (start us, length us, event | category | flops | bytes accessed | tf_op | source)
XLA Modules:
  0.0 169.8 jit_solution(5648445457303112903)
XLA Ops:
  0.6 0.0 copy-start
  0.6 0.8 copy.10
  1.4 0.6 fusion.15.flag_ref
  2.0 0.6 select_add_fusion
  2.7 56.0 %shard_map.95 = (bf16[8,256,128]{2,1,0:T(8,128)(2,1)}, bf16[8,256,128]{2,1,0:T(8,128)(2,1)}, bf16[8,8,256,128]{3,2,1,0:T(8,128)(2,1)}, bf16[8,8,256,128]{3,2,1,0:T(8,128)(2,1)}) custom-call(bf16[512,128]{1,0:T(8,128)(2,1)} %rows_ref.1), custom_call_target="tpu_custom_call" | custom-call | tf_op jit(solution)/shard_map/pallas_call | solution.py:216
  58.7 0.0 copy-start.3
  58.7 0.0 copy-start.1
  58.7 0.0 copy-start.4
  58.7 0.0 copy-start.5
  58.7 6.6 %shard_map.96 = f32[16,128,128]{2,1,0:T(8,128)} custom-call(s32[16,4]{1,0:T(8,128)} %fusion.15.flag_ref, s32[16,4]{1,0:T(8,128)} %get-tuple-element.11.first_ref, s32[16,4]{1,0:T(8,128)} %get-tuple-element.10.second_ref, bf16[128,128,128]{2,1,0:T(8,128)(2,1)} %bitcast.92, bf16[128,128,128]{2,1,0:T(8,128)(2,1)} %bitcast.108, bf16[128,128,128]{2,1,0:T(8,128)(2,1)} %bitcast.79, ...), custom_call_target="tpu_custom_call" | custom-call | tf_op jit(solution)/shard_map/pallas_call | solution.py:348
  65.4 0.0 copy-start.2
  65.4 19.1 %shard_map.97 = f32[512,128]{1,0:T(8,128)} custom-call(f32[4,512,128]{2,1,0:T(8,128)} %bitcast.144), custom_call_target="tpu_custom_call" | custom-call | tf_op jit(solution)/shard_map/pallas_call | solution.py:289
  84.5 0.0 copy-done
  84.5 0.0 copy-done.3
  84.5 1.2 convolution_add_fusion
  85.8 0.0 copy-done.1
  85.8 0.0 copy-done.4
  85.8 0.0 copy-done.5
  85.8 1.1 fusion.5
  86.9 1.2 fusion.4.rows_ref
  88.1 54.1 %shard_map.98 = (bf16[8,256,128]{2,1,0:T(8,128)(2,1)}, bf16[8,256,128]{2,1,0:T(8,128)(2,1)}, bf16[8,8,256,128]{3,2,1,0:T(8,128)(2,1)}, bf16[8,8,256,128]{3,2,1,0:T(8,128)(2,1)}) custom-call(bf16[512,128]{1,0:T(8,128)(2,1)} %fusion.4.rows_ref), custom_call_target="tpu_custom_call" | custom-call | tf_op jit(solution)/shard_map/pallas_call | solution.py:216
  142.2 6.6 %shard_map.99 = f32[16,128,128]{2,1,0:T(8,128)} custom-call(s32[16,4]{1,0:T(8,128)} %fusion.15.flag_ref, s32[16,4]{1,0:T(8,128)} %get-tuple-element.11.first_ref, s32[16,4]{1,0:T(8,128)} %get-tuple-element.10.second_ref, bf16[128,128,128]{2,1,0:T(8,128)(2,1)} %bitcast.28, bf16[128,128,128]{2,1,0:T(8,128)(2,1)} %bitcast.44, bf16[128,128,128]{2,1,0:T(8,128)(2,1)} %bitcast.15, ...), custom_call_target="tpu_custom_call" | custom-call | tf_op jit(solution)/shard_map/pallas_call | solution.py:348
  148.8 19.3 %shard_map.100 = f32[512,128]{1,0:T(8,128)} custom-call(f32[4,512,128]{2,1,0:T(8,128)} %bitcast.143), custom_call_target="tpu_custom_call" | custom-call | tf_op jit(solution)/shard_map/pallas_call | solution.py:289
  168.1 1.6 add_convert_fusion
  (1 shorter events, 0.0 us)
Async XLA Ops:
  0.6 83.9 %copy-start = (bf16[128,512]{1,0:T(8,128)(2,1)S(1)}, bf16[128,512]{1,0:T(8,128)(2,1)}, u32[]{:S(2)}) copy-start(bf16[128,512]{1,0:T(8,128)(2,1)} %param.11) | copy-start | bytes 393220
  58.7 25.8 %copy-start.3 = (f32[512]{0:T(512)S(1)}, f32[512]{0:T(512)}, u32[]{:S(2)}) copy-start(f32[512]{0:T(512)} %param.12) | copy-start | bytes 6148
  58.7 27.0 %copy-start.1 = (bf16[512,128]{1,0:T(8,128)(2,1)S(1)}, bf16[512,128]{1,0:T(8,128)(2,1)}, u32[]{:S(2)}) copy-start(bf16[512,128]{1,0:T(8,128)(2,1)} %rows_ref.1) | copy-start | bytes 393220
  58.7 27.0 %copy-start.4 = (bf16[512,128]{1,0:T(8,128)(2,1)S(1)}, bf16[512,128]{1,0:T(8,128)(2,1)}, u32[]{:S(2)}) copy-start(bf16[512,128]{1,0:T(8,128)(2,1)} %param.13) | copy-start | bytes 393220
  58.7 27.0 %copy-start.5 = (f32[128]{0:T(128)S(1)}, f32[128]{0:T(128)}, u32[]{:S(2)}) copy-start(f32[128]{0:T(128)} %param.14) | copy-start | bytes 1540
  65.4 21.5 %copy-start.2 = (bf16[512,128]{1,0:T(8,128)(2,1)S(1)}, bf16[512,128]{1,0:T(8,128)(2,1)}, u32[]{:S(2)}) copy-start(bf16[512,128]{1,0:T(8,128)(2,1)} %param.15) | copy-start | bytes 393220

commit v26 on v23

--- a/solution.py
+++ b/solution.py
@@ -138,15 +138,15 @@
     own_ring = pltpu.make_async_copy(ring_src, ring_out.at[z], local_sem.at[0, 1])
     own_ring.start()
     n = nx * ny
+    kind = n - 1
+    up_two = send(kind + 2, ring_src, ring_out.at[z], on_z(2))
+    down_two = send(kind + 3, ring_src, ring_out.at[z], on_z(-2))
+    up_one = send(kind, ring_src, ring_out.at[z], on_z(1))
+    down_one = send(kind + 1, ring_src, ring_out.at[z], on_z(-1))
     sends = []
     for d in range(1, n):
         p = lax.rem(me + d, n)
         sends.append(send(d - 1, tree_src, tree_out.at[me], {"x": p // ny, "ylo": p % ny}))
-    kind = n - 1
-    up_one = send(kind, ring_src, ring_out.at[z], on_z(1))
-    down_one = send(kind + 1, ring_src, ring_out.at[z], on_z(-1))
-    up_two = send(kind + 2, ring_src, ring_out.at[z], on_z(2))
-    down_two = send(kind + 3, ring_src, ring_out.at[z], on_z(-2))
     split = ring_src.shape[0] // 2
     up_two.wait_recv()
     below = lax.rem(z + nz - 2, nz)

time: 172 us -> 169 us (0.983); the launches traced: 170 us -> 169 us
  no operation moved by 1% of the time
where the time goes in v26:
time: 169 us
  Pallas kernels  161 us (95%)
  matrix products  3.54 us (2%)
  other arithmetic  2.86 us (2%)
    pallas_call x2, Pallas kernels, gather_blk(): pl.pallas_call(gather_kernel, out_shape=(jax.ShapeDtypeStruct((nz, *piece...  110 us
    pallas_call x2, Pallas kernels, reduce_rep(): pl.pallas_call(reduce_kernel, out_shape=jax.ShapeDtypeStruct(piece, piece...  37.2 us
    pallas_call x2, Pallas kernels, tile_products(): pl.pallas_call(products_kernel, out_shape=jax.ShapeDtypeStruct((rows, BLO...  13.3 us

profile of v26, /device:TPU:9, one launch (start us, length us, event | category | flops | bytes accessed | tf_op | source)
XLA Modules:
  0.0 168.9 jit_solution(6247027665879693537)
XLA Ops:
  0.6 0.0 copy-start
  0.6 0.8 copy.10
  1.4 0.6 fusion.15.flag_ref
  2.0 0.6 select_add_fusion
  2.7 56.0 %shard_map.95 = (bf16[8,256,128]{2,1,0:T(8,128)(2,1)}, bf16[8,256,128]{2,1,0:T(8,128)(2,1)}, bf16[8,8,256,128]{3,2,1,0:T(8,128)(2,1)}, bf16[8,8,256,128]{3,2,1,0:T(8,128)(2,1)}) custom-call(bf16[512,128]{1,0:T(8,128)(2,1)} %rows_ref.1), custom_call_target="tpu_custom_call" | custom-call | tf_op jit(solution)/shard_map/pallas_call | solution.py:201
  58.7 0.0 copy-start.3
  58.7 0.0 copy-start.1
  58.7 0.0 copy-start.4
  58.7 0.0 copy-start.5
  58.7 6.7 %shard_map.96 = f32[16,128,128]{2,1,0:T(8,128)} custom-call(s32[16,4]{1,0:T(8,128)} %fusion.15.flag_ref, s32[16,4]{1,0:T(8,128)} %get-tuple-element.11.first_ref, s32[16,4]{1,0:T(8,128)} %get-tuple-element.10.second_ref, bf16[128,128,128]{2,1,0:T(8,128)(2,1)} %bitcast.92, bf16[128,128,128]{2,1,0:T(8,128)(2,1)} %bitcast.108, bf16[128,128,128]{2,1,0:T(8,128)(2,1)} %bitcast.79, ...), custom_call_target="tpu_custom_call" | custom-call | tf_op jit(solution)/shard_map/pallas_call | solution.py:333
  65.4 0.0 copy-start.2
  65.4 17.9 %shard_map.97 = f32[512,128]{1,0:T(8,128)} custom-call(f32[4,512,128]{2,1,0:T(8,128)} %bitcast.144), custom_call_target="tpu_custom_call" | custom-call | tf_op jit(solution)/shard_map/pallas_call | solution.py:274
  83.3 0.0 copy-done
  83.3 0.0 copy-done.3
  83.4 1.2 convolution_add_fusion
  84.6 0.0 copy-done.1
  84.6 0.0 copy-done.4
  84.6 1.1 fusion.5
  85.7 0.0 copy-done.2
  85.7 1.2 fusion.4.rows_ref
  86.9 54.4 %shard_map.98 = (bf16[8,256,128]{2,1,0:T(8,128)(2,1)}, bf16[8,256,128]{2,1,0:T(8,128)(2,1)}, bf16[8,8,256,128]{3,2,1,0:T(8,128)(2,1)}, bf16[8,8,256,128]{3,2,1,0:T(8,128)(2,1)}) custom-call(bf16[512,128]{1,0:T(8,128)(2,1)} %fusion.4.rows_ref), custom_call_target="tpu_custom_call" | custom-call | tf_op jit(solution)/shard_map/pallas_call | solution.py:201
  141.3 6.7 %shard_map.99 = f32[16,128,128]{2,1,0:T(8,128)} custom-call(s32[16,4]{1,0:T(8,128)} %fusion.15.flag_ref, s32[16,4]{1,0:T(8,128)} %get-tuple-element.11.first_ref, s32[16,4]{1,0:T(8,128)} %get-tuple-element.10.second_ref, bf16[128,128,128]{2,1,0:T(8,128)(2,1)} %bitcast.28, bf16[128,128,128]{2,1,0:T(8,128)(2,1)} %bitcast.44, bf16[128,128,128]{2,1,0:T(8,128)(2,1)} %bitcast.15, ...), custom_call_target="tpu_custom_call" | custom-call | tf_op jit(solution)/shard_map/pallas_call | solution.py:333
  148.0 19.2 %shard_map.100 = f32[512,128]{1,0:T(8,128)} custom-call(f32[4,512,128]{2,1,0:T(8,128)} %bitcast.143), custom_call_target="tpu_custom_call" | custom-call | tf_op jit(solution)/shard_map/pallas_call | solution.py:274
  167.2 1.6 add_convert_fusion
  (1 shorter events, 0.0 us)
Async XLA Ops:
  0.6 82.7 %copy-start = (bf16[128,512]{1,0:T(8,128)(2,1)S(1)}, bf16[128,512]{1,0:T(8,128)(2,1)}, u32[]{:S(2)}) copy-start(bf16[128,512]{1,0:T(8,128)(2,1)} %param.11) | copy-start | bytes 393220
  58.7 24.7 %copy-start.3 = (f32[512]{0:T(512)S(1)}, f32[512]{0:T(512)}, u32[]{:S(2)}) copy-start(f32[512]{0:T(512)} %param.12) | copy-start | bytes 6148
  58.7 25.9 %copy-start.1 = (bf16[512,128]{1,0:T(8,128)(2,1)S(1)}, bf16[512,128]{1,0:T(8,128)(2,1)}, u32[]{:S(2)}) copy-start(bf16[512,128]{1,0:T(8,128)(2,1)} %rows_ref.1) | copy-start | bytes 393220
  58.7 25.9 %copy-start.4 = (bf16[512,128]{1,0:T(8,128)(2,1)S(1)}, bf16[512,128]{1,0:T(8,128)(2,1)}, u32[]{:S(2)}) copy-start(bf16[512,128]{1,0:T(8,128)(2,1)} %param.13) | copy-start | bytes 393220
  58.7 25.9 %copy-start.5 = (f32[128]{0:T(128)S(1)}, f32[128]{0:T(128)}, u32[]{:S(2)}) copy-start(f32[128]{0:T(128)} %param.14) | copy-start | bytes 1540
  65.4 20.3 %copy-start.2 = (bf16[512,128]{1,0:T(8,128)(2,1)S(1)}, bf16[512,128]{1,0:T(8,128)(2,1)}, u32[]{:S(2)}) copy-start(bf16[512,128]{1,0:T(8,128)(2,1)} %param.15) | copy-start | bytes 393220

commit v27 on v26

--- a/solution.py
+++ b/solution.py
@@ -87,13 +87,13 @@
                 )
 
     tree_split = tree_src.shape[0] // 2
+    ring_step(2)
     first_right.wait_recv()
     from_left = left * ny + y
     second_right = send(3, tree_out.at[from_left, :tree_split], tree_out.at[from_left, :tree_split], to_right)
     first_left.wait_recv()
     from_right = right * ny + y
     second_left = send(7, tree_out.at[from_right, tree_split:], tree_out.at[from_right, tree_split:], to_left)
-    ring_step(2)
     first_other.wait_recv()
     from_other = x * ny + other
     other_right = send(4, tree_out.at[from_other], tree_out.at[from_other], to_right)

time: 169 us -> 164 us (0.970)
  Pallas kernels: 161 us -> 155 us
    pallas_call x2, Pallas kernels: 37.2 us -> 28.9 us  [reduce_rep(): pl.pallas_call(reduce_kernel, out_shape=jax.ShapeDtypeStruct(piece, piece...]
where the time goes in v27:
time: 164 us; the launch traced here: 163 us
  Pallas kernels  155 us (95%)
  matrix products  3.54 us (2%)
  other arithmetic  2.86 us (2%)
    pallas_call x2, Pallas kernels, gather_blk(): pl.pallas_call(gather_kernel, out_shape=(jax.ShapeDtypeStruct((nz, *piece...  112 us
    pallas_call x2, Pallas kernels, reduce_rep(): pl.pallas_call(reduce_kernel, out_shape=jax.ShapeDtypeStruct(piece, piece...  28.9 us
    pallas_call x2, Pallas kernels, tile_products(): pl.pallas_call(products_kernel, out_shape=jax.ShapeDtypeStruct((rows, BLO...  14.6 us

profile of v27, /device:TPU:9, one launch (start us, length us, event | category | flops | bytes accessed | tf_op | source)
XLA Modules:
  0.0 163.2 jit_solution(1865433581909885703)
XLA Ops:
  0.6 0.0 copy-start
  0.6 0.8 copy.10
  1.4 0.6 fusion.15.flag_ref
  2.0 0.6 select_add_fusion
  2.7 57.8 %shard_map.95 = (bf16[8,256,128]{2,1,0:T(8,128)(2,1)}, bf16[8,256,128]{2,1,0:T(8,128)(2,1)}, bf16[8,8,256,128]{3,2,1,0:T(8,128)(2,1)}, bf16[8,8,256,128]{3,2,1,0:T(8,128)(2,1)}) custom-call(bf16[512,128]{1,0:T(8,128)(2,1)} %rows_ref.1), custom_call_target="tpu_custom_call" | custom-call | tf_op jit(solution)/shard_map/pallas_call | solution.py:201
  60.5 0.0 copy-start.3
  60.5 0.0 copy-start.1
  60.5 0.0 copy-start.4
  60.5 0.0 copy-start.5
  60.6 7.3 %shard_map.96 = f32[16,128,128]{2,1,0:T(8,128)} custom-call(s32[16,4]{1,0:T(8,128)} %fusion.15.flag_ref, s32[16,4]{1,0:T(8,128)} %get-tuple-element.11.first_ref, s32[16,4]{1,0:T(8,128)} %get-tuple-element.10.second_ref, bf16[128,128,128]{2,1,0:T(8,128)(2,1)} %bitcast.92, bf16[128,128,128]{2,1,0:T(8,128)(2,1)} %bitcast.108, bf16[128,128,128]{2,1,0:T(8,128)(2,1)} %bitcast.79, ...), custom_call_target="tpu_custom_call" | custom-call | tf_op jit(solution)/shard_map/pallas_call | solution.py:333
  67.9 0.0 copy-start.2
  67.9 14.3 %shard_map.97 = f32[512,128]{1,0:T(8,128)} custom-call(f32[4,512,128]{2,1,0:T(8,128)} %bitcast.144), custom_call_target="tpu_custom_call" | custom-call | tf_op jit(solution)/shard_map/pallas_call | solution.py:274
  82.2 0.0 copy-done
  82.2 0.0 copy-done.3
  82.2 1.2 convolution_add_fusion
  83.4 0.0 copy-done.1
  83.4 0.0 copy-done.4
  83.5 0.0 copy-done.5
  83.5 1.1 fusion.5
  84.6 1.2 fusion.4.rows_ref
  85.8 53.8 %shard_map.98 = (bf16[8,256,128]{2,1,0:T(8,128)(2,1)}, bf16[8,256,128]{2,1,0:T(8,128)(2,1)}, bf16[8,8,256,128]{3,2,1,0:T(8,128)(2,1)}, bf16[8,8,256,128]{3,2,1,0:T(8,128)(2,1)}) custom-call(bf16[512,128]{1,0:T(8,128)(2,1)} %fusion.4.rows_ref), custom_call_target="tpu_custom_call" | custom-call | tf_op jit(solution)/shard_map/pallas_call | solution.py:201
  139.6 7.3 %shard_map.99 = f32[16,128,128]{2,1,0:T(8,128)} custom-call(s32[16,4]{1,0:T(8,128)} %fusion.15.flag_ref, s32[16,4]{1,0:T(8,128)} %get-tuple-element.11.first_ref, s32[16,4]{1,0:T(8,128)} %get-tuple-element.10.second_ref, bf16[128,128,128]{2,1,0:T(8,128)(2,1)} %bitcast.28, bf16[128,128,128]{2,1,0:T(8,128)(2,1)} %bitcast.44, bf16[128,128,128]{2,1,0:T(8,128)(2,1)} %bitcast.15, ...), custom_call_target="tpu_custom_call" | custom-call | tf_op jit(solution)/shard_map/pallas_call | solution.py:333
  146.9 14.6 %shard_map.100 = f32[512,128]{1,0:T(8,128)} custom-call(f32[4,512,128]{2,1,0:T(8,128)} %bitcast.143), custom_call_target="tpu_custom_call" | custom-call | tf_op jit(solution)/shard_map/pallas_call | solution.py:274
  161.6 1.6 %add_convert_fusion = bf16[512,128]{1,0:T(8,128)(2,1)} fusion(f32[512,128]{1,0:T(8,128)} %shard_map.100, bf16[512,128]{1,0:T(8,128)(2,1)S(1)} %copy-done.2), kind=kLoop, calls=%fused_computation.15 | loop fusion | flops 196608 | bytes 524288 | tf_op jit(solution)/shard_map/convert_element_type | solution.py:366
  (1 shorter events, 0.0 us)
Async XLA Ops:
  0.6 81.6 %copy-start = (bf16[128,512]{1,0:T(8,128)(2,1)S(1)}, bf16[128,512]{1,0:T(8,128)(2,1)}, u32[]{:S(2)}) copy-start(bf16[128,512]{1,0:T(8,128)(2,1)} %param.11) | copy-start | bytes 393220
  60.5 21.7 %copy-start.3 = (f32[512]{0:T(512)S(1)}, f32[512]{0:T(512)}, u32[]{:S(2)}) copy-start(f32[512]{0:T(512)} %param.12) | copy-start | bytes 6148
  60.5 22.9 %copy-start.1 = (bf16[512,128]{1,0:T(8,128)(2,1)S(1)}, bf16[512,128]{1,0:T(8,128)(2,1)}, u32[]{:S(2)}) copy-start(bf16[512,128]{1,0:T(8,128)(2,1)} %rows_ref.1) | copy-start | bytes 393220
  60.5 22.9 %copy-start.4 = (bf16[512,128]{1,0:T(8,128)(2,1)S(1)}, bf16[512,128]{1,0:T(8,128)(2,1)}, u32[]{:S(2)}) copy-start(bf16[512,128]{1,0:T(8,128)(2,1)} %param.13) | copy-start | bytes 393220
  60.5 22.9 %copy-start.5 = (f32[128]{0:T(128)S(1)}, f32[128]{0:T(128)}, u32[]{:S(2)}) copy-start(f32[128]{0:T(128)} %param.14) | copy-start | bytes 1540
  67.9 16.7 %copy-start.2 = (bf16[512,128]{1,0:T(8,128)(2,1)S(1)}, bf16[512,128]{1,0:T(8,128)(2,1)}, u32[]{:S(2)}) copy-start(bf16[512,128]{1,0:T(8,128)(2,1)} %param.15) | copy-start | bytes 393220

commit v28 on v27

--- a/solution.py
+++ b/solution.py
@@ -94,11 +94,11 @@
     first_left.wait_recv()
     from_right = right * ny + y
     second_left = send(7, tree_out.at[from_right, tree_split:], tree_out.at[from_right, tree_split:], to_left)
+    ring_step(3)
     first_other.wait_recv()
     from_other = x * ny + other
     other_right = send(4, tree_out.at[from_other], tree_out.at[from_other], to_right)
     other_left = send(5, tree_out.at[from_other], tree_out.at[from_other], to_left)
-    ring_step(3)
     other_right.wait_recv()
     from_left_other = left * ny + other
     third_right = send(

time: 164 us -> 172 us (1.049)
  Pallas kernels: 155 us -> 163 us
    pallas_call x2, Pallas kernels: 28.9 us -> 34.2 us  [reduce_rep(): pl.pallas_call(reduce_kernel, out_shape=jax.ShapeDtypeStruct(piece, piece...]
    pallas_call x2, Pallas kernels: 112 us -> 116 us  [gather_blk(): pl.pallas_call(gather_kernel, out_shape=(jax.ShapeDtypeStruct((nz, *piece...]
where the time goes in v28:
time: 172 us; the launch traced here: 171 us
  Pallas kernels  163 us (95%)
  matrix products  3.53 us (2%)
  other arithmetic  2.86 us (2%)
    pallas_call x2, Pallas kernels, gather_blk(): pl.pallas_call(gather_kernel, out_shape=(jax.ShapeDtypeStruct((nz, *piece...  116 us
    pallas_call x2, Pallas kernels, reduce_rep(): pl.pallas_call(reduce_kernel, out_shape=jax.ShapeDtypeStruct(piece, piece...  34.2 us
    pallas_call x2, Pallas kernels, tile_products(): pl.pallas_call(products_kernel, out_shape=jax.ShapeDtypeStruct((rows, BLO...  13.2 us

profile of v28, /device:TPU:9, one launch (start us, length us, event | category | flops | bytes accessed | tf_op | source)
XLA Modules:
  0.0 171.3 jit_solution(4937806995389223086)
XLA Ops:
  0.6 0.0 copy-start
  0.6 0.8 copy.10
  1.4 0.6 fusion.15.flag_ref
  2.0 0.6 select_add_fusion
  2.7 60.6 %shard_map.95 = (bf16[8,256,128]{2,1,0:T(8,128)(2,1)}, bf16[8,256,128]{2,1,0:T(8,128)(2,1)}, bf16[8,8,256,128]{3,2,1,0:T(8,128)(2,1)}, bf16[8,8,256,128]{3,2,1,0:T(8,128)(2,1)}) custom-call(bf16[512,128]{1,0:T(8,128)(2,1)} %rows_ref.1), custom_call_target="tpu_custom_call" | custom-call | tf_op jit(solution)/shard_map/pallas_call | solution.py:201
  63.3 0.0 copy-start.3
  63.3 0.0 copy-start.1
  63.3 0.0 copy-start.4
  63.3 0.0 copy-start.5
  63.3 6.6 %shard_map.96 = f32[16,128,128]{2,1,0:T(8,128)} custom-call(s32[16,4]{1,0:T(8,128)} %fusion.15.flag_ref, s32[16,4]{1,0:T(8,128)} %get-tuple-element.11.first_ref, s32[16,4]{1,0:T(8,128)} %get-tuple-element.10.second_ref, bf16[128,128,128]{2,1,0:T(8,128)(2,1)} %bitcast.92, bf16[128,128,128]{2,1,0:T(8,128)(2,1)} %bitcast.108, bf16[128,128,128]{2,1,0:T(8,128)(2,1)} %bitcast.79, ...), custom_call_target="tpu_custom_call" | custom-call | tf_op jit(solution)/shard_map/pallas_call | solution.py:333
  69.9 0.0 copy-start.2
  70.0 16.5 %shard_map.97 = f32[512,128]{1,0:T(8,128)} custom-call(f32[4,512,128]{2,1,0:T(8,128)} %bitcast.144), custom_call_target="tpu_custom_call" | custom-call | tf_op jit(solution)/shard_map/pallas_call | solution.py:274
  86.5 0.0 copy-done
  86.5 0.0 copy-done.3
  86.5 1.2 convolution_add_fusion
  87.7 0.0 copy-done.1
  87.8 0.0 copy-done.4
  87.8 1.1 fusion.5
  88.9 0.0 copy-done.2
  88.9 1.2 fusion.4.rows_ref
  90.1 55.4 %shard_map.98 = (bf16[8,256,128]{2,1,0:T(8,128)(2,1)}, bf16[8,256,128]{2,1,0:T(8,128)(2,1)}, bf16[8,8,256,128]{3,2,1,0:T(8,128)(2,1)}, bf16[8,8,256,128]{3,2,1,0:T(8,128)(2,1)}) custom-call(bf16[512,128]{1,0:T(8,128)(2,1)} %fusion.4.rows_ref), custom_call_target="tpu_custom_call" | custom-call | tf_op jit(solution)/shard_map/pallas_call | solution.py:201
  145.5 6.6 %shard_map.99 = f32[16,128,128]{2,1,0:T(8,128)} custom-call(s32[16,4]{1,0:T(8,128)} %fusion.15.flag_ref, s32[16,4]{1,0:T(8,128)} %get-tuple-element.11.first_ref, s32[16,4]{1,0:T(8,128)} %get-tuple-element.10.second_ref, bf16[128,128,128]{2,1,0:T(8,128)(2,1)} %bitcast.28, bf16[128,128,128]{2,1,0:T(8,128)(2,1)} %bitcast.44, bf16[128,128,128]{2,1,0:T(8,128)(2,1)} %bitcast.15, ...), custom_call_target="tpu_custom_call" | custom-call | tf_op jit(solution)/shard_map/pallas_call | solution.py:333
  152.1 17.6 %shard_map.100 = f32[512,128]{1,0:T(8,128)} custom-call(f32[4,512,128]{2,1,0:T(8,128)} %bitcast.143), custom_call_target="tpu_custom_call" | custom-call | tf_op jit(solution)/shard_map/pallas_call | solution.py:274
  169.7 1.6 add_convert_fusion
  (1 shorter events, 0.0 us)
Async XLA Ops:
  0.6 85.9 %copy-start = (bf16[128,512]{1,0:T(8,128)(2,1)S(1)}, bf16[128,512]{1,0:T(8,128)(2,1)}, u32[]{:S(2)}) copy-start(bf16[128,512]{1,0:T(8,128)(2,1)} %param.11) | copy-start | bytes 393220
  63.3 23.2 %copy-start.3 = (f32[512]{0:T(512)S(1)}, f32[512]{0:T(512)}, u32[]{:S(2)}) copy-start(f32[512]{0:T(512)} %param.12) | copy-start | bytes 6148
  63.3 24.4 %copy-start.1 = (bf16[512,128]{1,0:T(8,128)(2,1)S(1)}, bf16[512,128]{1,0:T(8,128)(2,1)}, u32[]{:S(2)}) copy-start(bf16[512,128]{1,0:T(8,128)(2,1)} %rows_ref.1) | copy-start | bytes 393220
  63.3 24.4 %copy-start.4 = (bf16[512,128]{1,0:T(8,128)(2,1)S(1)}, bf16[512,128]{1,0:T(8,128)(2,1)}, u32[]{:S(2)}) copy-start(bf16[512,128]{1,0:T(8,128)(2,1)} %param.13) | copy-start | bytes 393220
  63.3 24.4 %copy-start.5 = (f32[128]{0:T(128)S(1)}, f32[128]{0:T(128)}, u32[]{:S(2)}) copy-start(f32[128]{0:T(128)} %param.14) | copy-start | bytes 1540
  69.9 18.9 %copy-start.2 = (bf16[512,128]{1,0:T(8,128)(2,1)S(1)}, bf16[512,128]{1,0:T(8,128)(2,1)}, u32[]{:S(2)}) copy-start(bf16[512,128]{1,0:T(8,128)(2,1)} %param.15) | copy-start | bytes 393220
